TPU v7x, 128 devices: a whole 4x4x4 slice. The times are simulated.
128 devices in a mesh: leaf: 8 (over x, core), grp: 16 (over y, z).
Axes of the slice: x: 4, y: 4, z: 4, core: 2. Of those that a mesh axis runs over, the one named last changes fastest.
Arguments:
- rhs_leaf: float32 [64, 262144], P(None, ('leaf', 'grp')), may hold values from -6 to 6
- rhs_sep: float32 [64, 32768], P(None, ('leaf', 'grp')), may hold values from -6 to 6
- rhs_top: float32 [64, 2048], replicated, may hold values from -6 to 6
- leaf_inverse: float32 [2048, 128, 128], P(('leaf', 'grp')), may hold values from -1.5 to 1.5, as said below
- leaf_coupling: bfloat16 [2048, 2, 256, 128], P(('leaf', 'grp')), may hold values from -0.09375 to 0.09375
- leaf_targets: int32 [2048, 2], P(('leaf', 'grp')), may hold values from 0 to 15, all different within a row
- sep_inverse: float32 [128, 256, 256], P(('leaf', 'grp')), may hold values from -1.5 to 1.5, as said below
- sep_blocks: bfloat16 [128, 16, 256, 256], P(('leaf', 'grp')), may hold values from -1 to 1, as said below
- top_coupling: bfloat16 [32768, 2048], P(('leaf', 'grp')), may hold values from -0.125 to 0.125
- top_inverse: float32 [16, 128, 128], replicated, may hold values from -1.5 to 1.5, as said below
- top_lower: bfloat16 [2048, 2048], replicated, may hold values from -1 to 1, as said below
- dest_map: int32 [2048, 1], P(('leaf', 'grp')), may hold values from 0 to 15; in each aligned block of 16 rows (0 to 15, 16 to 31, ...) at most 2 rows name the same one
- centers: float32 [2048, 3, 128], P(('leaf', 'grp')), may hold values from 0 to 1
- points: float32 [128, 3, 2048], P(('leaf', 'grp')), may hold values from 0 to 1
- eval_pattern: int32 [2048, 32], P(('leaf', 'grp')), may hold values 0 or 1
Outputs:
- coef_leaf: float32 [64, 262144], P(None, ('leaf', 'grp'))
- coef_sep: float32 [64, 32768], P(None, ('leaf', 'grp'))
- coef_top: float32 [64, 2048], replicated
- values: float32 [64, 262144], P(None, ('leaf', 'grp'))
Inputs may be any that keep to these rules, and one draw needn't show every extreme that they name: `leaf_inverse`: each matrix is lower triangular with a diagonal between 0.5 and 1.5. `sep_inverse`: lower triangular with a diagonal between 0.5 and 1.5. `top_inverse`: lower triangular with a diagonal between 0.5 and 1.5. `sep_blocks`: slot q of device p of a group holds the factor block of separator blocks max(p, q) and min(p, q) of that group, the same on both devices; slot p is zero. `top_lower`: zero except in the 128 by 128 blocks strictly below the diagonal. `leaf_targets`: the 2 entries of a row differ. `dest_map`: of the 16 blocks of one device, at most 2 name the same device.
All inputs are finite; a program needn't handle non-finite values. No bound on the sum of `eval_pattern` on one device may be relied on, other than what follows from the above.
Results may differ from a plain program's by a relative error of at most 0.025.
Values may be sent and summed in bfloat16 or wider, within the bound.
A program may use at most 64 MiB of HBM per device.

v0:
```python
import jax
import jax.numpy as jnp
from jax import lax
from jax.sharding import PartitionSpec as P

CAP = 2


highest = lax.Precision.HIGHEST
support_sq = 0.25


def split_up(shard, dim, peers):
    dims = shard.shape
    pieces = shard.reshape(*dims[:dim], peers, dims[dim] // peers, *dims[dim + 1 :])
    return jnp.moveaxis(pieces, dim, 0)


def sum_at_owner(shard, axis, dim):
    pieces = split_up(shard, dim, lax.axis_size(axis))
    arrived = lax.all_to_all(pieces, axis, split_axis=0, concat_axis=0, tiled=True)
    return arrived.astype(jnp.float32).sum(axis=0)


def from_root(shard, axis, root):
    return lax.dynamic_index_in_dim(lax.all_gather(shard, axis), root, 0, keepdims=False)


def copy_for_each(shard, axis):
    copies = jnp.broadcast_to(shard, (lax.axis_size(axis), *shard.shape))
    return lax.all_to_all(copies, axis, split_axis=0, concat_axis=0, tiled=True)


def over_copies(shard, axis):
    return copy_for_each(shard, axis).astype(jnp.float32).sum(axis=0)


def joined_along(pieces, dim):
    dims = list(pieces.shape[1:])
    dims[dim] *= pieces.shape[0]
    return jnp.moveaxis(pieces, 0, dim).reshape(dims)


def gather_directly(shard, axis, dim):
    pieces = copy_for_each(shard, axis)
    return joined_along(pieces, dim)


def slot_ranks(dest_rows, grp_size):
    onehot = (dest_rows[..., None] == jnp.arange(grp_size)).astype(jnp.int32)
    before = jnp.cumsum(onehot, axis=-2) - onehot
    return jnp.sum(before * onehot, axis=-1)


def evaluate(coef_all, centre_all, block_points, block_mask):
    dist = jnp.zeros((centre_all.shape[0], centre_all.shape[2], block_points.shape[1]), jnp.float32)
    for comp in range(3):
        delta = centre_all[:, comp, :, None] - block_points[None, comp, None, :]
        dist = dist + delta * delta
    weight = jnp.maximum(1.0 - dist / support_sq, 0.0) ** 3
    kernel = (weight * block_mask.astype(jnp.float32)[:, None, None]).astype(jnp.bfloat16)
    return jnp.einsum("krs,ksp->rp", coef_all, kernel, preferred_element_type=jnp.float32)


def on_device(
    rhs_leaf,
    rhs_sep,
    rhs_top,
    leaf_inverse,
    leaf_coupling,
    leaf_targets,
    sep_inverse,
    sep_blocks,
    top_coupling,
    top_inverse,
    top_lower,
    dest_map,
    centers,
    points,
    eval_pattern,
):
    grp_size = lax.axis_size("grp")
    my_index = lax.axis_index("grp")
    blocks_here = leaf_inverse.shape[0]
    snapshots = rhs_leaf.shape[0]
    span = leaf_inverse.shape[1]
    slot_count = CAP
    leaf_rhs = rhs_leaf.reshape(snapshots, blocks_here, span).transpose(1, 0, 2)
    leaf_sol = jnp.einsum("nrs,nts->nrt", leaf_rhs, leaf_inverse, precision=highest)
    leaf_half = leaf_sol.astype(jnp.bfloat16)
    partial_value = jnp.einsum(
        "nrs,ncbs->ncrb", leaf_half, leaf_coupling, preferred_element_type=jnp.float32
    )
    onehot = (leaf_targets[:, :, None] == jnp.arange(grp_size)[None, None, :]).astype(jnp.float32)
    picked = onehot
    shared = sum_at_owner(
        jnp.einsum("ncq,ncrb->qrb", picked, partial_value, precision=highest).astype(jnp.bfloat16),
        "grp",
        0,
    )
    sep_start = rhs_sep - shared[0]
    inverse_own = sep_inverse[0]
    own_blocks = sep_blocks[0]

    def forward_step(target, carry):
        residue, solved = carry
        candidate = jnp.dot(residue, inverse_own.T, precision=highest)
        arrived = from_root(candidate.astype(jnp.bfloat16), "grp", target)
        solved = jnp.where(my_index == target, candidate, solved)
        factor_block = lax.dynamic_index_in_dim(own_blocks, target, 0, keepdims=False)
        update = lax.dot_general(
            arrived, factor_block, (((1,), (1,)), ((), ())), preferred_element_type=jnp.float32
        )
        residue = jnp.where(my_index > target, residue - update, residue)
        return (residue, solved)

    leftover, sep_sol = lax.fori_loop(
        0, grp_size, forward_step, (sep_start, jnp.zeros_like(sep_start))
    )
    sep_half = sep_sol.astype(jnp.bfloat16)
    top_term = jnp.dot(sep_half, top_coupling, preferred_element_type=jnp.float32)
    top_part = sum_at_owner(top_term.astype(jnp.bfloat16), "grp", 1)
    top_part = over_copies(top_part.astype(jnp.bfloat16), "leaf").astype(jnp.float32)
    top_total = gather_directly(top_part.astype(jnp.bfloat16), "grp", 1).astype(top_part.dtype)
    top_start = rhs_top - top_total
    top_count = top_inverse.shape[0]
    top_span = top_inverse.shape[1]

    def top_forward(block_id, carry):
        half_all, full_all = carry
        lower_rows = lax.dynamic_slice_in_dim(top_lower, block_id * top_span, top_span, 0)
        residue = lax.dynamic_slice_in_dim(
            top_start, block_id * top_span, top_span, 1
        ) - lax.dot_general(
            half_all, lower_rows, (((1,), (1,)), ((), ())), preferred_element_type=jnp.float32
        )
        inverse_block = lax.dynamic_index_in_dim(top_inverse, block_id, 0, keepdims=False)
        solved_block = jnp.dot(residue, inverse_block.T, precision=highest)
        half_all = lax.dynamic_update_slice_in_dim(
            half_all, solved_block.astype(jnp.bfloat16), block_id * top_span, 1
        )
        full_all = lax.dynamic_update_slice_in_dim(full_all, solved_block, block_id * top_span, 1)
        return (half_all, full_all)

    empty_half = jnp.zeros(top_start.shape, jnp.bfloat16)
    empty_full = jnp.zeros(top_start.shape, jnp.float32)
    leftover_half, top_fwd = lax.fori_loop(0, top_count, top_forward, (empty_half, empty_full))

    def top_backward(step_id, carry):
        half_all, full_all = carry
        block_id = top_count - 1 - step_id
        lower_cols = lax.dynamic_slice_in_dim(top_lower, block_id * top_span, top_span, 1)
        residue = lax.dynamic_slice_in_dim(top_fwd, block_id * top_span, top_span, 1) - jnp.dot(
            half_all, lower_cols, preferred_element_type=jnp.float32
        )
        inverse_block = lax.dynamic_index_in_dim(top_inverse, block_id, 0, keepdims=False)
        solved_block = jnp.dot(residue, inverse_block, precision=highest)
        half_all = lax.dynamic_update_slice_in_dim(
            half_all, solved_block.astype(jnp.bfloat16), block_id * top_span, 1
        )
        full_all = lax.dynamic_update_slice_in_dim(full_all, solved_block, block_id * top_span, 1)
        return (half_all, full_all)

    top_half, coef_top = lax.fori_loop(0, top_count, top_backward, (empty_half, empty_full))
    back_start = sep_sol - lax.dot_general(
        top_half, top_coupling, (((1,), (1,)), ((), ())), preferred_element_type=jnp.float32
    )

    def backward_step(step_id, carry):
        residue, solved, known_table = carry
        target = grp_size - 1 - step_id
        candidate = jnp.dot(residue, inverse_own, precision=highest)
        arrived = from_root(candidate.astype(jnp.bfloat16), "grp", target)
        solved = jnp.where(my_index == target, candidate, solved)
        known_table = lax.dynamic_update_index_in_dim(known_table, arrived, target, 0)
        factor_block = lax.dynamic_index_in_dim(own_blocks, target, 0, keepdims=False)
        update = jnp.dot(arrived, factor_block, preferred_element_type=jnp.float32)
        residue = jnp.where(my_index < target, residue - update, residue)
        return (residue, solved, known_table)

    empty_table = jnp.zeros((grp_size,) + back_start.shape, jnp.bfloat16)
    leftover_back, coef_sep, known_table = lax.fori_loop(
        0, grp_size, backward_step, (back_start, jnp.zeros_like(back_start), empty_table)
    )
    picked = jnp.einsum(
        "ncq,qrb->ncrb",
        onehot.astype(jnp.bfloat16),
        known_table,
        preferred_element_type=jnp.float32,
    ).astype(jnp.bfloat16)
    reduced = jnp.einsum(
        "ncrb,ncbs->nrs", picked, leaf_coupling, preferred_element_type=jnp.float32
    )
    leaf_coef = jnp.einsum("nrs,nst->nrt", leaf_sol - reduced, leaf_inverse, precision=highest)
    coef_leaf = leaf_coef.transpose(1, 0, 2).reshape(snapshots, blocks_here * span)
    leaf_out = leaf_coef.astype(jnp.bfloat16)
    slot_ids = jnp.arange(slot_count)
    grp_ids = jnp.arange(grp_size)
    own_dest = dest_map[:, 0]
    slot_rank = slot_ranks(own_dest[None, :], grp_size)[0]
    selector = (own_dest[None, None, :] == grp_ids[:, None, None]) & (
        slot_rank[None, None, :] == slot_ids[None, :, None]
    )
    send_coef = jnp.einsum(
        "dkj,jrt->dkrt", selector.astype(jnp.bfloat16), leaf_out, preferred_element_type=jnp.float32
    ).astype(jnp.bfloat16)
    send_centre = jnp.einsum(
        "dkj,jct->dkct", selector.astype(jnp.float32), centers, precision=highest
    )
    received, recv_centre = (
        lax.all_to_all(send_coef, "grp", split_axis=0, concat_axis=0, tiled=True),
        lax.all_to_all(
            send_centre.astype(jnp.bfloat16), "grp", split_axis=0, concat_axis=0, tiled=True
        ).astype(send_centre.dtype),
    )
    slot_total = grp_size * slot_count
    coef_all = received.reshape(slot_total, snapshots, span)
    centre_all = recv_centre.reshape(slot_total, 3, span)
    point_blocks = eval_pattern.shape[0]
    pts_blocks = points[0].reshape(3, point_blocks, span).transpose(1, 0, 2)

    def one_block(block_item):
        return evaluate(coef_all, centre_all, block_item[0], block_item[1])

    blocks_out = lax.map(one_block, (pts_blocks, eval_pattern))
    values = blocks_out.transpose(1, 0, 2).reshape(snapshots, point_blocks * span)
    return (coef_leaf, coef_sep, coef_top, values)


def solution(mesh):
    in_specs = (
        P(None, ("leaf", "grp")),
        P(None, ("leaf", "grp")),
        P(),
        P(("leaf", "grp"), None, None),
        P(("leaf", "grp"), None, None, None),
        P(("leaf", "grp"), None),
        P(("leaf", "grp"), None, None),
        P(("leaf", "grp"), None, None, None),
        P(("leaf", "grp"), None),
        P(),
        P(),
        P(("leaf", "grp"), None),
        P(("leaf", "grp"), None, None),
        P(("leaf", "grp"), None, None),
        P(("leaf", "grp"), None),
    )
    out_specs = (P(None, ("leaf", "grp")), P(None, ("leaf", "grp")), P(), P(None, ("leaf", "grp")))
    return jax.shard_map(
        on_device, mesh=mesh, in_specs=in_specs, out_specs=out_specs, check_vma=False
    )
```

profile of v0, /device:TPU:24, one launch (start us, length us, event | category | flops | bytes accessed | tf_op | source)
XLA Modules:
  0.0 1061.1 jit_solution(6811389980969749353)
XLA Ops:
  26.8 386.1 %while.81 = (s32[]{:T(128)}, f32[64,256]{1,0:T(8,128)S(1)}, f32[64,256]{1,0:T(8,128)S(1)}, s32[]{:T(128)}, f32[256,256]{1,0:T(8,128)S(1)}, /*index=5*/bf16[16,256,256]{2,1,0:T(8,128)(2,1)}, s32[]{:T(128)}, s32[]{:T(128)}) while((s32[]{:T(128)}, f32[64,256]{1,0:T(8,128)S(1)}, f32[64,256]{1,0:T(8,128)S(1)}, s32[]{:T(128)}, ...), condition=%wide.region_2.3_spmd.clone, body=%wide.region_1.2_spmd.clone.sunk | while | flops 58802180 | bytes 1344627 | solution.py:117
  27.2 23.1 %all-gather.6 = bf16[1024,256]{1,0:T(8,128)(2,1)S(1)} all-gather(bf16[64,256]{1,0:T(8,128)(2,1)S(1)} %get-tuple-element.964), channel_id=2, replica_groups=mesh['leaf'=8,'grp'=16] {'grp'}, dimensions={0}, use_global_device_ids=true | all-gather | bytes 557056 | tf_op jit(solution)/shard_map/while/body/eval_jaxpr/all_gather | solution.py:26
  75.3 23.3 %all-gather.6 = bf16[1024,256]{1,0:T(8,128)(2,1)S(1)} all-gather(bf16[64,256]{1,0:T(8,128)(2,1)S(1)} %get-tuple-element.964), channel_id=2, replica_groups=mesh['leaf'=8,'grp'=16] {'grp'}, dimensions={0}, use_global_device_ids=true | all-gather | bytes 557056 | tf_op jit(solution)/shard_map/while/body/eval_jaxpr/all_gather | solution.py:26
  100.1 22.2 %all-gather.6 = bf16[1024,256]{1,0:T(8,128)(2,1)S(1)} all-gather(bf16[64,256]{1,0:T(8,128)(2,1)S(1)} %get-tuple-element.964), channel_id=2, replica_groups=mesh['leaf'=8,'grp'=16] {'grp'}, dimensions={0}, use_global_device_ids=true | all-gather | bytes 557056 | tf_op jit(solution)/shard_map/while/body/eval_jaxpr/all_gather | solution.py:26
  123.8 23.0 %all-gather.6 = bf16[1024,256]{1,0:T(8,128)(2,1)S(1)} all-gather(bf16[64,256]{1,0:T(8,128)(2,1)S(1)} %get-tuple-element.964), channel_id=2, replica_groups=mesh['leaf'=8,'grp'=16] {'grp'}, dimensions={0}, use_global_device_ids=true | all-gather | bytes 557056 | tf_op jit(solution)/shard_map/while/body/eval_jaxpr/all_gather | solution.py:26
  148.3 22.2 %all-gather.6 = bf16[1024,256]{1,0:T(8,128)(2,1)S(1)} all-gather(bf16[64,256]{1,0:T(8,128)(2,1)S(1)} %get-tuple-element.964), channel_id=2, replica_groups=mesh['leaf'=8,'grp'=16] {'grp'}, dimensions={0}, use_global_device_ids=true | all-gather | bytes 557056 | tf_op jit(solution)/shard_map/while/body/eval_jaxpr/all_gather | solution.py:26
  171.9 23.1 %all-gather.6 = bf16[1024,256]{1,0:T(8,128)(2,1)S(1)} all-gather(bf16[64,256]{1,0:T(8,128)(2,1)S(1)} %get-tuple-element.964), channel_id=2, replica_groups=mesh['leaf'=8,'grp'=16] {'grp'}, dimensions={0}, use_global_device_ids=true | all-gather | bytes 557056 | tf_op jit(solution)/shard_map/while/body/eval_jaxpr/all_gather | solution.py:26
  196.5 22.0 %all-gather.6 = bf16[1024,256]{1,0:T(8,128)(2,1)S(1)} all-gather(bf16[64,256]{1,0:T(8,128)(2,1)S(1)} %get-tuple-element.964), channel_id=2, replica_groups=mesh['leaf'=8,'grp'=16] {'grp'}, dimensions={0}, use_global_device_ids=true | all-gather | bytes 557056 | tf_op jit(solution)/shard_map/while/body/eval_jaxpr/all_gather | solution.py:26
  220.1 23.0 %all-gather.6 = bf16[1024,256]{1,0:T(8,128)(2,1)S(1)} all-gather(bf16[64,256]{1,0:T(8,128)(2,1)S(1)} %get-tuple-element.964), channel_id=2, replica_groups=mesh['leaf'=8,'grp'=16] {'grp'}, dimensions={0}, use_global_device_ids=true | all-gather | bytes 557056 | tf_op jit(solution)/shard_map/while/body/eval_jaxpr/all_gather | solution.py:26
  244.6 22.2 %all-gather.6 = bf16[1024,256]{1,0:T(8,128)(2,1)S(1)} all-gather(bf16[64,256]{1,0:T(8,128)(2,1)S(1)} %get-tuple-element.964), channel_id=2, replica_groups=mesh['leaf'=8,'grp'=16] {'grp'}, dimensions={0}, use_global_device_ids=true | all-gather | bytes 557056 | tf_op jit(solution)/shard_map/while/body/eval_jaxpr/all_gather | solution.py:26
  268.4 22.8 %all-gather.6 = bf16[1024,256]{1,0:T(8,128)(2,1)S(1)} all-gather(bf16[64,256]{1,0:T(8,128)(2,1)S(1)} %get-tuple-element.964), channel_id=2, replica_groups=mesh['leaf'=8,'grp'=16] {'grp'}, dimensions={0}, use_global_device_ids=true | all-gather | bytes 557056 | tf_op jit(solution)/shard_map/while/body/eval_jaxpr/all_gather | solution.py:26
  292.7 22.3 %all-gather.6 = bf16[1024,256]{1,0:T(8,128)(2,1)S(1)} all-gather(bf16[64,256]{1,0:T(8,128)(2,1)S(1)} %get-tuple-element.964), channel_id=2, replica_groups=mesh['leaf'=8,'grp'=16] {'grp'}, dimensions={0}, use_global_device_ids=true | all-gather | bytes 557056 | tf_op jit(solution)/shard_map/while/body/eval_jaxpr/all_gather | solution.py:26
  316.6 23.4 %all-gather.6 = bf16[1024,256]{1,0:T(8,128)(2,1)S(1)} all-gather(bf16[64,256]{1,0:T(8,128)(2,1)S(1)} %get-tuple-element.964), channel_id=2, replica_groups=mesh['leaf'=8,'grp'=16] {'grp'}, dimensions={0}, use_global_device_ids=true | all-gather | bytes 557056 | tf_op jit(solution)/shard_map/while/body/eval_jaxpr/all_gather | solution.py:26
  341.5 22.2 %all-gather.6 = bf16[1024,256]{1,0:T(8,128)(2,1)S(1)} all-gather(bf16[64,256]{1,0:T(8,128)(2,1)S(1)} %get-tuple-element.964), channel_id=2, replica_groups=mesh['leaf'=8,'grp'=16] {'grp'}, dimensions={0}, use_global_device_ids=true | all-gather | bytes 557056 | tf_op jit(solution)/shard_map/while/body/eval_jaxpr/all_gather | solution.py:26
  365.2 22.9 %all-gather.6 = bf16[1024,256]{1,0:T(8,128)(2,1)S(1)} all-gather(bf16[64,256]{1,0:T(8,128)(2,1)S(1)} %get-tuple-element.964), channel_id=2, replica_groups=mesh['leaf'=8,'grp'=16] {'grp'}, dimensions={0}, use_global_device_ids=true | all-gather | bytes 557056 | tf_op jit(solution)/shard_map/while/body/eval_jaxpr/all_gather | solution.py:26
  389.6 22.2 %all-gather.6 = bf16[1024,256]{1,0:T(8,128)(2,1)S(1)} all-gather(bf16[64,256]{1,0:T(8,128)(2,1)S(1)} %get-tuple-element.964), channel_id=2, replica_groups=mesh['leaf'=8,'grp'=16] {'grp'}, dimensions={0}, use_global_device_ids=true | all-gather | bytes 557056 | tf_op jit(solution)/shard_map/while/body/eval_jaxpr/all_gather | solution.py:26
  460.8 49.1 %while.78 = (s32[]{:T(128)}, bf16[64,2048]{1,0:T(8,128)(2,1)S(1)}, f32[64,2048]{1,0:T(8,128)}, f32[64,2048]{1,0:T(8,128)}, bf16[2048,2048]{1,0:T(8,128)(2,1)}, /...) while((s32[]{:T(128)}, bf16[64,2048]{1,0:T(8,128)(2,1)S(1)}, ...), condition=%wide.region_6.7_spmd, body=%wide.region_5.6_spmd.sunk | while | flops 46153732 | bytes 1066651 | solution.py:147
  510.8 47.2 %while.79 = (s32[]{:T(128)}, bf16[64,2048]{1,0:T(8,128)(2,1)S(1)}, f32[64,2048]{1,0:T(8,128)}, f32[64,2048]{1,0:T(8,128)}, bf16[2048,2048]{1,0:T(8,128)(2,1)}, /...) while((s32[]{:T(128)}, bf16[64,2048]{1,0:T(8,128)(2,1)S(1)}, ...), condition=%wide.region_8.9_spmd, body=%wide.region_7.8_spmd.sunk | while | flops 46153736 | bytes 1066205 | solution.py:164
  560.5 416.1 %while.82 = (s32[]{:T(128)}, f32[64,256]{1,0:T(8,128)S(1)}, f32[64,256]{1,0:T(8,128)}, bf16[16,64,256]{2,1,0:T(8,128)(2,1)}, s32[]{:T(128)}, /*index=5*/f32[256,...) while((s32[]{:T(128)}, f32[64,256]{1,0:T(8,128)S(1)}, ...), condition=%wide.region_10.11_spmd.clone, body=%wide.region_9.10_spmd.clone.sunk | while | flops 58802184 | bytes 1410748 | solution.py:182
  561.3 23.6 %all-gather.7 = bf16[1024,256]{1,0:T(8,128)(2,1)S(1)} all-gather(bf16[64,256]{1,0:T(8,128)(2,1)S(1)} %get-tuple-element.973), channel_id=3, replica_groups=mesh['leaf'=8,'grp'=16] {'grp'}, dimensions={0}, use_global_device_ids=true | all-gather | bytes 557056 | tf_op jit(solution)/shard_map/while/body/eval_jaxpr/all_gather | solution.py:26
  613.6 23.2 %all-gather.7 = bf16[1024,256]{1,0:T(8,128)(2,1)S(1)} all-gather(bf16[64,256]{1,0:T(8,128)(2,1)S(1)} %get-tuple-element.973), channel_id=3, replica_groups=mesh['leaf'=8,'grp'=16] {'grp'}, dimensions={0}, use_global_device_ids=true | all-gather | bytes 557056 | tf_op jit(solution)/shard_map/while/body/eval_jaxpr/all_gather | solution.py:26
  640.2 22.1 %all-gather.7 = bf16[1024,256]{1,0:T(8,128)(2,1)S(1)} all-gather(bf16[64,256]{1,0:T(8,128)(2,1)S(1)} %get-tuple-element.973), channel_id=3, replica_groups=mesh['leaf'=8,'grp'=16] {'grp'}, dimensions={0}, use_global_device_ids=true | all-gather | bytes 557056 | tf_op jit(solution)/shard_map/while/body/eval_jaxpr/all_gather | solution.py:26
  665.7 23.0 %all-gather.7 = bf16[1024,256]{1,0:T(8,128)(2,1)S(1)} all-gather(bf16[64,256]{1,0:T(8,128)(2,1)S(1)} %get-tuple-element.973), channel_id=3, replica_groups=mesh['leaf'=8,'grp'=16] {'grp'}, dimensions={0}, use_global_device_ids=true | all-gather | bytes 557056 | tf_op jit(solution)/shard_map/while/body/eval_jaxpr/all_gather | solution.py:26
  692.1 22.1 %all-gather.7 = bf16[1024,256]{1,0:T(8,128)(2,1)S(1)} all-gather(bf16[64,256]{1,0:T(8,128)(2,1)S(1)} %get-tuple-element.973), channel_id=3, replica_groups=mesh['leaf'=8,'grp'=16] {'grp'}, dimensions={0}, use_global_device_ids=true | all-gather | bytes 557056 | tf_op jit(solution)/shard_map/while/body/eval_jaxpr/all_gather | solution.py:26
  717.6 23.2 %all-gather.7 = bf16[1024,256]{1,0:T(8,128)(2,1)S(1)} all-gather(bf16[64,256]{1,0:T(8,128)(2,1)S(1)} %get-tuple-element.973), channel_id=3, replica_groups=mesh['leaf'=8,'grp'=16] {'grp'}, dimensions={0}, use_global_device_ids=true | all-gather | bytes 557056 | tf_op jit(solution)/shard_map/while/body/eval_jaxpr/all_gather | solution.py:26
  744.3 22.1 %all-gather.7 = bf16[1024,256]{1,0:T(8,128)(2,1)S(1)} all-gather(bf16[64,256]{1,0:T(8,128)(2,1)S(1)} %get-tuple-element.973), channel_id=3, replica_groups=mesh['leaf'=8,'grp'=16] {'grp'}, dimensions={0}, use_global_device_ids=true | all-gather | bytes 557056 | tf_op jit(solution)/shard_map/while/body/eval_jaxpr/all_gather | solution.py:26
  769.8 23.3 %all-gather.7 = bf16[1024,256]{1,0:T(8,128)(2,1)S(1)} all-gather(bf16[64,256]{1,0:T(8,128)(2,1)S(1)} %get-tuple-element.973), channel_id=3, replica_groups=mesh['leaf'=8,'grp'=16] {'grp'}, dimensions={0}, use_global_device_ids=true | all-gather | bytes 557056 | tf_op jit(solution)/shard_map/while/body/eval_jaxpr/all_gather | solution.py:26
  821.8 23.4 %all-gather.7 = bf16[1024,256]{1,0:T(8,128)(2,1)S(1)} all-gather(bf16[64,256]{1,0:T(8,128)(2,1)S(1)} %get-tuple-element.973), channel_id=3, replica_groups=mesh['leaf'=8,'grp'=16] {'grp'}, dimensions={0}, use_global_device_ids=true | all-gather | bytes 557056 | tf_op jit(solution)/shard_map/while/body/eval_jaxpr/all_gather | solution.py:26
  874.0 23.2 %all-gather.7 = bf16[1024,256]{1,0:T(8,128)(2,1)S(1)} all-gather(bf16[64,256]{1,0:T(8,128)(2,1)S(1)} %get-tuple-element.973), channel_id=3, replica_groups=mesh['leaf'=8,'grp'=16] {'grp'}, dimensions={0}, use_global_device_ids=true | all-gather | bytes 557056 | tf_op jit(solution)/shard_map/while/body/eval_jaxpr/all_gather | solution.py:26
  900.7 22.4 %all-gather.7 = bf16[1024,256]{1,0:T(8,128)(2,1)S(1)} all-gather(bf16[64,256]{1,0:T(8,128)(2,1)S(1)} %get-tuple-element.973), channel_id=3, replica_groups=mesh['leaf'=8,'grp'=16] {'grp'}, dimensions={0}, use_global_device_ids=true | all-gather | bytes 557056 | tf_op jit(solution)/shard_map/while/body/eval_jaxpr/all_gather | solution.py:26
  926.5 23.0 %all-gather.7 = bf16[1024,256]{1,0:T(8,128)(2,1)S(1)} all-gather(bf16[64,256]{1,0:T(8,128)(2,1)S(1)} %get-tuple-element.973), channel_id=3, replica_groups=mesh['leaf'=8,'grp'=16] {'grp'}, dimensions={0}, use_global_device_ids=true | all-gather | bytes 557056 | tf_op jit(solution)/shard_map/while/body/eval_jaxpr/all_gather | solution.py:26
  996.2 62.8 %while.80 = (s32[]{:T(128)}, f32[16,64,128]{2,1,0:T(8,128)}, f32[32,3,128]{2,0,1:T(8,128)S(1)}, f32[16,3,128]{2,0,1:T(8,128)}, s32[16,32]{1,0:T(8,128)}, /*index...) while((s32[]{:T(128)}, f32[16,64,128]{2,1,0:T(8,128)}, ...), condition=%wide.region_14.15_spmd, body=%wide.region_13.14_spmd.sunk | while | flops 74973216 | bytes 710157 | solution.py:225
  (306 shorter events, 444.5 us)
Async XLA Ops:
  0.6 3.7 copy-start
  4.3 0.9 copy-start.5
  7.2 19.5 %copy-start.1 = (f32[1,256,256]{2,1,0:T(8,128)S(1)}, f32[1,256,256]{2,1,0:T(8,128)}, u32[]{:S(2)}) copy-start(f32[1,256,256]{2,1,0:T(8,128)} %param.31) | copy-start | bytes 786436
  8.2 17.6 %all-to-all-start = ((bf16[16,1,64,256]{3,2,1,0:T(8,128)(2,1)}), bf16[16,1,64,256]{3,2,1,0:T(8,128)(2,1)S(1)}, u32[]{:S(2)}, u32[]{:S(2)}) async-start(bf16[16,1,64,256]{3,2,1,0:T(8,128)(2,1)} %copy.91), calls=%async_computation | async-start | bytes 1048576 | tf_op jit(solution)/shard_map/all_to_all | solution.py:21
  412.9 8.5 copy-start.4
  412.9 32.6 %copy-start.3 = (f32[16,3,128]{2,0,1:T(8,128)S(1)}, f32[16,3,128]{2,0,1:T(8,128)}, u32[]{:S(2)}) copy-start(f32[16,3,128]{2,0,1:T(8,128)} %param.37) | copy-start | bytes 73732
  415.2 12.6 %all-to-all-start.1 = ((bf16[16,64,128]{2,1,0:T(8,128)(2,1)}), bf16[16,64,128]{2,1,0:T(8,128)(2,1)S(1)}, u32[]{:S(2)}, u32[]{:S(2)}) async-start(bf16[16,64,128]{2,1,0:T(8,128)(2,1)} %bitcast.165), calls=%async_computation.1 | async-start | bytes 524288 | tf_op jit(solution)/shard_map/all_to_all | solution.py:21
  428.5 10.4 all-to-all-start.2
  439.8 12.1 %all-to-all-start.3 = ((bf16[16,64,128]{2,1,0:T(8,128)(2,1)}), bf16[16,64,128]{2,1,0:T(8,128)(2,1)S(1)}, u32[]{:S(2)}, u32[]{:S(2)}) async-start(bf16[16,64,128]{2,1,0:T(8,128)(2,1)} %broadcast_in_dim.33), calls=%async_computation.3 | async-start | bytes 524288 | tf_op jit(solution)/shard_map/all_to_all | solution.py:31
  451.9 529.8 %all-to-all-start.4 = ((bf16[16,2,3,128]{3,1,2,0:T(2,128)(2,1)}), bf16[16,2,3,128]{3,1,2,0:T(2,128)(2,1)}, u32[]{:S(2)}, u32[]{:S(2)}) async-start(bf16[16,2,3,128]{3,1,2,0:T(2,128)(2,1)} %copy.97), calls=%async_computation.4 | async-start | bytes 49152 | tf_op jit(solution)/shard_map/all_to_all | solution.py:212
  978.2 1.2 copy-start.2
  981.7 14.5 %all-to-all-start.5 = ((bf16[16,2,64,128]{3,2,1,0:T(8,128)(2,1)}), bf16[16,2,64,128]{3,2,1,0:T(8,128)(2,1)S(1)}, u32[]{:S(2)}, u32[]{:S(2)}) async-start(bf16[16,2,64,128]{3,2,1,0:T(8,128)(2,1)} %copy.101), calls=%async_computation.5 | async-start | bytes 1048576 | tf_op jit(solution)/shard_map/all_to_all | solution.py:211
where the time goes:
time: 1070 us; the launch traced here: 1060 us
  blocking collectives  724 us (68%)
  matrix products  197 us (18%)
  local copies, waits for them, and re-layouts  51.6 us (5%)
  starting transfers between devices  37 us (3%)
  waiting for transfers between devices  34.6 us (3%)
  other arithmetic  15 us (1%)
    all_gather x32, blocking collectives, from_root(): lax.all_gather(shard, axis)  724 us
    dot_general x16, matrix products, evaluate(): jnp.einsum('krs,ksp->rp', coef_all, kernel, preferred_element_type=jnp.fl...  40 us
    dot_general x16, matrix products, backward_step(): candidate = jnp.dot(residue, inverse_own, precision=highest)  26.7 us
    dot_general x16, matrix products, top_forward(): lax.dot_general(half_all, lower_rows, (((1,), (1,)), ((), ())), preferred...  21.5 us
  transfers between devices with their start and end apart: 6, of which 5 were waited for; matrix products, arithmetic and copies ran while one was open for 15% of the time, Pallas kernels for 0%

commit v1 on v0

--- a/solution.py
+++ b/solution.py
@@ -1,7 +1,13 @@
+import functools
+
 import jax
 import jax.numpy as jnp
 from jax import lax
 from jax.sharding import PartitionSpec as P
+from jax.experimental import pallas as pl
+from jax.experimental.pallas import tpu as pltpu
+
+MESH = pl.DeviceIdType.MESH
 
 CAP = 2
 
@@ -44,6 +50,142 @@
 def gather_directly(shard, axis, dim):
     pieces = copy_for_each(shard, axis)
     return joined_along(pieces, dim)
+
+
+def _nt(a, b):
+    return lax.dot_general(a, b, (((1,), (1,)), ((), ())), preferred_element_type=jnp.float32)
+
+
+def _nn(a, b):
+    return lax.dot_general(a, b, (((1,), (0,)), ((), ())), preferred_element_type=jnp.float32)
+
+
+def _nt_exact(a, b):
+    return lax.dot_general(
+        a, b, (((1,), (1,)), ((), ())), precision=highest, preferred_element_type=jnp.float32
+    )
+
+
+def _nn_exact(a, b):
+    return lax.dot_general(
+        a, b, (((1,), (0,)), ((), ())), precision=highest, preferred_element_type=jnp.float32
+    )
+
+
+def _greet_group(n, leaf, me):
+    barrier = pltpu.get_barrier_semaphore()
+    for r in range(n):
+        @pl.when(me != r)
+        def _():
+            pl.semaphore_signal(barrier, inc=1, device_id=(leaf, r), device_id_type=MESH)
+    pl.semaphore_wait(barrier, n - 1)
+
+
+def _block_copy(halves, q, dest, send_sem, recv_sem, leaf):
+    return pltpu.make_async_remote_copy(
+        src_ref=halves.at[q],
+        dst_ref=halves.at[q],
+        send_sem=send_sem,
+        recv_sem=recv_sem.at[q],
+        device_id=(leaf, dest),
+        device_id_type=MESH,
+    )
+
+
+def sep_forward_kernel(n, start_ref, inv_ref, blocks_ref, sol_ref, halves, resid, send_sem, recv_sem):
+    me = lax.axis_index("grp")
+    leaf = lax.axis_index("leaf")
+    _greet_group(n, leaf, me)
+    resid[...] = start_ref[...]
+
+    def step(q, carry):
+        @pl.when(me == q)
+        def _():
+            solved = _nt_exact(resid[...], inv_ref[...])
+            sol_ref[...] = solved
+            halves[q] = solved.astype(jnp.bfloat16)
+            for k in range(1, n):
+                @pl.when(q + k < n)
+                def _():
+                    _block_copy(halves, q, q + k, send_sem.at[k], recv_sem, leaf).start()
+            for k in range(1, n):
+                @pl.when(q + k < n)
+                def _():
+                    _block_copy(halves, q, q + k, send_sem.at[k], recv_sem, leaf).wait_send()
+
+        @pl.when(me > q)
+        def _():
+            _block_copy(halves, q, q, send_sem.at[0], recv_sem, leaf).wait_recv()
+            resid[...] = resid[...] - _nt(halves[q], blocks_ref[q])
+
+        return carry
+
+    lax.fori_loop(0, n, step, 0)
+
+
+def sep_backward_kernel(n, start_ref, inv_ref, blocks_ref, sol_ref, table_ref, halves, resid, send_sem, recv_sem):
+    me = lax.axis_index("grp")
+    leaf = lax.axis_index("leaf")
+    _greet_group(n, leaf, me)
+    resid[...] = start_ref[...]
+
+    def step(s, carry):
+        q = n - 1 - s
+
+        @pl.when(me == q)
+        def _():
+            solved = _nn_exact(resid[...], inv_ref[...])
+            sol_ref[...] = solved
+            halves[q] = solved.astype(jnp.bfloat16)
+            for k in range(1, n):
+                dest = lax.rem(q - k + n, n)
+                _block_copy(halves, q, dest, send_sem.at[k], recv_sem, leaf).start()
+            for k in range(1, n):
+                dest = lax.rem(q - k + n, n)
+                _block_copy(halves, q, dest, send_sem.at[k], recv_sem, leaf).wait_send()
+
+        @pl.when(me != q)
+        def _():
+            _block_copy(halves, q, q, send_sem.at[0], recv_sem, leaf).wait_recv()
+
+        @pl.when(me < q)
+        def _():
+            resid[...] = resid[...] - _nn(halves[q], blocks_ref[q])
+
+        return carry
+
+    lax.fori_loop(0, n, step, 0)
+    table_ref[...] = halves[...]
+
+
+def sep_solve(kind, start, inv, blocks, n):
+    rows, width = start.shape
+    vmem = pl.BlockSpec(memory_space=pltpu.VMEM)
+    scratch = [
+        pltpu.VMEM((n, rows, width), jnp.bfloat16),
+        pltpu.VMEM((rows, width), jnp.float32),
+        pltpu.SemaphoreType.DMA((n,)),
+        pltpu.SemaphoreType.DMA((n,)),
+    ]
+    sol_shape = jax.ShapeDtypeStruct((rows, width), jnp.float32)
+    params = dict(has_side_effects=True, vmem_limit_bytes=48 * 1024 * 1024)
+    if kind == "forward":
+        return pl.pallas_call(
+            functools.partial(sep_forward_kernel, n),
+            out_shape=sol_shape,
+            in_specs=[vmem] * 3,
+            out_specs=vmem,
+            scratch_shapes=scratch,
+            compiler_params=pltpu.CompilerParams(collective_id=0, **params),
+        )(start, inv, blocks)
+    return pl.pallas_call(
+        functools.partial(sep_backward_kernel, n),
+        out_shape=(sol_shape, jax.ShapeDtypeStruct((n, rows, width), jnp.bfloat16)),
+        in_specs=[vmem] * 3,
+        out_specs=(vmem, vmem),
+        scratch_shapes=scratch,
+        compiler_params=pltpu.CompilerParams(collective_id=1, **params),
+    )(start, inv, blocks)
 
 
 def slot_ranks(dest_rows, grp_size):
@@ -102,21 +244,7 @@
     inverse_own = sep_inverse[0]
     own_blocks = sep_blocks[0]
 
-    def forward_step(target, carry):
-        residue, solved = carry
-        candidate = jnp.dot(residue, inverse_own.T, precision=highest)
-        arrived = from_root(candidate.astype(jnp.bfloat16), "grp", target)
-        solved = jnp.where(my_index == target, candidate, solved)
-        factor_block = lax.dynamic_index_in_dim(own_blocks, target, 0, keepdims=False)
-        update = lax.dot_general(
-            arrived, factor_block, (((1,), (1,)), ((), ())), preferred_element_type=jnp.float32
-        )
-        residue = jnp.where(my_index > target, residue - update, residue)
-        return (residue, solved)
-
-    leftover, sep_sol = lax.fori_loop(
-        0, grp_size, forward_step, (sep_start, jnp.zeros_like(sep_start))
-    )
+    sep_sol = sep_solve("forward", sep_start, inverse_own, own_blocks, grp_size)
     sep_half = sep_sol.astype(jnp.bfloat16)
     top_term = jnp.dot(sep_half, top_coupling, preferred_element_type=jnp.float32)
     top_part = sum_at_owner(top_term.astype(jnp.bfloat16), "grp", 1)
@@ -166,22 +294,7 @@
         top_half, top_coupling, (((1,), (1,)), ((), ())), preferred_element_type=jnp.float32
     )
 
-    def backward_step(step_id, carry):
-        residue, solved, known_table = carry
-        target = grp_size - 1 - step_id
-        candidate = jnp.dot(residue, inverse_own, precision=highest)
-        arrived = from_root(candidate.astype(jnp.bfloat16), "grp", target)
-        solved = jnp.where(my_index == target, candidate, solved)
-        known_table = lax.dynamic_update_index_in_dim(known_table, arrived, target, 0)
-        factor_block = lax.dynamic_index_in_dim(own_blocks, target, 0, keepdims=False)
-        update = jnp.dot(arrived, factor_block, preferred_element_type=jnp.float32)
-        residue = jnp.where(my_index < target, residue - update, residue)
-        return (residue, solved, known_table)
-
-    empty_table = jnp.zeros((grp_size,) + back_start.shape, jnp.bfloat16)
-    leftover_back, coef_sep, known_table = lax.fori_loop(
-        0, grp_size, backward_step, (back_start, jnp.zeros_like(back_start), empty_table)
-    )
+    coef_sep, known_table = sep_solve("backward", back_start, inverse_own, own_blocks, grp_size)
     picked = jnp.einsum(
         "ncq,qrb->ncrb",
         onehot.astype(jnp.bfloat16),

time: 1070 us -> 382 us (0.36)
  blocking collectives: 724 us -> 17.7 us
  Pallas kernels: 0 us -> 112 us
  matrix products: 197 us -> 127 us
    all_gather x32 -> x0, blocking collectives: 724 us -> none  [from_root(): lax.all_gather(shard, axis)]
    pallas_call x0 -> x2, Pallas kernels: none -> 112 us  [the longest x1 61.8 us: sep_solve(): pl.pallas_call(functools.partial(sep_backward_kernel, n), out_shape=(sol_...]
    dot_general x64 -> x0, matrix products: 67.5 us -> none  [the longest x16 26.7 us: backward_step(): candidate = jnp.dot(residue, inverse_own, precision=highest)]
    all_to_all x0 -> x1, blocking collectives: none -> 17.7 us  [sum_at_owner(): lax.all_to_all(pieces, axis, split_axis=0, concat_axis=0, tiled=True)]
  transfers between devices with their start and end apart: 6 -> 5, of which waited for: 5 -> 4; matrix products, arithmetic and copies ran while one was open for 15% -> 28% of each run, Pallas kernels for 0% -> 16%
where the time goes in v1:
time: 382 us; the launch traced here: 377 us
  matrix products  127 us (33%)
  Pallas kernels  112 us (29%)
  local copies, waits for them, and re-layouts  42.3 us (11%)
  starting transfers between devices  37.1 us (10%)
  waiting for transfers between devices  25.8 us (7%)
  blocking collectives  17.7 us (5%)
  other arithmetic  13.4 us (4%)
    pallas_call x1, Pallas kernels, sep_solve(): pl.pallas_call(functools.partial(sep_backward_kernel, n), out_shape=(sol_...  61.8 us
    pallas_call x1, Pallas kernels, sep_solve(): pl.pallas_call(functools.partial(sep_forward_kernel, n), out_shape=sol_sh...  50 us
    dot_general x16, matrix products, evaluate(): jnp.einsum('krs,ksp->rp', coef_all, kernel, preferred_element_type=jnp.fl...  39.9 us
    dot_general x16, matrix products, top_forward(): lax.dot_general(half_all, lower_rows, (((1,), (1,)), ((), ())), preferred...  21.5 us
    dot_general x16, matrix products, top_backward(): jnp.dot(half_all, lower_cols, preferred_element_type=jnp.float32)  20.2 us
    all_to_all x1, blocking collectives, sum_at_owner(): lax.all_to_all(pieces, axis, split_axis=0, concat_axis=0, tiled=True)  17.7 us
    dot_general x16, matrix products, top_forward(): solved_block = jnp.dot(residue, inverse_block.T, precision=highest)  17.5 us
    dot_general x16, matrix products, top_backward(): solved_block = jnp.dot(residue, inverse_block, precision=highest)  16.6 us
  transfers between devices with their start and end apart: 5, of which 4 were waited for; matrix products, arithmetic and copies ran while one was open for 28% of the time, Pallas kernels for 16%

profile of v1, /device:TPU:24, one launch (start us, length us, event | category | flops | bytes accessed | tf_op | source)
XLA Modules:
  0.0 376.5 jit_solution(3485363518332588756)
XLA Ops:
  0.6 3.7 fusion.49
  7.5 17.7 %all_to_all.30 = bf16[16,1,64,256]{3,2,1,0:T(8,128)(2,1)S(1)} all-to-all(bf16[16,1,64,256]{3,2,1,0:T(8,128)(2,1)S(1)} %copy.91), channel_id=1, replica_groups=mesh['leaf'=8,'grp'=16] {'grp'}, dimensions={0} | all-to-all | bytes 1048576 | tf_op jit(solution)/shard_map/all_to_all | solution.py:27
  25.3 50.0 %shard_map.174 = f32[64,256]{1,0:T(8,128)S(1)} custom-call(f32[64,256]{1,0:T(8,128)S(1)} %sub.104.start_ref, f32[256,256]{1,0:T(8,128)S(1)} %bitcast.176, bf16[16,256,256]{2,1,0:T(8,128)(2,1)S(1)} %bitcast.174), custom_call_target="tpu_custom_call" | custom-call | tf_op jit(solution)/shard_map/pallas_call | solution.py:173
  76.4 14.6 %all-to-all-start.1 = ((bf16[16,64,128]{2,1,0:T(8,128)(2,1)}), bf16[16,64,128]{2,1,0:T(8,128)(2,1)S(1)}, u32[]{:S(2)}, u32[]{:S(2)}) async-start(bf16[16,64,128]{2,1,0:T(8,128)(2,1)} %bitcast.147), calls=%async_computation.1 | async-start | bytes 524288 | tf_op jit(solution)/shard_map/all_to_all | solution.py:27
  91.1 6.3 %all-to-all-done.1 = bf16[16,64,128]{2,1,0:T(8,128)(2,1)S(1)} async-done(((bf16[16,64,128]{2,1,0:T(8,128)(2,1)}), bf16[16,64,128]{2,1,0:T(8,128)(2,1)S(1)}, u32[]{:S(2)}, u32[]{:S(2)}) %all-to-all-start.1) | async-done | bytes 262176 | tf_op jit(solution)/shard_map/all_to_all | solution.py:27
  98.1 4.3 %all-to-all-start.2 = ((bf16[8,64,128]{2,1,0:T(8,128)(2,1)}), bf16[8,64,128]{2,1,0:T(8,128)(2,1)S(1)}, u32[]{:S(2)}, u32[]{:S(2)}) async-start(bf16[8,64,128]{2,1,0:T(8,128)(2,1)} %broadcast_in_dim.27), calls=%async_computation.2 | async-start | bytes 262144 | tf_op jit(solution)/shard_map/all_to_all | solution.py:37
  102.7 5.9 %all-to-all-done.2 = bf16[8,64,128]{2,1,0:T(8,128)(2,1)S(1)} async-done(((bf16[8,64,128]{2,1,0:T(8,128)(2,1)}), bf16[8,64,128]{2,1,0:T(8,128)(2,1)S(1)}, u32[]{:S(2)}, u32[]{:S(2)}) %all-to-all-start.2) | async-done | bytes 131104 | tf_op jit(solution)/shard_map/all_to_all | solution.py:37
  109.3 5.7 %all-to-all-start.3 = ((bf16[16,64,128]{2,1,0:T(8,128)(2,1)}), bf16[16,64,128]{2,1,0:T(8,128)(2,1)S(1)}, u32[]{:S(2)}, u32[]{:S(2)}) async-start(bf16[16,64,128]{2,1,0:T(8,128)(2,1)} %broadcast_in_dim.28), calls=%async_computation.3 | async-start | bytes 524288 | tf_op jit(solution)/shard_map/all_to_all | solution.py:37
  115.9 5.6 %all-to-all-done.3 = bf16[16,64,128]{2,1,0:T(8,128)(2,1)S(1)} async-done(((bf16[16,64,128]{2,1,0:T(8,128)(2,1)}), bf16[16,64,128]{2,1,0:T(8,128)(2,1)S(1)}, u32[]{:S(2)}, u32[]{:S(2)}) %all-to-all-start.3) | async-done | bytes 262176 | tf_op jit(solution)/shard_map/all_to_all | solution.py:37
  121.5 5.7 %all-to-all-start.4 = ((bf16[16,2,3,128]{3,1,2,0:T(2,128)(2,1)}), bf16[16,2,3,128]{3,1,2,0:T(2,128)(2,1)S(1)}, u32[]{:S(2)}, u32[]{:S(2)}) async-start(bf16[16,2,3,128]{3,1,2,0:T(2,128)(2,1)} %copy.97), calls=%async_computation.4 | async-start | bytes 49152 | tf_op jit(solution)/shard_map/all_to_all | solution.py:325
  130.0 49.1 %while.42 = (s32[]{:T(128)}, bf16[64,2048]{1,0:T(8,128)(2,1)S(1)}, f32[64,2048]{1,0:T(8,128)}, f32[64,2048]{1,0:T(8,128)}, bf16[2048,2048]{1,0:T(8,128)(2,1)}, /...) while((s32[]{:T(128)}, bf16[64,2048]{1,0:T(8,128)(2,1)S(1)}, ...), condition=%wide.region_4.5_spmd, body=%wide.region_3.4_spmd.sunk | while | flops 46153732 | bytes 1066651 | solution.py:275
  180.0 47.2 %while.43 = (s32[]{:T(128)}, bf16[64,2048]{1,0:T(8,128)(2,1)S(1)}, f32[64,2048]{1,0:T(8,128)}, f32[64,2048]{1,0:T(8,128)}, bf16[2048,2048]{1,0:T(8,128)(2,1)}, /...) while((s32[]{:T(128)}, bf16[64,2048]{1,0:T(8,128)(2,1)S(1)}, ...), condition=%wide.region_6.7_spmd, body=%wide.region_5.6_spmd.sunk | while | flops 46153736 | bytes 1066205 | solution.py:292
  230.4 61.8 %shard_map.175 = (f32[64,256]{1,0:T(8,128)S(1)}, bf16[16,64,256]{2,1,0:T(8,128)(2,1)S(1)}) custom-call(f32[64,256]{1,0:T(8,128)S(1)} %convolution_subtract_fusion.start_ref, f32[256,256]{1,0:T(8,128)S(1)} %bitcast.177, bf16[16,256,256]{2,1,0:T(8,128)(2,1)S(1)} %bitcast.175), custom_call_target="tpu_custom_call" | custom-call | tf_op jit(solution)/shard_map/pallas_call | solution.py:181
  296.3 6.7 %all-to-all-start.5 = ((bf16[16,2,64,128]{3,2,1,0:T(8,128)(2,1)}), bf16[16,2,64,128]{3,2,1,0:T(8,128)(2,1)S(1)}, u32[]{:S(2)}, u32[]{:S(2)}) async-start(bf16[16,2,64,128]{3,2,1,0:T(8,128)(2,1)} %copy.101), calls=%async_computation.5 | async-start | bytes 1048576 | tf_op jit(solution)/shard_map/all_to_all | solution.py:324
  303.1 8.0 %all-to-all-done.5 = bf16[16,2,64,128]{3,2,1,0:T(8,128)(2,1)S(1)} async-done(((bf16[16,2,64,128]{3,2,1,0:T(8,128)(2,1)}), bf16[16,2,64,128]{3,2,1,0:T(8,128)(2,1)S(1)}, u32[]{:S(2)}, u32[]{:S(2)}) %all-to-all-start.5) | async-done | bytes 524320 | tf_op jit(solution)/shard_map/all_to_all | solution.py:324
  311.1 62.7 %while.44 = (s32[]{:T(128)}, f32[16,64,128]{2,1,0:T(8,128)}, f32[32,3,128]{2,0,1:T(8,128)S(1)}, f32[16,3,128]{2,0,1:T(8,128)}, s32[16,32]{1,0:T(8,128)}, /*index...) while((s32[]{:T(128)}, f32[16,64,128]{2,1,0:T(8,128)}, f32[32,3,128]{2,0,1:T(8,128)S(1)}, ...), condition=%wide.region_10.11_spmd, body=%wide.region_9.10_spmd.sunk | while | flops 74973216 | bytes 710157 | solution.py:338
  312.5 2.5 fusion.116
  316.4 2.5 fusion.116
  320.4 2.5 fusion.116
  324.3 2.5 fusion.116
  328.2 2.5 fusion.116
  332.1 2.5 fusion.116
  336.0 2.5 fusion.116
  339.9 2.5 fusion.116
  343.9 2.5 fusion.116
  347.8 2.5 fusion.116
  351.7 2.5 fusion.116
  355.6 2.5 fusion.116
  359.5 2.5 fusion.116
  363.4 2.5 fusion.116
  367.4 2.5 fusion.116
  371.3 2.5 fusion.116
  (199 shorter events, 138.9 us)
Async XLA Ops:
  0.6 3.7 copy-start
  4.3 0.9 copy-start.9
  5.2 20.0 %copy-start.6 = (f32[64,256]{1,0:T(8,128)S(1)}, f32[64,256]{1,0:T(8,128)}, u32[]{:S(2)}) copy-start(f32[64,256]{1,0:T(8,128)} %param.22) | copy-start | bytes 196612
  7.3 18.0 %copy-start.1 = (bf16[1,16,256,256]{3,2,1,0:T(8,128)(2,1)S(1)}, bf16[1,16,256,256]{3,2,1,0:T(8,128)(2,1)}, u32[]{:S(2)}) copy-start(bf16[1,16,256,256]{3,2,1,0:T(8,128)(2,1)} %param.28) | copy-start | bytes 6291460
  7.3 18.0 %copy-start.3 = (f32[1,256,256]{2,1,0:T(8,128)S(1)}, f32[1,256,256]{2,1,0:T(8,128)}, u32[]{:S(2)}) copy-start(f32[1,256,256]{2,1,0:T(8,128)} %param.27) | copy-start | bytes 786436
  7.4 67.8 %copy-start.4 = (bf16[256,2048]{1,0:T(8,128)(2,1)S(1)}, bf16[256,2048]{1,0:T(8,128)(2,1)}, u32[]{:S(2)}) copy-start(bf16[256,2048]{1,0:T(8,128)(2,1)} %param.29) | copy-start | bytes 3145732
  25.3 65.7 %copy-start.8 = (s32[16,1]{0,1:T(1,128)S(1)}, s32[16,1]{0,1:T(1,128)}, u32[]{:S(2)}) copy-start(s32[16,1]{0,1:T(1,128)} %param.32) | copy-start | bytes 196
  75.3 39.8 %copy-start.7 = (f32[16,3,128]{2,0,1:T(8,128)S(1)}, f32[16,3,128]{2,0,1:T(8,128)}, u32[]{:S(2)}) copy-start(f32[16,3,128]{2,0,1:T(8,128)} %param.33) | copy-start | bytes 73732
  76.4 21.0 %all-to-all-start.1 = ((bf16[16,64,128]{2,1,0:T(8,128)(2,1)}), bf16[16,64,128]{2,1,0:T(8,128)(2,1)S(1)}, u32[]{:S(2)}, u32[]{:S(2)}) async-start(bf16[16,64,128]{2,1,0:T(8,128)(2,1)} %bitcast.147), calls=%async_computation.1 | async-start | bytes 524288 | tf_op jit(solution)/shard_map/all_to_all | solution.py:27
  98.1 10.4 %all-to-all-start.2 = ((bf16[8,64,128]{2,1,0:T(8,128)(2,1)}), bf16[8,64,128]{2,1,0:T(8,128)(2,1)S(1)}, u32[]{:S(2)}, u32[]{:S(2)}) async-start(bf16[8,64,128]{2,1,0:T(8,128)(2,1)} %broadcast_in_dim.27), calls=%async_computation.2 | async-start | bytes 262144 | tf_op jit(solution)/shard_map/all_to_all | solution.py:37
  109.3 12.1 %all-to-all-start.3 = ((bf16[16,64,128]{2,1,0:T(8,128)(2,1)}), bf16[16,64,128]{2,1,0:T(8,128)(2,1)S(1)}, u32[]{:S(2)}, u32[]{:S(2)}) async-start(bf16[16,64,128]{2,1,0:T(8,128)(2,1)} %broadcast_in_dim.28), calls=%async_computation.3 | async-start | bytes 524288 | tf_op jit(solution)/shard_map/all_to_all | solution.py:37
  121.5 174.8 %all-to-all-start.4 = ((bf16[16,2,3,128]{3,1,2,0:T(2,128)(2,1)}), bf16[16,2,3,128]{3,1,2,0:T(2,128)(2,1)S(1)}, u32[]{:S(2)}, u32[]{:S(2)}) async-start(bf16[16,2,3,128]{3,1,2,0:T(2,128)(2,1)} %copy.97), calls=%async_computation.4 | async-start | bytes 49152 | tf_op jit(solution)/shard_map/all_to_all | solution.py:325
  228.8 1.6 copy-start.2
  292.8 1.2 copy-start.5
  296.3 14.8 %all-to-all-start.5 = ((bf16[16,2,64,128]{3,2,1,0:T(8,128)(2,1)}), bf16[16,2,64,128]{3,2,1,0:T(8,128)(2,1)S(1)}, u32[]{:S(2)}, u32[]{:S(2)}) async-start(bf16[16,2,64,128]{3,2,1,0:T(8,128)(2,1)} %copy.101), calls=%async_computation.5 | async-start | bytes 1048576 | tf_op jit(solution)/shard_map/all_to_all | solution.py:324

commit v2 on v1

--- a/solution.py
+++ b/solution.py
@@ -188,6 +188,45 @@
     )(start, inv, blocks)
 
 
+def top_solve_kernel(nt, span, start_ref, inv_ref, lower_ref, coef_ref, half_ref, fwd_half, fwd_full):
+    for t in range(nt):
+        cols = slice(t * span, (t + 1) * span)
+        residue = start_ref[:, cols]
+        if t > 0:
+            residue = residue - _nt(fwd_half[:, : t * span], lower_ref[cols, : t * span])
+        solved = _nt_exact(residue, inv_ref[t])
+        fwd_full[:, cols] = solved
+        fwd_half[:, cols] = solved.astype(jnp.bfloat16)
+    for t in reversed(range(nt)):
+        cols = slice(t * span, (t + 1) * span)
+        residue = fwd_full[:, cols]
+        if t < nt - 1:
+            residue = residue - _nn(half_ref[:, (t + 1) * span :], lower_ref[(t + 1) * span :, cols])
+        solved = _nn_exact(residue, inv_ref[t])
+        coef_ref[:, cols] = solved
+        half_ref[:, cols] = solved.astype(jnp.bfloat16)
+
+
+def top_solve(top_start, top_inverse, top_lower):
+    nt, span = top_inverse.shape[0], top_inverse.shape[1]
+    rows, width = top_start.shape
+    vmem = pl.BlockSpec(memory_space=pltpu.VMEM)
+    return pl.pallas_call(
+        functools.partial(top_solve_kernel, nt, span),
+        out_shape=(
+            jax.ShapeDtypeStruct((rows, width), jnp.float32),
+            jax.ShapeDtypeStruct((rows, width), jnp.bfloat16),
+        ),
+        in_specs=[vmem] * 3,
+        out_specs=(vmem, vmem),
+        scratch_shapes=[
+            pltpu.VMEM((rows, width), jnp.bfloat16),
+            pltpu.VMEM((rows, width), jnp.float32),
+        ],
+        compiler_params=pltpu.CompilerParams(vmem_limit_bytes=48 * 1024 * 1024),
+    )(top_start, top_inverse, top_lower)
+
+
 def slot_ranks(dest_rows, grp_size):
     onehot = (dest_rows[..., None] == jnp.arange(grp_size)).astype(jnp.int32)
     before = jnp.cumsum(onehot, axis=-2) - onehot
@@ -251,45 +290,7 @@
     top_part = over_copies(top_part.astype(jnp.bfloat16), "leaf").astype(jnp.float32)
     top_total = gather_directly(top_part.astype(jnp.bfloat16), "grp", 1).astype(top_part.dtype)
     top_start = rhs_top - top_total
-    top_count = top_inverse.shape[0]
-    top_span = top_inverse.shape[1]
-
-    def top_forward(block_id, carry):
-        half_all, full_all = carry
-        lower_rows = lax.dynamic_slice_in_dim(top_lower, block_id * top_span, top_span, 0)
-        residue = lax.dynamic_slice_in_dim(
-            top_start, block_id * top_span, top_span, 1
-        ) - lax.dot_general(
-            half_all, lower_rows, (((1,), (1,)), ((), ())), preferred_element_type=jnp.float32
-        )
-        inverse_block = lax.dynamic_index_in_dim(top_inverse, block_id, 0, keepdims=False)
-        solved_block = jnp.dot(residue, inverse_block.T, precision=highest)
-        half_all = lax.dynamic_update_slice_in_dim(
-            half_all, solved_block.astype(jnp.bfloat16), block_id * top_span, 1
-        )
-        full_all = lax.dynamic_update_slice_in_dim(full_all, solved_block, block_id * top_span, 1)
-        return (half_all, full_all)
-
-    empty_half = jnp.zeros(top_start.shape, jnp.bfloat16)
-    empty_full = jnp.zeros(top_start.shape, jnp.float32)
-    leftover_half, top_fwd = lax.fori_loop(0, top_count, top_forward, (empty_half, empty_full))
-
-    def top_backward(step_id, carry):
-        half_all, full_all = carry
-        block_id = top_count - 1 - step_id
-        lower_cols = lax.dynamic_slice_in_dim(top_lower, block_id * top_span, top_span, 1)
-        residue = lax.dynamic_slice_in_dim(top_fwd, block_id * top_span, top_span, 1) - jnp.dot(
-            half_all, lower_cols, preferred_element_type=jnp.float32
-        )
-        inverse_block = lax.dynamic_index_in_dim(top_inverse, block_id, 0, keepdims=False)
-        solved_block = jnp.dot(residue, inverse_block, precision=highest)
-        half_all = lax.dynamic_update_slice_in_dim(
-            half_all, solved_block.astype(jnp.bfloat16), block_id * top_span, 1
-        )
-        full_all = lax.dynamic_update_slice_in_dim(full_all, solved_block, block_id * top_span, 1)
-        return (half_all, full_all)
-
-    top_half, coef_top = lax.fori_loop(0, top_count, top_backward, (empty_half, empty_full))
+    coef_top, top_half = top_solve(top_start, top_inverse, top_lower)
     back_start = sep_sol - lax.dot_general(
         top_half, top_coupling, (((1,), (1,)), ((), ())), preferred_element_type=jnp.float32
     )

time: 382 us -> 299 us (0.78)
  matrix products: 127 us -> 50 us
  local copies, waits for them, and re-layouts: 42.3 us -> 19 us
  Pallas kernels: 112 us -> 129 us
    dot_general x64 -> x0, matrix products: 75.7 us -> none  [the longest x16 21.5 us: top_forward(): lax.dot_general(half_all, lower_rows, (((1,), (1,)), ((), ())), preferred...]
    dynamic_update_slice x32 -> x0, local copies, waits for them, and re-layouts: 20 us -> none  [the longest x16 9.98 us: top_backward(): lax.dynamic_update_slice_in_dim(full_all, solved_block, block_id * top_sp...]
    pallas_call x0 -> x1, Pallas kernels: none -> 16.9 us  [top_solve(): pl.pallas_call(functools.partial(top_solve_kernel, nt, span), out_shape=(...]
  transfers between devices with their start and end apart: 5 -> 5, of which waited for: 4 -> 4; matrix products, arithmetic and copies ran while one was open for 28% -> 2% of each run, Pallas kernels for 16% -> 27%
where the time goes in v2:
time: 299 us; the launch traced here: 295 us
  Pallas kernels  129 us (43%)
  matrix products  50 us (17%)
  starting transfers between devices  37.5 us (13%)
  waiting for transfers between devices  26.2 us (9%)
  local copies, waits for them, and re-layouts  19 us (6%)
  blocking collectives  17.7 us (6%)
  other arithmetic  14.5 us (5%)
    pallas_call x1, Pallas kernels, sep_solve(): pl.pallas_call(functools.partial(sep_backward_kernel, n), out_shape=(sol_...  62.2 us
    pallas_call x1, Pallas kernels, sep_solve(): pl.pallas_call(functools.partial(sep_forward_kernel, n), out_shape=sol_sh...  50 us
    dot_general x16, matrix products, evaluate(): jnp.einsum('krs,ksp->rp', coef_all, kernel, preferred_element_type=jnp.fl...  40 us
    all_to_all x1, blocking collectives, sum_at_owner(): lax.all_to_all(pieces, axis, split_axis=0, concat_axis=0, tiled=True)  17.7 us
    pallas_call x1, Pallas kernels, top_solve(): pl.pallas_call(functools.partial(top_solve_kernel, nt, span), out_shape=(...  16.9 us
    all_to_all x1, starting transfers between devices, sum_at_owner(): lax.all_to_all(pieces, axis, split_axis=0, concat_axis=0, tiled=True)  14.6 us
    all_to_all x2, waiting for transfers between devices, copy_for_each(): return lax.all_to_all(copies, axis, split_axis=0, concat_axis=0, tiled=True)  11.8 us
    sub x32, local copies, waits for them, and re-layouts, evaluate(): delta = centre_all[:, comp, :, None] - block_points[None, comp, None, :]  11.7 us
  transfers between devices with their start and end apart: 5, of which 4 were waited for; matrix products, arithmetic and copies ran while one was open for 2% of the time, Pallas kernels for 27%

profile of v2, /device:TPU:24, one launch (start us, length us, event | category | flops | bytes accessed | tf_op | source)
XLA Modules:
  0.0 295.0 jit_solution(9936755637699530685)
XLA Ops:
  0.6 3.7 %fusion.35 = f32[16,64,128]{2,1,0:T(8,128)S(1)} fusion(f32[16,128,128]{2,1,0:T(8,128)} %param.20, f32[64,2048]{1,0:T(8,128)} %param.17), kind=kOutput, calls=%fused_computation.49 | convolution fusion | flops 201326592 | bytes 2097152 | tf_op jit(solution)/shard_map/nrs,nts->nrt/dot_general | solution.py:270
  7.5 17.7 %all_to_all.30 = bf16[16,1,64,256]{3,2,1,0:T(8,128)(2,1)S(1)} all-to-all(bf16[16,1,64,256]{3,2,1,0:T(8,128)(2,1)S(1)} %copy.77), channel_id=1, replica_groups=mesh['leaf'=8,'grp'=16] {'grp'}, dimensions={0} | all-to-all | bytes 1048576 | tf_op jit(solution)/shard_map/all_to_all | solution.py:27
  25.3 50.0 %shard_map.174 = f32[64,256]{1,0:T(8,128)S(1)} custom-call(f32[64,256]{1,0:T(8,128)S(1)} %sub.77.start_ref, f32[256,256]{1,0:T(8,128)S(1)} %bitcast.138, bf16[16,256,256]{2,1,0:T(8,128)(2,1)S(1)} %bitcast.136), custom_call_target="tpu_custom_call" | custom-call | tf_op jit(solution)/shard_map/pallas_call | solution.py:173
  76.4 14.6 %all-to-all-start.1 = ((bf16[16,64,128]{2,1,0:T(8,128)(2,1)}), bf16[16,64,128]{2,1,0:T(8,128)(2,1)}, u32[]{:S(2)}, u32[]{:S(2)}) async-start(bf16[16,64,128]{2,1,0:T(8,128)(2,1)} %bitcast.141), calls=%async_computation.1 | async-start | bytes 524288 | tf_op jit(solution)/shard_map/all_to_all | solution.py:27
  91.1 6.4 %all-to-all-done.1 = bf16[16,64,128]{2,1,0:T(8,128)(2,1)} async-done(((bf16[16,64,128]{2,1,0:T(8,128)(2,1)}), bf16[16,64,128]{2,1,0:T(8,128)(2,1)}, u32[]{:S(2)}, u32[]{:S(2)}) %all-to-all-start.1) | async-done | bytes 262176 | tf_op jit(solution)/shard_map/all_to_all | solution.py:27
  99.2 4.3 %all-to-all-start.2 = ((bf16[8,64,128]{2,1,0:T(8,128)(2,1)}), bf16[8,64,128]{2,1,0:T(8,128)(2,1)}, u32[]{:S(2)}, u32[]{:S(2)}) async-start(bf16[8,64,128]{2,1,0:T(8,128)(2,1)} %broadcast_in_dim.9), calls=%async_computation.2 | async-start | bytes 262144 | tf_op jit(solution)/shard_map/all_to_all | solution.py:37
  103.8 6.0 %all-to-all-done.2 = bf16[8,64,128]{2,1,0:T(8,128)(2,1)} async-done(((bf16[8,64,128]{2,1,0:T(8,128)(2,1)}), bf16[8,64,128]{2,1,0:T(8,128)(2,1)}, u32[]{:S(2)}, u32[]{:S(2)}) %all-to-all-start.2) | async-done | bytes 131104 | tf_op jit(solution)/shard_map/all_to_all | solution.py:37
  111.5 6.2 %all-to-all-start.3 = ((bf16[16,64,128]{2,1,0:T(8,128)(2,1)}), bf16[16,64,128]{2,1,0:T(8,128)(2,1)}, u32[]{:S(2)}, u32[]{:S(2)}) async-start(bf16[16,64,128]{2,1,0:T(8,128)(2,1)} %broadcast_in_dim.20), calls=%async_computation.3 | async-start | bytes 524288 | tf_op jit(solution)/shard_map/all_to_all | solution.py:37
  118.4 5.8 %all-to-all-done.3 = bf16[16,64,128]{2,1,0:T(8,128)(2,1)} async-done(((bf16[16,64,128]{2,1,0:T(8,128)(2,1)}), bf16[16,64,128]{2,1,0:T(8,128)(2,1)}, u32[]{:S(2)}, u32[]{:S(2)}) %all-to-all-start.3) | async-done | bytes 262176 | tf_op jit(solution)/shard_map/all_to_all | solution.py:37
  124.2 5.8 %all-to-all-start.4 = ((bf16[16,2,3,128]{3,1,2,0:T(2,128)(2,1)}), bf16[16,2,3,128]{3,1,2,0:T(2,128)(2,1)S(1)}, u32[]{:S(2)}, u32[]{:S(2)}) async-start(bf16[16,2,3,128]{3,1,2,0:T(2,128)(2,1)} %copy.83), calls=%async_computation.4 | async-start | bytes 49152 | tf_op jit(solution)/shard_map/all_to_all | solution.py:326
  131.2 16.9 %shard_map.175 = (f32[64,2048]{1,0:T(8,128)}, bf16[64,2048]{1,0:T(8,128)(2,1)S(1)}) custom-call(f32[64,2048]{1,0:T(8,128)S(1)} %bitcast_subtract_fusion.start_ref, f32[16,128,128]{2,1,0:T(8,128)S(1)} %copy-done.3, bf16[2048,2048]{1,0:T(8,128)(2,1)} %lower_ref.1), custom_call_target="tpu_custom_call" | custom-call | tf_op jit(solution)/shard_map/pallas_call | solution.py:214
  148.5 62.2 %shard_map.176 = (f32[64,256]{1,0:T(8,128)S(1)}, bf16[16,64,256]{2,1,0:T(8,128)(2,1)S(1)}) custom-call(f32[64,256]{1,0:T(8,128)S(1)} %convolution_subtract_fusion.start_ref, f32[256,256]{1,0:T(8,128)S(1)} %bitcast.139, bf16[16,256,256]{2,1,0:T(8,128)(2,1)S(1)} %bitcast.137), custom_call_target="tpu_custom_call" | custom-call | tf_op jit(solution)/shard_map/pallas_call | solution.py:181
  214.7 6.7 %all-to-all-start.5 = ((bf16[16,2,64,128]{3,2,1,0:T(8,128)(2,1)}), bf16[16,2,64,128]{3,2,1,0:T(8,128)(2,1)S(1)}, u32[]{:S(2)}, u32[]{:S(2)}) async-start(bf16[16,2,64,128]{3,2,1,0:T(8,128)(2,1)} %copy.87), calls=%async_computation.5 | async-start | bytes 1048576 | tf_op jit(solution)/shard_map/all_to_all | solution.py:325
  221.4 8.0 %all-to-all-done.5 = bf16[16,2,64,128]{3,2,1,0:T(8,128)(2,1)S(1)} async-done(((bf16[16,2,64,128]{3,2,1,0:T(8,128)(2,1)}), bf16[16,2,64,128]{3,2,1,0:T(8,128)(2,1)S(1)}, u32[]{:S(2)}, u32[]{:S(2)}) %all-to-all-start.5) | async-done | bytes 524320 | tf_op jit(solution)/shard_map/all_to_all | solution.py:325
  229.5 62.8 %while.10 = (s32[]{:T(128)}, f32[16,64,128]{2,1,0:T(8,128)}, f32[32,3,128]{2,0,1:T(8,128)S(1)}, f32[16,3,128]{2,0,1:T(8,128)}, s32[16,32]{1,0:T(8,128)}, /*index...) while((s32[]{:T(128)}, f32[16,64,128]{2,1,0:T(8,128)}, f32[32,3,128]{2,0,1:T(8,128)S(1)}, ...), condition=%wide.region_6.7_spmd, body=%wide.region_5.6_spmd.sunk | while | flops 74973216 | bytes 710157 | solution.py:339
  230.9 2.5 fusion.82
  234.8 2.5 fusion.82
  238.7 2.5 fusion.82
  242.7 2.5 fusion.82
  246.6 2.5 fusion.82
  250.5 2.5 fusion.82
  254.4 2.5 fusion.82
  258.4 2.5 fusion.82
  262.3 2.5 fusion.82
  266.2 2.5 fusion.82
  270.1 2.5 fusion.82
  274.1 2.5 fusion.82
  278.0 2.5 fusion.82
  281.9 2.5 fusion.82
  285.8 2.5 fusion.82
  289.8 2.5 fusion.82
  292.3 2.1 copy_bitcast_fusion
  (106 shorter events, 37.7 us)
Async XLA Ops:
  0.6 3.7 %copy-start = (bf16[16,2,256,128]{3,2,1,0:T(8,128)(2,1)S(1)}, bf16[16,2,256,128]{3,2,1,0:T(8,128)(2,1)}, u32[]{:S(2)}) copy-start(bf16[16,2,256,128]{3,2,1,0:T(8,128)(2,1)} %param.21) | copy-start | bytes 6291460
  4.3 0.9 copy-start.5
  4.3 0.9 copy-start.13
  5.2 20.0 %copy-start.10 = (f32[64,256]{1,0:T(8,128)S(1)}, f32[64,256]{1,0:T(8,128)}, u32[]{:S(2)}) copy-start(f32[64,256]{1,0:T(8,128)} %param.18) | copy-start | bytes 196612
  7.3 18.0 %copy-start.1 = (bf16[1,16,256,256]{3,2,1,0:T(8,128)(2,1)S(1)}, bf16[1,16,256,256]{3,2,1,0:T(8,128)(2,1)}, u32[]{:S(2)}) copy-start(bf16[1,16,256,256]{3,2,1,0:T(8,128)(2,1)} %param.24) | copy-start | bytes 6291460
  7.3 18.0 %copy-start.4 = (f32[1,256,256]{2,1,0:T(8,128)S(1)}, f32[1,256,256]{2,1,0:T(8,128)}, u32[]{:S(2)}) copy-start(f32[1,256,256]{2,1,0:T(8,128)} %param.23) | copy-start | bytes 786436
  7.5 67.8 %copy-start.7 = (bf16[256,2048]{1,0:T(8,128)(2,1)S(1)}, bf16[256,2048]{1,0:T(8,128)(2,1)}, u32[]{:S(2)}) copy-start(bf16[256,2048]{1,0:T(8,128)(2,1)} %param.25) | copy-start | bytes 3145732
  25.3 65.8 %copy-start.12 = (s32[16,1]{0,1:T(1,128)S(1)}, s32[16,1]{0,1:T(1,128)}, u32[]{:S(2)}) copy-start(s32[16,1]{0,1:T(1,128)} %param.28) | copy-start | bytes 196
  75.3 42.3 %copy-start.11 = (f32[16,3,128]{2,0,1:T(8,128)S(1)}, f32[16,3,128]{2,0,1:T(8,128)}, u32[]{:S(2)}) copy-start(f32[16,3,128]{2,0,1:T(8,128)} %param.29) | copy-start | bytes 73732
  75.6 55.5 %copy-start.3 = (f32[16,128,128]{2,1,0:T(8,128)S(1)}, f32[16,128,128]{2,1,0:T(8,128)}, u32[]{:S(2)}) copy-start(f32[16,128,128]{2,1,0:T(8,128)} %inv_ref.1) | copy-start | bytes 3145732
  76.4 21.2 %all-to-all-start.1 = ((bf16[16,64,128]{2,1,0:T(8,128)(2,1)}), bf16[16,64,128]{2,1,0:T(8,128)(2,1)}, u32[]{:S(2)}, u32[]{:S(2)}) async-start(bf16[16,64,128]{2,1,0:T(8,128)(2,1)} %bitcast.141), calls=%async_computation.1 | async-start | bytes 524288 | tf_op jit(solution)/shard_map/all_to_all | solution.py:27
  99.2 10.5 %all-to-all-start.2 = ((bf16[8,64,128]{2,1,0:T(8,128)(2,1)}), bf16[8,64,128]{2,1,0:T(8,128)(2,1)}, u32[]{:S(2)}, u32[]{:S(2)}) async-start(bf16[8,64,128]{2,1,0:T(8,128)(2,1)} %broadcast_in_dim.9), calls=%async_computation.2 | async-start | bytes 262144 | tf_op jit(solution)/shard_map/all_to_all | solution.py:37
  111.5 12.7 %all-to-all-start.3 = ((bf16[16,64,128]{2,1,0:T(8,128)(2,1)}), bf16[16,64,128]{2,1,0:T(8,128)(2,1)}, u32[]{:S(2)}, u32[]{:S(2)}) async-start(bf16[16,64,128]{2,1,0:T(8,128)(2,1)} %broadcast_in_dim.20), calls=%async_computation.3 | async-start | bytes 524288 | tf_op jit(solution)/shard_map/all_to_all | solution.py:37
  124.2 90.5 %all-to-all-start.4 = ((bf16[16,2,3,128]{3,1,2,0:T(2,128)(2,1)}), bf16[16,2,3,128]{3,1,2,0:T(2,128)(2,1)S(1)}, u32[]{:S(2)}, u32[]{:S(2)}) async-start(bf16[16,2,3,128]{3,1,2,0:T(2,128)(2,1)} %copy.83), calls=%async_computation.4 | async-start | bytes 49152 | tf_op jit(solution)/shard_map/all_to_all | solution.py:326
  131.1 16.9 %copy-start.8 = (bf16[256,2048]{1,0:T(8,128)(2,1)S(1)}, bf16[256,2048]{1,0:T(8,128)(2,1)}, u32[]{:S(2)}) copy-start(bf16[256,2048]{1,0:T(8,128)(2,1)} %param.25) | copy-start | bytes 3145732
  131.2 17.3 %copy-start.2 = (bf16[1,16,256,256]{3,2,1,0:T(8,128)(2,1)S(1)}, bf16[1,16,256,256]{3,2,1,0:T(8,128)(2,1)}, u32[]{:S(2)}) copy-start(bf16[1,16,256,256]{3,2,1,0:T(8,128)(2,1)} %param.24) | copy-start | bytes 6291460
  148.5 62.7 %copy-start.6 = (f32[16,64,128]{2,1,0:T(8,128)S(1)}, f32[16,64,128]{2,1,0:T(8,128)}, u32[]{:S(2)}) copy-start(f32[16,64,128]{2,1,0:T(8,128)} %copy-done.5) | copy-start | bytes 1572868
  211.2 1.2 copy-start.9
  214.7 14.7 %all-to-all-start.5 = ((bf16[16,2,64,128]{3,2,1,0:T(8,128)(2,1)}), bf16[16,2,64,128]{3,2,1,0:T(8,128)(2,1)S(1)}, u32[]{:S(2)}, u32[]{:S(2)}) async-start(bf16[16,2,64,128]{3,2,1,0:T(8,128)(2,1)} %copy.87), calls=%async_computation.5 | async-start | bytes 1048576 | tf_op jit(solution)/shard_map/all_to_all | solution.py:325

commit v3 on v2

--- a/solution.py
+++ b/solution.py
@@ -227,6 +227,54 @@
     )(top_start, top_inverse, top_lower)
 
 
+def evaluate_kernel(slots, pattern_ref, coef_ref, centre_ref, column_ref, out_ref, acc):
+    m = pl.program_id(0)
+    acc[...] = jnp.zeros_like(acc)
+    column = column_ref[0]
+
+    def one_slot(s, carry):
+        flag = pattern_ref[m, s]
+
+        @pl.when(flag != 0)
+        def _():
+            centre = centre_ref[s]
+            dist = jnp.zeros((column.shape[0], centre.shape[1]), jnp.float32)
+            for comp in range(3):
+                delta = centre[comp : comp + 1, :] - column[:, comp : comp + 1]
+                dist = dist + delta * delta
+            weight = jnp.maximum(1.0 - dist / support_sq, 0.0)
+            weight = weight * weight * weight
+            kernel = (weight * flag.astype(jnp.float32)).astype(jnp.bfloat16)
+            acc[...] += _nt(coef_ref[s], kernel)
+
+        return carry
+
+    lax.fori_loop(0, slots, one_slot, 0)
+    out_ref[...] = acc[...]
+
+
+def evaluate_all(coef_all, centre_all, point_columns, pattern):
+    slots, rows, span = coef_all.shape
+    blocks = point_columns.shape[0]
+    full = lambda shape: pl.BlockSpec(shape, lambda m, pat: (0,) * len(shape))
+    grid_spec = pltpu.PrefetchScalarGridSpec(
+        num_scalar_prefetch=1,
+        grid=(blocks,),
+        in_specs=[
+            full(coef_all.shape),
+            full(centre_all.shape),
+            pl.BlockSpec((1, span, point_columns.shape[2]), lambda m, pat: (m, 0, 0)),
+        ],
+        out_specs=pl.BlockSpec((rows, span), lambda m, pat: (0, m)),
+        scratch_shapes=[pltpu.VMEM((rows, span), jnp.float32)],
+    )
+    return pl.pallas_call(
+        functools.partial(evaluate_kernel, slots),
+        out_shape=jax.ShapeDtypeStruct((rows, blocks * span), jnp.float32),
+        grid_spec=grid_spec,
+    )(pattern, coef_all, centre_all, point_columns)
+
+
 def slot_ranks(dest_rows, grp_size):
     onehot = (dest_rows[..., None] == jnp.arange(grp_size)).astype(jnp.int32)
     before = jnp.cumsum(onehot, axis=-2) - onehot
@@ -331,13 +379,8 @@
     coef_all = received.reshape(slot_total, snapshots, span)
     centre_all = recv_centre.reshape(slot_total, 3, span)
     point_blocks = eval_pattern.shape[0]
-    pts_blocks = points[0].reshape(3, point_blocks, span).transpose(1, 0, 2)
-
-    def one_block(block_item):
-        return evaluate(coef_all, centre_all, block_item[0], block_item[1])
-
-    blocks_out = lax.map(one_block, (pts_blocks, eval_pattern))
-    values = blocks_out.transpose(1, 0, 2).reshape(snapshots, point_blocks * span)
+    point_columns = points[0].T.reshape(point_blocks, span, points.shape[1])
+    values = evaluate_all(coef_all, centre_all, point_columns, eval_pattern)
     return (coef_leaf, coef_sep, coef_top, values)
 
 

time: 299 us -> 311 us (1.040); the launches traced: 295 us -> 310 us
  Pallas kernels: 129 us -> 208 us
  matrix products: 50 us -> 9.92 us
  other arithmetic: 14.5 us -> 3.47 us
  local copies, waits for them, and re-layouts: 19 us -> 9.33 us
  waiting for transfers between devices: 26.2 us -> 23 us
    pallas_call x0 -> x1, Pallas kernels: none -> 79.5 us  [evaluate_all(): pl.pallas_call(functools.partial(evaluate_kernel, slots), out_shape=jax.S...]
    dot_general x16 -> x0, matrix products: 40 us -> none  [evaluate(): jnp.einsum('krs,ksp->rp', coef_all, kernel, preferred_element_type=jnp.fl...]
    sub x32 -> x0, local copies, waits for them, and re-layouts: 11.7 us -> none  [evaluate(): delta = centre_all[:, comp, :, None] - block_points[None, comp, None, :]]
    convert_element_type x16 -> x0, other arithmetic: 11.1 us -> none  [evaluate(): block_mask.astype(jnp.float32)[:, None, None]]
  transfers between devices with their start and end apart: 5 -> 5, of which waited for: 4 -> 4; matrix products, arithmetic and copies ran while one was open for 2% -> 3% of each run, Pallas kernels for 27% -> 25%
where the time goes in v3:
time: 311 us; the launch traced here: 310 us
  Pallas kernels  208 us (67%)
  starting transfers between devices  37.6 us (12%)
  waiting for transfers between devices  23 us (7%)
  blocking collectives  17.7 us (6%)
  matrix products  9.92 us (3%)
  local copies, waits for them, and re-layouts  9.33 us (3%)
  other arithmetic  3.47 us (1%)
    pallas_call x1, Pallas kernels, evaluate_all(): pl.pallas_call(functools.partial(evaluate_kernel, slots), out_shape=jax.S...  79.5 us
    pallas_call x1, Pallas kernels, sep_solve(): pl.pallas_call(functools.partial(sep_backward_kernel, n), out_shape=(sol_...  62.2 us
    pallas_call x1, Pallas kernels, sep_solve(): pl.pallas_call(functools.partial(sep_forward_kernel, n), out_shape=sol_sh...  50 us
    all_to_all x1, blocking collectives, sum_at_owner(): lax.all_to_all(pieces, axis, split_axis=0, concat_axis=0, tiled=True)  17.7 us
    pallas_call x1, Pallas kernels, top_solve(): pl.pallas_call(functools.partial(top_solve_kernel, nt, span), out_shape=(...  16.9 us
    all_to_all x1, starting transfers between devices, sum_at_owner(): lax.all_to_all(pieces, axis, split_axis=0, concat_axis=0, tiled=True)  14.6 us
    all_to_all x2, starting transfers between devices, copy_for_each(): return lax.all_to_all(copies, axis, split_axis=0, concat_axis=0, tiled=True)  10.5 us
    all_to_all x2, waiting for transfers between devices, copy_for_each(): return lax.all_to_all(copies, axis, split_axis=0, concat_axis=0, tiled=True)  9.97 us
  transfers between devices with their start and end apart: 5, of which 4 were waited for; matrix products, arithmetic and copies ran while one was open for 3% of the time, Pallas kernels for 25%

profile of v3, /device:TPU:24, one launch (start us, length us, event | category | flops | bytes accessed | tf_op | source)
XLA Modules:
  0.0 310.4 jit_solution(5348636835771089089)
XLA Ops:
  0.6 3.7 %fusion.14 = f32[16,64,128]{2,1,0:T(8,128)S(1)} fusion(f32[16,128,128]{2,1,0:T(8,128)} %param.18, f32[64,2048]{1,0:T(8,128)} %param.15), kind=kOutput, calls=%fused_computation.19 | convolution fusion | flops 201326592 | bytes 2097152 | tf_op jit(solution)/shard_map/nrs,nts->nrt/dot_general | solution.py:318
  4.3 0.9 convolution_bitcast_fusion
  5.2 2.0 fusion.8
  7.5 17.7 %all_to_all.30 = bf16[16,1,64,256]{3,2,1,0:T(8,128)(2,1)S(1)} all-to-all(bf16[16,1,64,256]{3,2,1,0:T(8,128)(2,1)S(1)} %copy.74), channel_id=1, replica_groups=mesh['leaf'=8,'grp'=16] {'grp'}, dimensions={0} | all-to-all | bytes 1048576 | tf_op jit(solution)/shard_map/all_to_all | solution.py:27
  25.3 50.0 %shard_map.174 = f32[64,256]{1,0:T(8,128)S(1)} custom-call(f32[64,256]{1,0:T(8,128)S(1)} %sub.23.start_ref, f32[256,256]{1,0:T(8,128)S(1)} %bitcast.96, bf16[16,256,256]{2,1,0:T(8,128)(2,1)S(1)} %bitcast.94), custom_call_target="tpu_custom_call" | custom-call | tf_op jit(solution)/shard_map/pallas_call | solution.py:173
  75.6 0.8 copy.125
  76.4 14.6 %all-to-all-start.1 = ((bf16[16,64,128]{2,1,0:T(8,128)(2,1)}), bf16[16,64,128]{2,1,0:T(8,128)(2,1)}, u32[]{:S(2)}, u32[]{:S(2)}) async-start(bf16[16,64,128]{2,1,0:T(8,128)(2,1)} %bitcast.92), calls=%async_computation.1 | async-start | bytes 524288 | tf_op jit(solution)/shard_map/all_to_all | solution.py:27
  91.1 6.4 %all-to-all-done.1 = bf16[16,64,128]{2,1,0:T(8,128)(2,1)} async-done(((bf16[16,64,128]{2,1,0:T(8,128)(2,1)}), bf16[16,64,128]{2,1,0:T(8,128)(2,1)}, u32[]{:S(2)}, u32[]{:S(2)}) %all-to-all-start.1) | async-done | bytes 262176 | tf_op jit(solution)/shard_map/all_to_all | solution.py:27
  97.6 1.0 reduce_sum.43
  98.6 0.7 broadcast_in_dim.4
  99.2 4.3 %all-to-all-start.2 = ((bf16[8,64,128]{2,1,0:T(8,128)(2,1)}), bf16[8,64,128]{2,1,0:T(8,128)(2,1)}, u32[]{:S(2)}, u32[]{:S(2)}) async-start(bf16[8,64,128]{2,1,0:T(8,128)(2,1)} %broadcast_in_dim.4), calls=%async_computation.2 | async-start | bytes 262144 | tf_op jit(solution)/shard_map/all_to_all | solution.py:37
  103.8 6.0 %all-to-all-done.2 = bf16[8,64,128]{2,1,0:T(8,128)(2,1)} async-done(((bf16[8,64,128]{2,1,0:T(8,128)(2,1)}), bf16[8,64,128]{2,1,0:T(8,128)(2,1)}, u32[]{:S(2)}, u32[]{:S(2)}) %all-to-all-start.2) | async-done | bytes 131104 | tf_op jit(solution)/shard_map/all_to_all | solution.py:37
  109.8 0.9 reduce_sum.44
  110.7 0.8 broadcast_in_dim.5
  111.5 6.2 %all-to-all-start.3 = ((bf16[16,64,128]{2,1,0:T(8,128)(2,1)}), bf16[16,64,128]{2,1,0:T(8,128)(2,1)}, u32[]{:S(2)}, u32[]{:S(2)}) async-start(bf16[16,64,128]{2,1,0:T(8,128)(2,1)} %broadcast_in_dim.5), calls=%async_computation.3 | async-start | bytes 524288 | tf_op jit(solution)/shard_map/all_to_all | solution.py:37
  118.2 0.6 copy.82
  118.9 1.4 copy.85
  120.2 4.0 %all-to-all-done.3 = bf16[16,64,128]{2,1,0:T(8,128)(2,1)} async-done(((bf16[16,64,128]{2,1,0:T(8,128)(2,1)}), bf16[16,64,128]{2,1,0:T(8,128)(2,1)}, u32[]{:S(2)}, u32[]{:S(2)}) %all-to-all-start.3) | async-done | bytes 262176 | tf_op jit(solution)/shard_map/all_to_all | solution.py:37
  124.2 5.8 %all-to-all-start.5 = ((bf16[16,2,3,128]{3,1,2,0:T(2,128)(2,1)}), bf16[16,2,3,128]{3,1,2,0:T(2,128)(2,1)S(1)}, u32[]{:S(2)}, u32[]{:S(2)}) async-start(bf16[16,2,3,128]{3,1,2,0:T(2,128)(2,1)} %copy.82), calls=%async_computation.5 | async-start | bytes 49152 | tf_op jit(solution)/shard_map/all_to_all | solution.py:374
  130.0 1.2 bitcast_subtract_fusion.start_ref
  131.2 16.9 %shard_map.175 = (f32[64,2048]{1,0:T(8,128)}, bf16[64,2048]{1,0:T(8,128)(2,1)S(1)}) custom-call(f32[64,2048]{1,0:T(8,128)S(1)} %bitcast_subtract_fusion.start_ref, f32[16,128,128]{2,1,0:T(8,128)S(1)} %copy-done.3, bf16[2048,2048]{1,0:T(8,128)(2,1)} %lower_ref.1), custom_call_target="tpu_custom_call" | custom-call | tf_op jit(solution)/shard_map/pallas_call | solution.py:214
  148.5 62.2 %shard_map.176 = (f32[64,256]{1,0:T(8,128)S(1)}, bf16[16,64,256]{2,1,0:T(8,128)(2,1)S(1)}) custom-call(f32[64,256]{1,0:T(8,128)S(1)} %convolution_subtract_fusion.start_ref, f32[256,256]{1,0:T(8,128)S(1)} %bitcast.97, bf16[16,256,256]{2,1,0:T(8,128)(2,1)S(1)} %bitcast.95), custom_call_target="tpu_custom_call" | custom-call | tf_op jit(solution)/shard_map/pallas_call | solution.py:181
  211.2 0.6 fusion.11
  212.4 1.1 fusion.39
  213.8 0.9 copy.81
  214.8 6.7 %all-to-all-start.4 = ((bf16[16,2,64,128]{3,2,1,0:T(8,128)(2,1)}), bf16[16,2,64,128]{3,2,1,0:T(8,128)(2,1)S(1)}, u32[]{:S(2)}, u32[]{:S(2)}) async-start(bf16[16,2,64,128]{3,2,1,0:T(8,128)(2,1)} %copy.81), calls=%async_computation.4 | async-start | bytes 1048576 | tf_op jit(solution)/shard_map/all_to_all | solution.py:373
  221.5 0.7 copy.84
  222.1 0.8 copy_bitcast_fusion
  222.9 6.6 %all-to-all-done.4 = bf16[16,2,64,128]{3,2,1,0:T(8,128)(2,1)S(1)} async-done(((bf16[16,2,64,128]{3,2,1,0:T(8,128)(2,1)}), bf16[16,2,64,128]{3,2,1,0:T(8,128)(2,1)S(1)}, u32[]{:S(2)}, u32[]{:S(2)}) %all-to-all-start.4) | async-done | bytes 524320 | tf_op jit(solution)/shard_map/all_to_all | solution.py:373
  229.5 0.8 copy-done.10
  230.3 79.5 %shard_map.177 = f32[64,2048]{1,0:T(8,128)} custom-call(s32[16,32]{1,0:T(8,128)} %pattern_ref.1, bf16[32,64,128]{2,1,0:T(8,128)(2,1)} %bitcast.99, f32[32,3,128]{2,1,0:T(4,128)} %bitcast.100, f32[16,128,3]{2,1,0:T(8,128)} %bitcast.98), custom_call_target="tpu_custom_call" | custom-call | tf_op jit(solution)/shard_map/pallas_call | solution.py:271
  309.8 0.6 copy.128
  (57 shorter events, 3.4 us)
Async XLA Ops:
  0.6 3.7 %copy-start = (bf16[16,2,256,128]{3,2,1,0:T(8,128)(2,1)S(1)}, bf16[16,2,256,128]{3,2,1,0:T(8,128)(2,1)}, u32[]{:S(2)}) copy-start(bf16[16,2,256,128]{3,2,1,0:T(8,128)(2,1)} %param.19) | copy-start | bytes 6291460
  4.3 0.9 copy-start.5
  4.3 0.9 copy-start.17
  5.2 20.0 %copy-start.11 = (f32[64,256]{1,0:T(8,128)S(1)}, f32[64,256]{1,0:T(8,128)}, u32[]{:S(2)}) copy-start(f32[64,256]{1,0:T(8,128)} %param.16) | copy-start | bytes 196612
  7.3 18.0 %copy-start.1 = (bf16[1,16,256,256]{3,2,1,0:T(8,128)(2,1)S(1)}, bf16[1,16,256,256]{3,2,1,0:T(8,128)(2,1)}, u32[]{:S(2)}) copy-start(bf16[1,16,256,256]{3,2,1,0:T(8,128)(2,1)} %param.22) | copy-start | bytes 6291460
  7.3 18.0 %copy-start.4 = (f32[1,256,256]{2,1,0:T(8,128)S(1)}, f32[1,256,256]{2,1,0:T(8,128)}, u32[]{:S(2)}) copy-start(f32[1,256,256]{2,1,0:T(8,128)} %param.21) | copy-start | bytes 786436
  7.5 67.8 %copy-start.7 = (bf16[256,2048]{1,0:T(8,128)(2,1)S(1)}, bf16[256,2048]{1,0:T(8,128)(2,1)}, u32[]{:S(2)}) copy-start(bf16[256,2048]{1,0:T(8,128)(2,1)} %param.23) | copy-start | bytes 3145732
  25.3 65.8 %copy-start.16 = (s32[16,1]{0,1:T(1,128)S(1)}, s32[16,1]{0,1:T(1,128)}, u32[]{:S(2)}) copy-start(s32[16,1]{0,1:T(1,128)} %param.26) | copy-start | bytes 196
  75.3 42.3 %copy-start.13 = (f32[16,3,128]{2,0,1:T(8,128)S(1)}, f32[16,3,128]{2,0,1:T(8,128)}, u32[]{:S(2)}) copy-start(f32[16,3,128]{2,0,1:T(8,128)} %param.27) | copy-start | bytes 73732
  75.3 43.5 %copy-start.12 = (f32[1,3,2048]{2,0,1:T(1,128)S(1)}, f32[1,3,2048]{2,0,1:T(1,128)}, u32[]{:S(2)}) copy-start(f32[1,3,2048]{2,0,1:T(1,128)} %param.28) | copy-start | bytes 73732
  76.4 21.2 %all-to-all-start.1 = ((bf16[16,64,128]{2,1,0:T(8,128)(2,1)}), bf16[16,64,128]{2,1,0:T(8,128)(2,1)}, u32[]{:S(2)}, u32[]{:S(2)}) async-start(bf16[16,64,128]{2,1,0:T(8,128)(2,1)} %bitcast.92), calls=%async_computation.1 | async-start | bytes 524288 | tf_op jit(solution)/shard_map/all_to_all | solution.py:27
  91.1 40.0 %copy-start.3 = (f32[16,128,128]{2,1,0:T(8,128)S(1)}, f32[16,128,128]{2,1,0:T(8,128)}, u32[]{:S(2)}) copy-start(f32[16,128,128]{2,1,0:T(8,128)} %inv_ref.1) | copy-start | bytes 3145732
  99.2 10.5 %all-to-all-start.2 = ((bf16[8,64,128]{2,1,0:T(8,128)(2,1)}), bf16[8,64,128]{2,1,0:T(8,128)(2,1)}, u32[]{:S(2)}, u32[]{:S(2)}) async-start(bf16[8,64,128]{2,1,0:T(8,128)(2,1)} %broadcast_in_dim.4), calls=%async_computation.2 | async-start | bytes 262144 | tf_op jit(solution)/shard_map/all_to_all | solution.py:37
  103.6 14.3 %copy-start.14 = (pred[16,16]{1,0:T(8,128)(4,1)}, pred[16,16]{1,0:T(8,128)(4,1)S(1)}, u32[]{:S(2)}) copy-start(pred[16,16]{1,0:T(8,128)(4,1)S(1)} %iota_compare_fusion.2) | copy-start | bytes 772
  111.5 12.7 %all-to-all-start.3 = ((bf16[16,64,128]{2,1,0:T(8,128)(2,1)}), bf16[16,64,128]{2,1,0:T(8,128)(2,1)}, u32[]{:S(2)}, u32[]{:S(2)}) async-start(bf16[16,64,128]{2,1,0:T(8,128)(2,1)} %broadcast_in_dim.5), calls=%async_computation.3 | async-start | bytes 524288 | tf_op jit(solution)/shard_map/all_to_all | solution.py:37
  117.6 0.6 copy-start.19
  124.2 90.6 %all-to-all-start.5 = ((bf16[16,2,3,128]{3,1,2,0:T(2,128)(2,1)}), bf16[16,2,3,128]{3,1,2,0:T(2,128)(2,1)S(1)}, u32[]{:S(2)}, u32[]{:S(2)}) async-start(bf16[16,2,3,128]{3,1,2,0:T(2,128)(2,1)} %copy.82), calls=%async_computation.5 | async-start | bytes 49152 | tf_op jit(solution)/shard_map/all_to_all | solution.py:374
  131.1 16.9 %copy-start.8 = (bf16[256,2048]{1,0:T(8,128)(2,1)S(1)}, bf16[256,2048]{1,0:T(8,128)(2,1)}, u32[]{:S(2)}) copy-start(bf16[256,2048]{1,0:T(8,128)(2,1)} %param.23) | copy-start | bytes 3145732
  131.2 17.3 %copy-start.2 = (bf16[1,16,256,256]{3,2,1,0:T(8,128)(2,1)S(1)}, bf16[1,16,256,256]{3,2,1,0:T(8,128)(2,1)}, u32[]{:S(2)}) copy-start(bf16[1,16,256,256]{3,2,1,0:T(8,128)(2,1)} %param.22) | copy-start | bytes 6291460
  148.0 62.6 %copy-start.18 = (s32[16,2]{0,1:T(2,128)S(1)}, s32[16,2]{0,1:T(2,128)}, u32[]{:S(2)}) copy-start(s32[16,2]{0,1:T(2,128)} %param.20) | copy-start | bytes 388
  148.5 62.7 %copy-start.6 = (f32[16,64,128]{2,1,0:T(8,128)S(1)}, f32[16,64,128]{2,1,0:T(8,128)}, u32[]{:S(2)}) copy-start(f32[16,64,128]{2,1,0:T(8,128)} %copy-done.5) | copy-start | bytes 1572868
  211.2 1.2 copy-start.9
  212.4 1.1 copy-start.15
  212.4 1.1 copy-start.20
  214.8 14.7 %all-to-all-start.4 = ((bf16[16,2,64,128]{3,2,1,0:T(8,128)(2,1)}), bf16[16,2,64,128]{3,2,1,0:T(8,128)(2,1)S(1)}, u32[]{:S(2)}, u32[]{:S(2)}) async-start(bf16[16,2,64,128]{3,2,1,0:T(8,128)(2,1)} %copy.81), calls=%async_computation.4 | async-start | bytes 1048576 | tf_op jit(solution)/shard_map/all_to_all | solution.py:373
  229.5 0.8 copy-start.10

commit v4 on v3

--- a/solution.py
+++ b/solution.py
@@ -227,24 +227,24 @@
     )(top_start, top_inverse, top_lower)
 
 
-def evaluate_kernel(slots, pattern_ref, coef_ref, centre_ref, column_ref, out_ref, acc):
+def evaluate_kernel(slots, pattern_ref, coef_ref, centre_ref, column_ref, out_ref, acc, spread):
     m = pl.program_id(0)
     acc[...] = jnp.zeros_like(acc)
     column = column_ref[0]
+    width = centre_ref.shape[2]
+    for comp in range(3):
+        spread[comp] = jnp.broadcast_to(column[:, comp : comp + 1], (column.shape[0], width))
 
     def one_slot(s, carry):
-        flag = pattern_ref[m, s]
-
-        @pl.when(flag != 0)
+        @pl.when(pattern_ref[m, s] != 0)
         def _():
             centre = centre_ref[s]
-            dist = jnp.zeros((column.shape[0], centre.shape[1]), jnp.float32)
+            dist = None
             for comp in range(3):
-                delta = centre[comp : comp + 1, :] - column[:, comp : comp + 1]
-                dist = dist + delta * delta
-            weight = jnp.maximum(1.0 - dist / support_sq, 0.0)
-            weight = weight * weight * weight
-            kernel = (weight * flag.astype(jnp.float32)).astype(jnp.bfloat16)
+                delta = centre[comp : comp + 1, :] - spread[comp]
+                dist = delta * delta if dist is None else dist + delta * delta
+            weight = jnp.maximum(1.0 - dist * (1.0 / support_sq), 0.0)
+            kernel = (weight * weight * weight).astype(jnp.bfloat16)
             acc[...] += _nt(coef_ref[s], kernel)
 
         return carry
@@ -266,7 +266,10 @@
             pl.BlockSpec((1, span, point_columns.shape[2]), lambda m, pat: (m, 0, 0)),
         ],
         out_specs=pl.BlockSpec((rows, span), lambda m, pat: (0, m)),
-        scratch_shapes=[pltpu.VMEM((rows, span), jnp.float32)],
+        scratch_shapes=[
+            pltpu.VMEM((rows, span), jnp.float32),
+            pltpu.VMEM((3, span, centre_all.shape[2]), jnp.float32),
+        ],
     )
     return pl.pallas_call(
         functools.partial(evaluate_kernel, slots),

time: 311 us -> 281 us (0.904)
  Pallas kernels: 208 us -> 178 us
    pallas_call x1, Pallas kernels: 79.5 us -> 49 us  [evaluate_all(): pl.pallas_call(functools.partial(evaluate_kernel, slots), out_shape=jax.S...]
  transfers between devices with their start and end apart: 5 -> 5, of which waited for: 4 -> 4; matrix products, arithmetic and copies ran while one was open for 3% -> 3% of each run, Pallas kernels for 25% -> 28%
where the time goes in v4:
time: 281 us; the launch traced here: 280 us
  Pallas kernels  178 us (63%)
  starting transfers between devices  37.6 us (13%)
  waiting for transfers between devices  23 us (8%)
  blocking collectives  17.7 us (6%)
  matrix products  9.92 us (4%)
  local copies, waits for them, and re-layouts  9.33 us (3%)
  other arithmetic  3.47 us (1%)
    pallas_call x1, Pallas kernels, sep_solve(): pl.pallas_call(functools.partial(sep_backward_kernel, n), out_shape=(sol_...  62.2 us
    pallas_call x1, Pallas kernels, sep_solve(): pl.pallas_call(functools.partial(sep_forward_kernel, n), out_shape=sol_sh...  50 us
    pallas_call x1, Pallas kernels, evaluate_all(): pl.pallas_call(functools.partial(evaluate_kernel, slots), out_shape=jax.S...  49 us
    all_to_all x1, blocking collectives, sum_at_owner(): lax.all_to_all(pieces, axis, split_axis=0, concat_axis=0, tiled=True)  17.7 us
    pallas_call x1, Pallas kernels, top_solve(): pl.pallas_call(functools.partial(top_solve_kernel, nt, span), out_shape=(...  16.9 us
    all_to_all x1, starting transfers between devices, sum_at_owner(): lax.all_to_all(pieces, axis, split_axis=0, concat_axis=0, tiled=True)  14.6 us
    all_to_all x2, starting transfers between devices, copy_for_each(): return lax.all_to_all(copies, axis, split_axis=0, concat_axis=0, tiled=True)  10.5 us
    all_to_all x2, waiting for transfers between devices, copy_for_each(): return lax.all_to_all(copies, axis, split_axis=0, concat_axis=0, tiled=True)  9.97 us
  transfers between devices with their start and end apart: 5, of which 4 were waited for; matrix products, arithmetic and copies ran while one was open for 3% of the time, Pallas kernels for 28%

profile of v4, /device:TPU:24, one launch (start us, length us, event | category | flops | bytes accessed | tf_op | source)
XLA Modules:
  0.0 280.0 jit_solution(2788705311633353670)
XLA Ops:
  0.6 3.7 %fusion.14 = f32[16,64,128]{2,1,0:T(8,128)S(1)} fusion(f32[16,128,128]{2,1,0:T(8,128)} %param.18, f32[64,2048]{1,0:T(8,128)} %param.15), kind=kOutput, calls=%fused_computation.19 | convolution fusion | flops 201326592 | bytes 2097152 | tf_op jit(solution)/shard_map/nrs,nts->nrt/dot_general | solution.py:321
  4.3 0.9 convolution_bitcast_fusion
  5.2 2.0 fusion.8
  7.5 17.7 %all_to_all.30 = bf16[16,1,64,256]{3,2,1,0:T(8,128)(2,1)S(1)} all-to-all(bf16[16,1,64,256]{3,2,1,0:T(8,128)(2,1)S(1)} %copy.74), channel_id=1, replica_groups=mesh['leaf'=8,'grp'=16] {'grp'}, dimensions={0} | all-to-all | bytes 1048576 | tf_op jit(solution)/shard_map/all_to_all | solution.py:27
  25.3 50.0 %shard_map.174 = f32[64,256]{1,0:T(8,128)S(1)} custom-call(f32[64,256]{1,0:T(8,128)S(1)} %sub.23.start_ref, f32[256,256]{1,0:T(8,128)S(1)} %bitcast.96, bf16[16,256,256]{2,1,0:T(8,128)(2,1)S(1)} %bitcast.94), custom_call_target="tpu_custom_call" | custom-call | tf_op jit(solution)/shard_map/pallas_call | solution.py:173
  75.6 0.8 copy.125
  76.4 14.6 %all-to-all-start.1 = ((bf16[16,64,128]{2,1,0:T(8,128)(2,1)}), bf16[16,64,128]{2,1,0:T(8,128)(2,1)}, u32[]{:S(2)}, u32[]{:S(2)}) async-start(bf16[16,64,128]{2,1,0:T(8,128)(2,1)} %bitcast.92), calls=%async_computation.1 | async-start | bytes 524288 | tf_op jit(solution)/shard_map/all_to_all | solution.py:27
  91.1 6.4 %all-to-all-done.1 = bf16[16,64,128]{2,1,0:T(8,128)(2,1)} async-done(((bf16[16,64,128]{2,1,0:T(8,128)(2,1)}), bf16[16,64,128]{2,1,0:T(8,128)(2,1)}, u32[]{:S(2)}, u32[]{:S(2)}) %all-to-all-start.1) | async-done | bytes 262176 | tf_op jit(solution)/shard_map/all_to_all | solution.py:27
  97.6 1.0 reduce_sum.43
  98.6 0.7 broadcast_in_dim.4
  99.2 4.3 %all-to-all-start.2 = ((bf16[8,64,128]{2,1,0:T(8,128)(2,1)}), bf16[8,64,128]{2,1,0:T(8,128)(2,1)}, u32[]{:S(2)}, u32[]{:S(2)}) async-start(bf16[8,64,128]{2,1,0:T(8,128)(2,1)} %broadcast_in_dim.4), calls=%async_computation.2 | async-start | bytes 262144 | tf_op jit(solution)/shard_map/all_to_all | solution.py:37
  103.8 6.0 %all-to-all-done.2 = bf16[8,64,128]{2,1,0:T(8,128)(2,1)} async-done(((bf16[8,64,128]{2,1,0:T(8,128)(2,1)}), bf16[8,64,128]{2,1,0:T(8,128)(2,1)}, u32[]{:S(2)}, u32[]{:S(2)}) %all-to-all-start.2) | async-done | bytes 131104 | tf_op jit(solution)/shard_map/all_to_all | solution.py:37
  109.8 0.9 reduce_sum.44
  110.7 0.8 broadcast_in_dim.5
  111.5 6.2 %all-to-all-start.3 = ((bf16[16,64,128]{2,1,0:T(8,128)(2,1)}), bf16[16,64,128]{2,1,0:T(8,128)(2,1)}, u32[]{:S(2)}, u32[]{:S(2)}) async-start(bf16[16,64,128]{2,1,0:T(8,128)(2,1)} %broadcast_in_dim.5), calls=%async_computation.3 | async-start | bytes 524288 | tf_op jit(solution)/shard_map/all_to_all | solution.py:37
  118.2 0.6 copy.82
  118.9 1.4 copy.85
  120.2 4.0 %all-to-all-done.3 = bf16[16,64,128]{2,1,0:T(8,128)(2,1)} async-done(((bf16[16,64,128]{2,1,0:T(8,128)(2,1)}), bf16[16,64,128]{2,1,0:T(8,128)(2,1)}, u32[]{:S(2)}, u32[]{:S(2)}) %all-to-all-start.3) | async-done | bytes 262176 | tf_op jit(solution)/shard_map/all_to_all | solution.py:37
  124.2 5.8 %all-to-all-start.5 = ((bf16[16,2,3,128]{3,1,2,0:T(2,128)(2,1)}), bf16[16,2,3,128]{3,1,2,0:T(2,128)(2,1)S(1)}, u32[]{:S(2)}, u32[]{:S(2)}) async-start(bf16[16,2,3,128]{3,1,2,0:T(2,128)(2,1)} %copy.82), calls=%async_computation.5 | async-start | bytes 49152 | tf_op jit(solution)/shard_map/all_to_all | solution.py:377
  130.0 1.2 bitcast_subtract_fusion.start_ref
  131.2 16.9 %shard_map.175 = (f32[64,2048]{1,0:T(8,128)}, bf16[64,2048]{1,0:T(8,128)(2,1)S(1)}) custom-call(f32[64,2048]{1,0:T(8,128)S(1)} %bitcast_subtract_fusion.start_ref, f32[16,128,128]{2,1,0:T(8,128)S(1)} %copy-done.3, bf16[2048,2048]{1,0:T(8,128)(2,1)} %lower_ref.1), custom_call_target="tpu_custom_call" | custom-call | tf_op jit(solution)/shard_map/pallas_call | solution.py:214
  148.5 62.2 %shard_map.176 = (f32[64,256]{1,0:T(8,128)S(1)}, bf16[16,64,256]{2,1,0:T(8,128)(2,1)S(1)}) custom-call(f32[64,256]{1,0:T(8,128)S(1)} %convolution_subtract_fusion.start_ref, f32[256,256]{1,0:T(8,128)S(1)} %bitcast.97, bf16[16,256,256]{2,1,0:T(8,128)(2,1)S(1)} %bitcast.95), custom_call_target="tpu_custom_call" | custom-call | tf_op jit(solution)/shard_map/pallas_call | solution.py:181
  211.2 0.6 fusion.11
  212.4 1.1 fusion.39
  213.8 0.9 copy.81
  214.8 6.7 %all-to-all-start.4 = ((bf16[16,2,64,128]{3,2,1,0:T(8,128)(2,1)}), bf16[16,2,64,128]{3,2,1,0:T(8,128)(2,1)S(1)}, u32[]{:S(2)}, u32[]{:S(2)}) async-start(bf16[16,2,64,128]{3,2,1,0:T(8,128)(2,1)} %copy.81), calls=%async_computation.4 | async-start | bytes 1048576 | tf_op jit(solution)/shard_map/all_to_all | solution.py:376
  221.5 0.7 copy.84
  222.1 0.8 copy_bitcast_fusion
  222.9 6.6 %all-to-all-done.4 = bf16[16,2,64,128]{3,2,1,0:T(8,128)(2,1)S(1)} async-done(((bf16[16,2,64,128]{3,2,1,0:T(8,128)(2,1)}), bf16[16,2,64,128]{3,2,1,0:T(8,128)(2,1)S(1)}, u32[]{:S(2)}, u32[]{:S(2)}) %all-to-all-start.4) | async-done | bytes 524320 | tf_op jit(solution)/shard_map/all_to_all | solution.py:376
  229.5 0.8 copy-done.10
  230.3 49.0 %shard_map.177 = f32[64,2048]{1,0:T(8,128)} custom-call(s32[16,32]{1,0:T(8,128)} %pattern_ref.1, bf16[32,64,128]{2,1,0:T(8,128)(2,1)} %bitcast.99, f32[32,3,128]{2,1,0:T(4,128)} %bitcast.100, f32[16,128,3]{2,1,0:T(8,128)} %bitcast.98), custom_call_target="tpu_custom_call" | custom-call | tf_op jit(solution)/shard_map/pallas_call | solution.py:274
  279.4 0.6 copy.128
  (57 shorter events, 3.4 us)
Async XLA Ops:
  0.6 3.7 %copy-start = (bf16[16,2,256,128]{3,2,1,0:T(8,128)(2,1)S(1)}, bf16[16,2,256,128]{3,2,1,0:T(8,128)(2,1)}, u32[]{:S(2)}) copy-start(bf16[16,2,256,128]{3,2,1,0:T(8,128)(2,1)} %param.19) | copy-start | bytes 6291460
  4.3 0.9 copy-start.5
  4.3 0.9 copy-start.17
  5.2 20.0 %copy-start.11 = (f32[64,256]{1,0:T(8,128)S(1)}, f32[64,256]{1,0:T(8,128)}, u32[]{:S(2)}) copy-start(f32[64,256]{1,0:T(8,128)} %param.16) | copy-start | bytes 196612
  7.3 18.0 %copy-start.1 = (bf16[1,16,256,256]{3,2,1,0:T(8,128)(2,1)S(1)}, bf16[1,16,256,256]{3,2,1,0:T(8,128)(2,1)}, u32[]{:S(2)}) copy-start(bf16[1,16,256,256]{3,2,1,0:T(8,128)(2,1)} %param.22) | copy-start | bytes 6291460
  7.3 18.0 %copy-start.4 = (f32[1,256,256]{2,1,0:T(8,128)S(1)}, f32[1,256,256]{2,1,0:T(8,128)}, u32[]{:S(2)}) copy-start(f32[1,256,256]{2,1,0:T(8,128)} %param.21) | copy-start | bytes 786436
  7.5 67.8 %copy-start.7 = (bf16[256,2048]{1,0:T(8,128)(2,1)S(1)}, bf16[256,2048]{1,0:T(8,128)(2,1)}, u32[]{:S(2)}) copy-start(bf16[256,2048]{1,0:T(8,128)(2,1)} %param.23) | copy-start | bytes 3145732
  25.3 65.8 %copy-start.16 = (s32[16,1]{0,1:T(1,128)S(1)}, s32[16,1]{0,1:T(1,128)}, u32[]{:S(2)}) copy-start(s32[16,1]{0,1:T(1,128)} %param.26) | copy-start | bytes 196
  75.3 42.3 %copy-start.13 = (f32[16,3,128]{2,0,1:T(8,128)S(1)}, f32[16,3,128]{2,0,1:T(8,128)}, u32[]{:S(2)}) copy-start(f32[16,3,128]{2,0,1:T(8,128)} %param.27) | copy-start | bytes 73732
  75.3 43.5 %copy-start.12 = (f32[1,3,2048]{2,0,1:T(1,128)S(1)}, f32[1,3,2048]{2,0,1:T(1,128)}, u32[]{:S(2)}) copy-start(f32[1,3,2048]{2,0,1:T(1,128)} %param.28) | copy-start | bytes 73732
  76.4 21.2 %all-to-all-start.1 = ((bf16[16,64,128]{2,1,0:T(8,128)(2,1)}), bf16[16,64,128]{2,1,0:T(8,128)(2,1)}, u32[]{:S(2)}, u32[]{:S(2)}) async-start(bf16[16,64,128]{2,1,0:T(8,128)(2,1)} %bitcast.92), calls=%async_computation.1 | async-start | bytes 524288 | tf_op jit(solution)/shard_map/all_to_all | solution.py:27
  91.1 40.0 %copy-start.3 = (f32[16,128,128]{2,1,0:T(8,128)S(1)}, f32[16,128,128]{2,1,0:T(8,128)}, u32[]{:S(2)}) copy-start(f32[16,128,128]{2,1,0:T(8,128)} %inv_ref.1) | copy-start | bytes 3145732
  99.2 10.5 %all-to-all-start.2 = ((bf16[8,64,128]{2,1,0:T(8,128)(2,1)}), bf16[8,64,128]{2,1,0:T(8,128)(2,1)}, u32[]{:S(2)}, u32[]{:S(2)}) async-start(bf16[8,64,128]{2,1,0:T(8,128)(2,1)} %broadcast_in_dim.4), calls=%async_computation.2 | async-start | bytes 262144 | tf_op jit(solution)/shard_map/all_to_all | solution.py:37
  103.6 14.3 %copy-start.14 = (pred[16,16]{1,0:T(8,128)(4,1)}, pred[16,16]{1,0:T(8,128)(4,1)S(1)}, u32[]{:S(2)}) copy-start(pred[16,16]{1,0:T(8,128)(4,1)S(1)} %iota_compare_fusion.2) | copy-start | bytes 772
  111.5 12.7 %all-to-all-start.3 = ((bf16[16,64,128]{2,1,0:T(8,128)(2,1)}), bf16[16,64,128]{2,1,0:T(8,128)(2,1)}, u32[]{:S(2)}, u32[]{:S(2)}) async-start(bf16[16,64,128]{2,1,0:T(8,128)(2,1)} %broadcast_in_dim.5), calls=%async_computation.3 | async-start | bytes 524288 | tf_op jit(solution)/shard_map/all_to_all | solution.py:37
  117.6 0.6 copy-start.19
  124.2 90.6 %all-to-all-start.5 = ((bf16[16,2,3,128]{3,1,2,0:T(2,128)(2,1)}), bf16[16,2,3,128]{3,1,2,0:T(2,128)(2,1)S(1)}, u32[]{:S(2)}, u32[]{:S(2)}) async-start(bf16[16,2,3,128]{3,1,2,0:T(2,128)(2,1)} %copy.82), calls=%async_computation.5 | async-start | bytes 49152 | tf_op jit(solution)/shard_map/all_to_all | solution.py:377
  131.1 16.9 %copy-start.8 = (bf16[256,2048]{1,0:T(8,128)(2,1)S(1)}, bf16[256,2048]{1,0:T(8,128)(2,1)}, u32[]{:S(2)}) copy-start(bf16[256,2048]{1,0:T(8,128)(2,1)} %param.23) | copy-start | bytes 3145732
  131.2 17.3 %copy-start.2 = (bf16[1,16,256,256]{3,2,1,0:T(8,128)(2,1)S(1)}, bf16[1,16,256,256]{3,2,1,0:T(8,128)(2,1)}, u32[]{:S(2)}) copy-start(bf16[1,16,256,256]{3,2,1,0:T(8,128)(2,1)} %param.22) | copy-start | bytes 6291460
  148.0 62.6 %copy-start.18 = (s32[16,2]{0,1:T(2,128)S(1)}, s32[16,2]{0,1:T(2,128)}, u32[]{:S(2)}) copy-start(s32[16,2]{0,1:T(2,128)} %param.20) | copy-start | bytes 388
  148.5 62.7 %copy-start.6 = (f32[16,64,128]{2,1,0:T(8,128)S(1)}, f32[16,64,128]{2,1,0:T(8,128)}, u32[]{:S(2)}) copy-start(f32[16,64,128]{2,1,0:T(8,128)} %copy-done.5) | copy-start | bytes 1572868
  211.2 1.2 copy-start.9
  212.4 1.1 copy-start.15
  212.4 1.1 copy-start.20
  214.8 14.7 %all-to-all-start.4 = ((bf16[16,2,64,128]{3,2,1,0:T(8,128)(2,1)}), bf16[16,2,64,128]{3,2,1,0:T(8,128)(2,1)S(1)}, u32[]{:S(2)}, u32[]{:S(2)}) async-start(bf16[16,2,64,128]{3,2,1,0:T(8,128)(2,1)} %copy.81), calls=%async_computation.4 | async-start | bytes 1048576 | tf_op jit(solution)/shard_map/all_to_all | solution.py:376
  229.5 0.8 copy-start.10

commit v5 on v4

--- a/solution.py
+++ b/solution.py
@@ -337,9 +337,7 @@
     sep_sol = sep_solve("forward", sep_start, inverse_own, own_blocks, grp_size)
     sep_half = sep_sol.astype(jnp.bfloat16)
     top_term = jnp.dot(sep_half, top_coupling, preferred_element_type=jnp.float32)
-    top_part = sum_at_owner(top_term.astype(jnp.bfloat16), "grp", 1)
-    top_part = over_copies(top_part.astype(jnp.bfloat16), "leaf").astype(jnp.float32)
-    top_total = gather_directly(top_part.astype(jnp.bfloat16), "grp", 1).astype(top_part.dtype)
+    top_total = lax.psum(top_term, ("leaf", "grp"))
     top_start = rhs_top - top_total
     coef_top, top_half = top_solve(top_start, top_inverse, top_lower)
     back_start = sep_sol - lax.dot_general(

time: 281 us -> 398 us (1.42)
  waiting for transfers between devices: 23 us -> 151 us
  blocking collectives: 17.7 us -> 0 us
  between operations: 1 us -> 14.4 us
  starting transfers between devices: 37.6 us -> 28.6 us
    psum x0 -> x1, waiting for transfers between devices: none -> 136 us  [on_device(): top_total = lax.psum(top_term, ('leaf', 'grp'))]
    all_to_all x1 -> x0, blocking collectives: 17.7 us -> none  [sum_at_owner(): lax.all_to_all(pieces, axis, split_axis=0, concat_axis=0, tiled=True)]
    all_to_all x2 -> x0, starting transfers between devices: 10.5 us -> none  [copy_for_each(): return lax.all_to_all(copies, axis, split_axis=0, concat_axis=0, tiled=True)]
    all_to_all x2 -> x0, waiting for transfers between devices: 9.97 us -> none  [copy_for_each(): return lax.all_to_all(copies, axis, split_axis=0, concat_axis=0, tiled=True)]
    all_to_all x1, starting transfers between devices: 5.78 us -> 14.3 us  [on_device(): lax.all_to_all(send_centre.astype(jnp.bfloat16), 'grp', split_axis=0, con...]
    all_to_all x1, starting transfers between devices: 14.6 us -> 8.32 us  [sum_at_owner(): lax.all_to_all(pieces, axis, split_axis=0, concat_axis=0, tiled=True)]
  transfers between devices with their start and end apart: 5 -> 4, of which waited for: 4 -> 3; matrix products, arithmetic and copies ran while one was open for 3% -> 3% of each run, Pallas kernels for 28% -> 20%
where the time goes in v5:
time: 398 us; the launch traced here: 395 us
  Pallas kernels  178 us (45%)
  waiting for transfers between devices  151 us (38%)
  starting transfers between devices  28.6 us (7%)
  between operations  14.4 us (4%)
  matrix products  10.7 us (3%)
  local copies, waits for them, and re-layouts  9.09 us (2%)
    psum x1, waiting for transfers between devices, on_device(): top_total = lax.psum(top_term, ('leaf', 'grp'))  136 us
    pallas_call x1, Pallas kernels, sep_solve(): pl.pallas_call(functools.partial(sep_backward_kernel, n), out_shape=(sol_...  63.6 us
    pallas_call x1, Pallas kernels, sep_solve(): pl.pallas_call(functools.partial(sep_forward_kernel, n), out_shape=sol_sh...  50 us
    pallas_call x1, Pallas kernels, evaluate_all(): pl.pallas_call(functools.partial(evaluate_kernel, slots), out_shape=jax.S...  47.7 us
    pallas_call x1, Pallas kernels, top_solve(): pl.pallas_call(functools.partial(top_solve_kernel, nt, span), out_shape=(...  16.9 us
    all_to_all x1, starting transfers between devices, on_device(): lax.all_to_all(send_centre.astype(jnp.bfloat16), 'grp', split_axis=0, con...  14.3 us
    all_to_all x1, starting transfers between devices, sum_at_owner(): lax.all_to_all(pieces, axis, split_axis=0, concat_axis=0, tiled=True)  8.32 us
    all_to_all x1, waiting for transfers between devices, sum_at_owner(): lax.all_to_all(pieces, axis, split_axis=0, concat_axis=0, tiled=True)  8.11 us
  transfers between devices with their start and end apart: 4, of which 3 were waited for; matrix products, arithmetic and copies ran while one was open for 3% of the time, Pallas kernels for 20%

profile of v5, /device:TPU:24, one launch (start us, length us, event | category | flops | bytes accessed | tf_op | source)
XLA Modules:
  0.0 395.4 jit_solution(13600148219684852939)
XLA Ops:
  7.2 3.7 fusion.13
  10.9 0.9 convolution_bitcast_fusion
  11.8 2.0 fusion.8
  13.8 1.0 copy.56
  14.8 8.3 %all-to-all-start = ((bf16[16,1,64,256]{3,2,1,0:T(8,128)(2,1)}), bf16[16,1,64,256]{3,2,1,0:T(8,128)(2,1)}, u32[]{:S(2)}, u32[]{:S(2)}) async-start(bf16[16,1,64,256]{3,2,1,0:T(8,128)(2,1)} %copy.56), calls=%async_computation | async-start | bytes 1048576 | tf_op jit(solution)/shard_map/all_to_all | solution.py:27
  23.3 0.7 select_reduce_fusion
  24.0 0.6 iota_compare_fusion.2
  24.6 8.1 %all-to-all-done = bf16[16,1,64,256]{3,2,1,0:T(8,128)(2,1)} async-done(((bf16[16,1,64,256]{3,2,1,0:T(8,128)(2,1)}), bf16[16,1,64,256]{3,2,1,0:T(8,128)(2,1)}, u32[]{:S(2)}, u32[]{:S(2)}) %all-to-all-start) | async-done | bytes 524320 | tf_op jit(solution)/shard_map/all_to_all | solution.py:27
  32.7 1.1 convert_reduce_fusion
  33.8 1.6 copy-done.1
  35.4 50.0 %shard_map.174 = f32[64,256]{1,0:T(8,128)S(1)} custom-call(f32[64,256]{1,0:T(8,128)S(1)} %sub.23.start_ref, f32[256,256]{1,0:T(8,128)S(1)} %bitcast.82, bf16[16,256,256]{2,1,0:T(8,128)(2,1)S(1)} %bitcast.80), custom_call_target="tpu_custom_call" | custom-call | tf_op jit(solution)/shard_map/pallas_call | solution.py:173
  85.4 1.1 fusion.21
  86.8 0.6 copy.62
  87.4 14.3 %all-to-all-start.2 = ((bf16[16,2,3,128]{3,1,2,0:T(2,128)(2,1)}), bf16[16,2,3,128]{3,1,2,0:T(2,128)(2,1)S(1)}, u32[]{:S(2)}, u32[]{:S(2)}) async-start(bf16[16,2,3,128]{3,1,2,0:T(2,128)(2,1)} %copy.62), calls=%async_computation.2 | async-start | bytes 49152 | tf_op jit(solution)/shard_map/all_to_all | solution.py:375
  101.7 1.4 copy.65
  103.0 135.9 %all-reduce.2.cloned.1.call-done = f32[64,2048]{1,0:T(8,128)} async-done(((f32[64,2048]{1,0:T(8,128)}), f32[64,2048]{1,0:T(8,128)}) %all-reduce.2.cloned.1.call-update) | async-done | bytes 524304 | tf_op jit(solution)/shard_map/psum | solution.py:340
  239.0 1.3 sub.24.start_ref
  240.3 16.9 %shard_map.175 = (f32[64,2048]{1,0:T(8,128)}, bf16[64,2048]{1,0:T(8,128)(2,1)S(1)}) custom-call(f32[64,2048]{1,0:T(8,128)S(1)} %sub.24.start_ref, f32[16,128,128]{2,1,0:T(8,128)S(1)} %copy-done.3, bf16[2048,2048]{1,0:T(8,128)(2,1)} %lower_ref.1), custom_call_target="tpu_custom_call" | custom-call | tf_op jit(solution)/shard_map/pallas_call | solution.py:214
  257.1 0.4 convolution_subtract_fusion.start_ref
  257.6 63.6 %shard_map.176 = (f32[64,256]{1,0:T(8,128)S(1)}, bf16[16,64,256]{2,1,0:T(8,128)(2,1)S(1)}) custom-call(f32[64,256]{1,0:T(8,128)S(1)} %convolution_subtract_fusion.start_ref, f32[256,256]{1,0:T(8,128)S(1)} %bitcast.83, bf16[16,256,256]{2,1,0:T(8,128)(2,1)S(1)} %bitcast.81), custom_call_target="tpu_custom_call" | custom-call | tf_op jit(solution)/shard_map/pallas_call | solution.py:181
  321.2 0.5 convolution_convert_fusion
  321.8 0.6 fusion.11
  322.4 0.6 copy-done.9
  323.0 1.1 fusion.39
  324.4 0.9 copy.61
  325.3 6.0 %all-to-all-start.1 = ((bf16[16,2,64,128]{3,2,1,0:T(8,128)(2,1)}), bf16[16,2,64,128]{3,2,1,0:T(8,128)(2,1)S(1)}, u32[]{:S(2)}, u32[]{:S(2)}) async-start(bf16[16,2,64,128]{3,2,1,0:T(8,128)(2,1)} %copy.61), calls=%async_computation.1 | async-start | bytes 1048576 | tf_op jit(solution)/shard_map/all_to_all | solution.py:374
  331.3 0.7 copy.64
  332.0 0.8 copy_bitcast_fusion
  332.8 6.6 %all-to-all-done.1 = bf16[16,2,64,128]{3,2,1,0:T(8,128)(2,1)S(1)} async-done(((bf16[16,2,64,128]{3,2,1,0:T(8,128)(2,1)}), bf16[16,2,64,128]{3,2,1,0:T(8,128)(2,1)S(1)}, u32[]{:S(2)}, u32[]{:S(2)}) %all-to-all-start.1) | async-done | bytes 524320 | tf_op jit(solution)/shard_map/all_to_all | solution.py:374
  339.4 0.8 copy-done.10
  340.2 47.7 %shard_map.177 = f32[64,2048]{1,0:T(8,128)} custom-call(s32[16,32]{1,0:T(8,128)} %pattern_ref.1, bf16[32,64,128]{2,1,0:T(8,128)(2,1)} %bitcast.85, f32[32,3,128]{2,1,0:T(4,128)} %bitcast.86, f32[16,128,3]{2,1,0:T(8,128)} %bitcast.84), custom_call_target="tpu_custom_call" | custom-call | tf_op jit(solution)/shard_map/pallas_call | solution.py:274
  387.9 0.6 copy.104
  (52 shorter events, 0.7 us)
Async XLA Ops:
  7.2 3.7 copy-start
  10.9 0.9 copy-start.5
  10.9 0.9 copy-start.17
  11.8 11.4 %copy-start.16 = (s32[16,1]{0,1:T(1,128)S(1)}, s32[16,1]{0,1:T(1,128)}, u32[]{:S(2)}) copy-start(s32[16,1]{0,1:T(1,128)} %param.26) | copy-start | bytes 196
  11.8 22.0 %copy-start.11 = (f32[64,256]{1,0:T(8,128)S(1)}, f32[64,256]{1,0:T(8,128)}, u32[]{:S(2)}) copy-start(f32[64,256]{1,0:T(8,128)} %param.16) | copy-start | bytes 196612
  13.8 20.0 %copy-start.4 = (f32[1,256,256]{2,1,0:T(8,128)S(1)}, f32[1,256,256]{2,1,0:T(8,128)}, u32[]{:S(2)}) copy-start(f32[1,256,256]{2,1,0:T(8,128)} %param.21) | copy-start | bytes 786436
  14.8 70.6 %copy-start.7 = (bf16[256,2048]{1,0:T(8,128)(2,1)S(1)}, bf16[256,2048]{1,0:T(8,128)(2,1)}, u32[]{:S(2)}) copy-start(bf16[256,2048]{1,0:T(8,128)(2,1)} %param.23) | copy-start | bytes 3145732
  14.8 17.9 %all-to-all-start = ((bf16[16,1,64,256]{3,2,1,0:T(8,128)(2,1)}), bf16[16,1,64,256]{3,2,1,0:T(8,128)(2,1)}, u32[]{:S(2)}, u32[]{:S(2)}) async-start(bf16[16,1,64,256]{3,2,1,0:T(8,128)(2,1)} %copy.56), calls=%async_computation | async-start | bytes 1048576 | tf_op jit(solution)/shard_map/all_to_all | solution.py:27
  23.1 215.9 %all-reduce.2.cloned.1.call-start = ((), (), s32[]{:S(2)}) async-start(), calls=%async_computation.3 | async-start | bytes 1048576 | tf_op jit(solution)/shard_map/psum | solution.py:340
  33.8 1.6 copy-start.1
  35.4 51.1 %copy-start.21 = (s32[16]{0:T(128)S(1)}, s32[16]{0:T(128)}, u32[]{:S(2)}) copy-start(s32[16]{0:T(128)} %select_reduce_fusion) | copy-start | bytes 196
  35.4 51.1 %copy-start.13 = (f32[16,3,128]{2,0,1:T(8,128)S(1)}, f32[16,3,128]{2,0,1:T(8,128)}, u32[]{:S(2)}) copy-start(f32[16,3,128]{2,0,1:T(8,128)} %param.27) | copy-start | bytes 73732
  35.4 51.2 %copy-start.14 = (pred[16,16]{1,0:T(8,128)(4,1)S(1)}, pred[16,16]{1,0:T(8,128)(4,1)}, u32[]{:S(2)}) copy-start(pred[16,16]{1,0:T(8,128)(4,1)} %iota_compare_fusion.2) | copy-start | bytes 772
  35.4 66.2 %copy-start.12 = (f32[1,3,2048]{2,0,1:T(1,128)S(1)}, f32[1,3,2048]{2,0,1:T(1,128)}, u32[]{:S(2)}) copy-start(f32[1,3,2048]{2,0,1:T(1,128)} %param.28) | copy-start | bytes 73732
  86.5 153.7 %copy-start.3 = (f32[16,128,128]{2,1,0:T(8,128)S(1)}, f32[16,128,128]{2,1,0:T(8,128)}, u32[]{:S(2)}) copy-start(f32[16,128,128]{2,1,0:T(8,128)} %inv_ref.1) | copy-start | bytes 3145732
  86.6 0.8 copy-start.19
  87.4 237.9 %all-to-all-start.2 = ((bf16[16,2,3,128]{3,1,2,0:T(2,128)(2,1)}), bf16[16,2,3,128]{3,1,2,0:T(2,128)(2,1)S(1)}, u32[]{:S(2)}, u32[]{:S(2)}) async-start(bf16[16,2,3,128]{3,1,2,0:T(2,128)(2,1)} %copy.62), calls=%async_computation.2 | async-start | bytes 49152 | tf_op jit(solution)/shard_map/all_to_all | solution.py:375
  240.2 16.9 %copy-start.8 = (bf16[256,2048]{1,0:T(8,128)(2,1)S(1)}, bf16[256,2048]{1,0:T(8,128)(2,1)}, u32[]{:S(2)}) copy-start(bf16[256,2048]{1,0:T(8,128)(2,1)} %param.23) | copy-start | bytes 3145732
  240.2 17.3 %copy-start.2 = (bf16[1,16,256,256]{3,2,1,0:T(8,128)(2,1)S(1)}, bf16[1,16,256,256]{3,2,1,0:T(8,128)(2,1)}, u32[]{:S(2)}) copy-start(bf16[1,16,256,256]{3,2,1,0:T(8,128)(2,1)} %param.22) | copy-start | bytes 6291460
  257.1 64.1 %copy-start.18 = (s32[16,2]{0,1:T(2,128)S(1)}, s32[16,2]{0,1:T(2,128)}, u32[]{:S(2)}) copy-start(s32[16,2]{0,1:T(2,128)} %param.20) | copy-start | bytes 388
  257.6 64.2 %copy-start.6 = (f32[16,64,128]{2,1,0:T(8,128)S(1)}, f32[16,64,128]{2,1,0:T(8,128)}, u32[]{:S(2)}) copy-start(f32[16,64,128]{2,1,0:T(8,128)} %copy-done.5) | copy-start | bytes 1572868
  321.8 1.2 copy-start.9
  323.0 1.1 copy-start.15
  323.0 1.1 copy-start.20
  325.3 14.1 %all-to-all-start.1 = ((bf16[16,2,64,128]{3,2,1,0:T(8,128)(2,1)}), bf16[16,2,64,128]{3,2,1,0:T(8,128)(2,1)S(1)}, u32[]{:S(2)}, u32[]{:S(2)}) async-start(bf16[16,2,64,128]{3,2,1,0:T(8,128)(2,1)} %copy.61), calls=%async_computation.1 | async-start | bytes 1048576 | tf_op jit(solution)/shard_map/all_to_all | solution.py:374
  339.4 0.8 copy-start.10
Sparse Core Ops, SparseCore 0:
  86.7 152.2 all-reduce.1

commit v6 on v5

--- a/solution.py
+++ b/solution.py
@@ -278,6 +278,113 @@
     )(pattern, coef_all, centre_all, point_columns)
 
 
+def top_reduce_kernel(n, groups, span, term_ref, total_ref, parts_a, parts_b, gathered, local_sem, send_a, recv_a, send_b, recv_b, send_c, recv_c):
+    me = lax.axis_index("grp")
+    leaf = lax.axis_index("leaf")
+    barrier = pltpu.get_barrier_semaphore()
+    for r in range(n):
+        @pl.when(me != r)
+        def _():
+            pl.semaphore_signal(barrier, inc=1, device_id=(leaf, r), device_id_type=MESH)
+    for g in range(groups):
+        @pl.when(leaf != g)
+        def _():
+            pl.semaphore_signal(barrier, inc=1, device_id=(g, me), device_id_type=MESH)
+    pl.semaphore_wait(barrier, n - 1 + groups - 1)
+
+    def column(q):
+        return term_ref.at[:, pl.ds(pl.multiple_of(q * span, span), span)]
+
+    def copy_a(k):
+        dest = lax.rem(me + k, n)
+        return pltpu.make_async_remote_copy(
+            column(dest), parts_a.at[me], send_a.at[k], recv_a.at[me], device_id=(leaf, dest), device_id_type=MESH
+        )
+
+    def wait_a(k):
+        src = lax.rem(me + n - k, n)
+        pltpu.make_async_remote_copy(
+            column(src), parts_a.at[src], send_a.at[0], recv_a.at[src], device_id=(leaf, src), device_id_type=MESH
+        ).wait_recv()
+
+    own = pltpu.make_async_copy(column(me), parts_a.at[me], local_sem.at[0])
+    own.start()
+    for k in range(1, n):
+        copy_a(k).start()
+    own.wait()
+    for k in range(1, n):
+        wait_a(k)
+    for k in range(1, n):
+        copy_a(k).wait_send()
+    total = parts_a[0]
+    for q in range(1, n):
+        total = total + parts_a[q]
+    parts_b[leaf] = total
+
+    def copy_b(k):
+        dest = lax.rem(leaf + k, groups)
+        return pltpu.make_async_remote_copy(
+            parts_b.at[leaf], parts_b.at[leaf], send_b.at[k], recv_b.at[leaf], device_id=(dest, me), device_id_type=MESH
+        )
+
+    for k in range(1, groups):
+        copy_b(k).start()
+    for k in range(1, groups):
+        src = lax.rem(leaf + groups - k, groups)
+        pltpu.make_async_remote_copy(
+            parts_b.at[src], parts_b.at[src], send_b.at[0], recv_b.at[src], device_id=(src, me), device_id_type=MESH
+        ).wait_recv()
+    for k in range(1, groups):
+        copy_b(k).wait_send()
+    summed = parts_b[0]
+    for g in range(1, groups):
+        summed = summed + parts_b[g]
+    gathered[me] = summed
+
+    def copy_c(k):
+        dest = lax.rem(me + k, n)
+        return pltpu.make_async_remote_copy(
+            gathered.at[me], gathered.at[me], send_c.at[k], recv_c.at[me], device_id=(leaf, dest), device_id_type=MESH
+        )
+
+    for k in range(1, n):
+        copy_c(k).start()
+    for k in range(1, n):
+        src = lax.rem(me + n - k, n)
+        pltpu.make_async_remote_copy(
+            gathered.at[src], gathered.at[src], send_c.at[0], recv_c.at[src], device_id=(leaf, src), device_id_type=MESH
+        ).wait_recv()
+    for k in range(1, n):
+        copy_c(k).wait_send()
+    for q in range(n):
+        total_ref[:, q * span : (q + 1) * span] = gathered[q]
+
+
+def top_reduce(term, n, groups):
+    rows, width = term.shape
+    span = width // n
+    vmem = pl.BlockSpec(memory_space=pltpu.VMEM)
+    return pl.pallas_call(
+        functools.partial(top_reduce_kernel, n, groups, span),
+        out_shape=jax.ShapeDtypeStruct((rows, width), jnp.float32),
+        in_specs=[vmem],
+        out_specs=vmem,
+        scratch_shapes=[
+            pltpu.VMEM((n, rows, span), jnp.float32),
+            pltpu.VMEM((groups, rows, span), jnp.float32),
+            pltpu.VMEM((n, rows, span), jnp.float32),
+            pltpu.SemaphoreType.DMA((1,)),
+            pltpu.SemaphoreType.DMA((n,)),
+            pltpu.SemaphoreType.DMA((n,)),
+            pltpu.SemaphoreType.DMA((groups,)),
+            pltpu.SemaphoreType.DMA((groups,)),
+            pltpu.SemaphoreType.DMA((n,)),
+            pltpu.SemaphoreType.DMA((n,)),
+        ],
+        compiler_params=pltpu.CompilerParams(collective_id=2, has_side_effects=True),
+    )(term)
+
+
 def slot_ranks(dest_rows, grp_size):
     onehot = (dest_rows[..., None] == jnp.arange(grp_size)).astype(jnp.int32)
     before = jnp.cumsum(onehot, axis=-2) - onehot
@@ -337,7 +444,7 @@
     sep_sol = sep_solve("forward", sep_start, inverse_own, own_blocks, grp_size)
     sep_half = sep_sol.astype(jnp.bfloat16)
     top_term = jnp.dot(sep_half, top_coupling, preferred_element_type=jnp.float32)
-    top_total = lax.psum(top_term, ("leaf", "grp"))
+    top_total = top_reduce(top_term, grp_size, lax.axis_size("leaf"))
     top_start = rhs_top - top_total
     coef_top, top_half = top_solve(top_start, top_inverse, top_lower)
     back_start = sep_sol - lax.dot_general(

time: 398 us -> 274 us (0.69)
  waiting for transfers between devices: 151 us -> 13.5 us
  Pallas kernels: 178 us -> 212 us
  between operations: 14.4 us -> 0.91 us
  starting transfers between devices: 28.6 us -> 20.2 us
    psum x1 -> x0, waiting for transfers between devices: 136 us -> none  [on_device(): top_total = lax.psum(top_term, ('leaf', 'grp'))]
    pallas_call x0 -> x1, Pallas kernels: none -> 35.6 us  [top_reduce(): pl.pallas_call(functools.partial(top_reduce_kernel, n, groups, span), out...]
    all_to_all x1, starting transfers between devices: 14.3 us -> 5.54 us  [on_device(): lax.all_to_all(send_centre.astype(jnp.bfloat16), 'grp', split_axis=0, con...]
  transfers between devices with their start and end apart: 4 -> 3, of which waited for: 3 -> 2; matrix products, arithmetic and copies ran while one was open for 3% -> 4% of each run, Pallas kernels for 20% -> 62%
where the time goes in v6:
time: 274 us; the launch traced here: 270 us
  Pallas kernels  212 us (77%)
  starting transfers between devices  20.2 us (7%)
  waiting for transfers between devices  13.5 us (5%)
  matrix products  12 us (4%)
  local copies, waits for them, and re-layouts  9.08 us (3%)
    pallas_call x1, Pallas kernels, sep_solve(): pl.pallas_call(functools.partial(sep_backward_kernel, n), out_shape=(sol_...  62.9 us
    pallas_call x1, Pallas kernels, sep_solve(): pl.pallas_call(functools.partial(sep_forward_kernel, n), out_shape=sol_sh...  51.6 us
    pallas_call x1, Pallas kernels, evaluate_all(): pl.pallas_call(functools.partial(evaluate_kernel, slots), out_shape=jax.S...  45.4 us
    pallas_call x1, Pallas kernels, top_reduce(): pl.pallas_call(functools.partial(top_reduce_kernel, n, groups, span), out...  35.6 us
    pallas_call x1, Pallas kernels, top_solve(): pl.pallas_call(functools.partial(top_solve_kernel, nt, span), out_shape=(...  16.9 us
    all_to_all x1, starting transfers between devices, sum_at_owner(): lax.all_to_all(pieces, axis, split_axis=0, concat_axis=0, tiled=True)  8.19 us
    all_to_all x1, waiting for transfers between devices, sum_at_owner(): lax.all_to_all(pieces, axis, split_axis=0, concat_axis=0, tiled=True)  6.96 us
    all_to_all x1, waiting for transfers between devices, on_device(): lax.all_to_all(send_coef, 'grp', split_axis=0, concat_axis=0, tiled=True)  6.57 us
  transfers between devices with their start and end apart: 3, of which 2 were waited for; matrix products, arithmetic and copies ran while one was open for 4% of the time, Pallas kernels for 62%

profile of v6, /device:TPU:24, one launch (start us, length us, event | category | flops | bytes accessed | tf_op | source)
XLA Modules:
  0.0 269.8 jit_solution(9794518144981947740)
XLA Ops:
  0.6 3.7 %fusion.13 = f32[16,64,128]{2,1,0:T(8,128)S(1)} fusion(f32[16,128,128]{2,1,0:T(8,128)} %param.18, f32[64,2048]{1,0:T(8,128)} %param.15), kind=kOutput, calls=%fused_computation.16 | convolution fusion | flops 201326592 | bytes 2097152 | tf_op jit(solution)/shard_map/nrs,nts->nrt/dot_general | solution.py:428
  4.3 0.9 convolution_bitcast_fusion
  5.3 2.0 fusion.8
  7.3 1.0 copy.56
  8.3 8.2 %all-to-all-start = ((bf16[16,1,64,256]{3,2,1,0:T(8,128)(2,1)}), bf16[16,1,64,256]{3,2,1,0:T(8,128)(2,1)S(1)}, u32[]{:S(2)}, u32[]{:S(2)}) async-start(bf16[16,1,64,256]{3,2,1,0:T(8,128)(2,1)} %copy.56), calls=%async_computation | async-start | bytes 1048576 | tf_op jit(solution)/shard_map/all_to_all | solution.py:27
  16.6 0.2 select_reduce_fusion
  16.8 0.1 convolution_convert_fusion.2
  16.9 0.6 copy.62
  17.6 1.4 copy.65
  19.0 7.0 %all-to-all-done = bf16[16,1,64,256]{3,2,1,0:T(8,128)(2,1)S(1)} async-done(((bf16[16,1,64,256]{3,2,1,0:T(8,128)(2,1)}), bf16[16,1,64,256]{3,2,1,0:T(8,128)(2,1)S(1)}, u32[]{:S(2)}, u32[]{:S(2)}) %all-to-all-start) | async-done | bytes 524320 | tf_op jit(solution)/shard_map/all_to_all | solution.py:27
  25.9 5.5 %all-to-all-start.2 = ((bf16[16,2,3,128]{3,1,2,0:T(2,128)(2,1)}), bf16[16,2,3,128]{3,1,2,0:T(2,128)(2,1)S(1)}, u32[]{:S(2)}, u32[]{:S(2)}) async-start(bf16[16,2,3,128]{3,1,2,0:T(2,128)(2,1)} %copy.62), calls=%async_computation.2 | async-start | bytes 49152 | tf_op jit(solution)/shard_map/all_to_all | solution.py:482
  31.6 1.6 copy-done.1
  33.2 51.6 %shard_map.174 = f32[64,256]{1,0:T(8,128)S(1)} custom-call(f32[64,256]{1,0:T(8,128)S(1)} %sub.23.start_ref, f32[256,256]{1,0:T(8,128)S(1)} %bitcast.82, bf16[16,256,256]{2,1,0:T(8,128)(2,1)S(1)} %bitcast.80), custom_call_target="tpu_custom_call" | custom-call | tf_op jit(solution)/shard_map/pallas_call | solution.py:173
  84.8 2.4 fusion.21.term_ref
  87.2 35.6 %shard_map.175 = f32[64,2048]{1,0:T(8,128)} custom-call(f32[64,2048]{1,0:T(8,128)} %fusion.21.term_ref), custom_call_target="tpu_custom_call" | custom-call | tf_op jit(solution)/shard_map/pallas_call | solution.py:367
  122.7 1.3 sub.24.start_ref
  124.0 16.9 %shard_map.176 = (f32[64,2048]{1,0:T(8,128)}, bf16[64,2048]{1,0:T(8,128)(2,1)S(1)}) custom-call(f32[64,2048]{1,0:T(8,128)S(1)} %sub.24.start_ref, f32[16,128,128]{2,1,0:T(8,128)S(1)} %copy-done.3, bf16[2048,2048]{1,0:T(8,128)(2,1)} %lower_ref.1), custom_call_target="tpu_custom_call" | custom-call | tf_op jit(solution)/shard_map/pallas_call | solution.py:214
  140.9 0.4 convolution_subtract_fusion.start_ref
  141.4 62.9 %shard_map.177 = (f32[64,256]{1,0:T(8,128)S(1)}, bf16[16,64,256]{2,1,0:T(8,128)(2,1)S(1)}) custom-call(f32[64,256]{1,0:T(8,128)S(1)} %convolution_subtract_fusion.start_ref, f32[256,256]{1,0:T(8,128)S(1)} %bitcast.83, bf16[16,256,256]{2,1,0:T(8,128)(2,1)S(1)} %bitcast.81), custom_call_target="tpu_custom_call" | custom-call | tf_op jit(solution)/shard_map/pallas_call | solution.py:181
  204.2 0.5 convolution_convert_fusion
  204.8 0.6 fusion.11
  205.4 0.6 copy-done.8
  206.0 1.1 fusion.39
  207.1 0.3 convolution_convert_fusion.1
  207.4 0.9 copy.61
  208.3 6.5 %all-to-all-start.1 = ((bf16[16,2,64,128]{3,2,1,0:T(8,128)(2,1)}), bf16[16,2,64,128]{3,2,1,0:T(8,128)(2,1)S(1)}, u32[]{:S(2)}, u32[]{:S(2)}) async-start(bf16[16,2,64,128]{3,2,1,0:T(8,128)(2,1)} %copy.61), calls=%async_computation.1 | async-start | bytes 1048576 | tf_op jit(solution)/shard_map/all_to_all | solution.py:481
  214.8 0.7 copy.64
  215.5 0.8 copy_bitcast_fusion
  216.3 6.6 %all-to-all-done.1 = bf16[16,2,64,128]{3,2,1,0:T(8,128)(2,1)S(1)} async-done(((bf16[16,2,64,128]{3,2,1,0:T(8,128)(2,1)}), bf16[16,2,64,128]{3,2,1,0:T(8,128)(2,1)S(1)}, u32[]{:S(2)}, u32[]{:S(2)}) %all-to-all-start.1) | async-done | bytes 524320 | tf_op jit(solution)/shard_map/all_to_all | solution.py:481
  222.9 0.8 copy-done.9
  223.7 45.4 %shard_map.178 = f32[64,2048]{1,0:T(8,128)} custom-call(s32[16,32]{1,0:T(8,128)} %pattern_ref.1, bf16[32,64,128]{2,1,0:T(8,128)(2,1)} %bitcast.85, f32[32,3,128]{2,1,0:T(4,128)} %bitcast.86, f32[16,128,3]{2,1,0:T(8,128)} %bitcast.84), custom_call_target="tpu_custom_call" | custom-call | tf_op jit(solution)/shard_map/pallas_call | solution.py:274
  269.1 0.6 copy.103
  (36 shorter events, 0.3 us)
Async XLA Ops:
  0.6 3.7 %copy-start = (bf16[16,2,256,128]{3,2,1,0:T(8,128)(2,1)S(1)}, bf16[16,2,256,128]{3,2,1,0:T(8,128)(2,1)}, u32[]{:S(2)}) copy-start(bf16[16,2,256,128]{3,2,1,0:T(8,128)(2,1)} %param.19) | copy-start | bytes 6291460
  4.3 0.9 copy-start.5
  4.3 0.9 copy-start.14
  5.2 11.3 %copy-start.13 = (s32[16,1]{0,1:T(1,128)S(1)}, s32[16,1]{0,1:T(1,128)}, u32[]{:S(2)}) copy-start(s32[16,1]{0,1:T(1,128)} %param.26) | copy-start | bytes 196
  5.2 11.6 %copy-start.12 = (f32[16,3,128]{2,0,1:T(8,128)S(1)}, f32[16,3,128]{2,0,1:T(8,128)}, u32[]{:S(2)}) copy-start(f32[16,3,128]{2,0,1:T(8,128)} %param.27) | copy-start | bytes 73732
  5.2 12.3 %copy-start.11 = (f32[1,3,2048]{2,0,1:T(1,128)S(1)}, f32[1,3,2048]{2,0,1:T(1,128)}, u32[]{:S(2)}) copy-start(f32[1,3,2048]{2,0,1:T(1,128)} %param.28) | copy-start | bytes 73732
  7.3 24.2 %copy-start.10 = (f32[64,256]{1,0:T(8,128)S(1)}, f32[64,256]{1,0:T(8,128)}, u32[]{:S(2)}) copy-start(f32[64,256]{1,0:T(8,128)} %param.16) | copy-start | bytes 196612
  7.3 24.2 %copy-start.4 = (f32[1,256,256]{2,1,0:T(8,128)S(1)}, f32[1,256,256]{2,1,0:T(8,128)}, u32[]{:S(2)}) copy-start(f32[1,256,256]{2,1,0:T(8,128)} %param.21) | copy-start | bytes 786436
  8.3 17.6 %all-to-all-start = ((bf16[16,1,64,256]{3,2,1,0:T(8,128)(2,1)}), bf16[16,1,64,256]{3,2,1,0:T(8,128)(2,1)S(1)}, u32[]{:S(2)}, u32[]{:S(2)}) async-start(bf16[16,1,64,256]{3,2,1,0:T(8,128)(2,1)} %copy.56), calls=%async_computation | async-start | bytes 1048576 | tf_op jit(solution)/shard_map/all_to_all | solution.py:27
  25.9 182.4 %all-to-all-start.2 = ((bf16[16,2,3,128]{3,1,2,0:T(2,128)(2,1)}), bf16[16,2,3,128]{3,1,2,0:T(2,128)(2,1)S(1)}, u32[]{:S(2)}, u32[]{:S(2)}) async-start(bf16[16,2,3,128]{3,1,2,0:T(2,128)(2,1)} %copy.62), calls=%async_computation.2 | async-start | bytes 49152 | tf_op jit(solution)/shard_map/all_to_all | solution.py:482
  31.6 1.6 copy-start.1
  84.8 39.3 %copy-start.3 = (f32[16,128,128]{2,1,0:T(8,128)S(1)}, f32[16,128,128]{2,1,0:T(8,128)}, u32[]{:S(2)}) copy-start(f32[16,128,128]{2,1,0:T(8,128)} %inv_ref.1) | copy-start | bytes 3145732
  124.0 16.9 %copy-start.7 = (bf16[256,2048]{1,0:T(8,128)(2,1)S(1)}, bf16[256,2048]{1,0:T(8,128)(2,1)}, u32[]{:S(2)}) copy-start(bf16[256,2048]{1,0:T(8,128)(2,1)} %param.23) | copy-start | bytes 3145732
  124.0 17.3 %copy-start.2 = (bf16[1,16,256,256]{3,2,1,0:T(8,128)(2,1)S(1)}, bf16[1,16,256,256]{3,2,1,0:T(8,128)(2,1)}, u32[]{:S(2)}) copy-start(bf16[1,16,256,256]{3,2,1,0:T(8,128)(2,1)} %param.22) | copy-start | bytes 6291460
  141.4 63.4 %copy-start.6 = (f32[16,64,128]{2,1,0:T(8,128)S(1)}, f32[16,64,128]{2,1,0:T(8,128)}, u32[]{:S(2)}) copy-start(f32[16,64,128]{2,1,0:T(8,128)} %copy-done.5) | copy-start | bytes 1572868
  204.8 1.2 copy-start.8
  208.3 14.6 %all-to-all-start.1 = ((bf16[16,2,64,128]{3,2,1,0:T(8,128)(2,1)}), bf16[16,2,64,128]{3,2,1,0:T(8,128)(2,1)S(1)}, u32[]{:S(2)}, u32[]{:S(2)}) async-start(bf16[16,2,64,128]{3,2,1,0:T(8,128)(2,1)} %copy.61), calls=%async_computation.1 | async-start | bytes 1048576 | tf_op jit(solution)/shard_map/all_to_all | solution.py:481
  222.9 0.8 copy-start.9

commit v7 on v6

--- a/solution.py
+++ b/solution.py
@@ -92,11 +92,37 @@
     )
 
 
-def sep_forward_kernel(n, start_ref, inv_ref, blocks_ref, sol_ref, halves, resid, send_sem, recv_sem):
+def sep_forward_kernel(n, rhs_ref, part_ref, inv_ref, blocks_ref, sol_ref, halves, resid, send_sem, recv_sem, arrived, local_sem, give_sem, take_sem):
     me = lax.axis_index("grp")
     leaf = lax.axis_index("leaf")
     _greet_group(n, leaf, me)
-    resid[...] = start_ref[...]
+
+    def give(dest):
+        return pltpu.make_async_remote_copy(
+            part_ref.at[dest], arrived.at[me], give_sem.at[dest], take_sem.at[me], device_id=(leaf, dest), device_id_type=MESH
+        )
+
+    own = pltpu.make_async_copy(part_ref.at[me], arrived.at[me], local_sem.at[0])
+    own.start()
+    for dest in range(n):
+        @pl.when(me != dest)
+        def _():
+            give(dest).start()
+    own.wait()
+    for src in range(n):
+        @pl.when(me != src)
+        def _():
+            pltpu.make_async_remote_copy(
+                part_ref.at[src], arrived.at[src], give_sem.at[src], take_sem.at[src], device_id=(leaf, src), device_id_type=MESH
+            ).wait_recv()
+    total = arrived[0].astype(jnp.float32)
+    for src in range(1, n):
+        total = total + arrived[src].astype(jnp.float32)
+    resid[...] = rhs_ref[...] - total
+    for dest in range(n):
+        @pl.when(me != dest)
+        def _():
+            give(dest).wait_send()
 
     def step(q, carry):
         @pl.when(me == q)
@@ -159,7 +185,7 @@
 
 
 def sep_solve(kind, start, inv, blocks, n):
-    rows, width = start.shape
+    rows, width = (start[0] if kind == "forward" else start).shape
     vmem = pl.BlockSpec(memory_space=pltpu.VMEM)
     scratch = [
         pltpu.VMEM((n, rows, width), jnp.bfloat16),
@@ -170,14 +196,21 @@
     sol_shape = jax.ShapeDtypeStruct((rows, width), jnp.float32)
     params = dict(has_side_effects=True, vmem_limit_bytes=48 * 1024 * 1024)
     if kind == "forward":
+        rhs, parts = start
         return pl.pallas_call(
             functools.partial(sep_forward_kernel, n),
             out_shape=sol_shape,
-            in_specs=[vmem] * 3,
+            in_specs=[vmem] * 4,
             out_specs=vmem,
-            scratch_shapes=scratch,
+            scratch_shapes=scratch
+            + [
+                pltpu.VMEM(parts.shape, parts.dtype),
+                pltpu.SemaphoreType.DMA((1,)),
+                pltpu.SemaphoreType.DMA((n,)),
+                pltpu.SemaphoreType.DMA((n,)),
+            ],
             compiler_params=pltpu.CompilerParams(collective_id=0, **params),
-        )(start, inv, blocks)
+        )(rhs, parts, inv, blocks)
     return pl.pallas_call(
         functools.partial(sep_backward_kernel, n),
         out_shape=(sol_shape, jax.ShapeDtypeStruct((n, rows, width), jnp.bfloat16)),
@@ -432,16 +465,10 @@
     )
     onehot = (leaf_targets[:, :, None] == jnp.arange(grp_size)[None, None, :]).astype(jnp.float32)
     picked = onehot
-    shared = sum_at_owner(
-        jnp.einsum("ncq,ncrb->qrb", picked, partial_value, precision=highest).astype(jnp.bfloat16),
-        "grp",
-        0,
-    )
-    sep_start = rhs_sep - shared[0]
+    parts = jnp.einsum("ncq,ncrb->qrb", picked, partial_value, precision=highest).astype(jnp.bfloat16)
     inverse_own = sep_inverse[0]
     own_blocks = sep_blocks[0]
-
-    sep_sol = sep_solve("forward", sep_start, inverse_own, own_blocks, grp_size)
+    sep_sol = sep_solve("forward", (rhs_sep, parts), inverse_own, own_blocks, grp_size)
     sep_half = sep_sol.astype(jnp.bfloat16)
     top_term = jnp.dot(sep_half, top_coupling, preferred_element_type=jnp.float32)
     top_total = top_reduce(top_term, grp_size, lax.axis_size("leaf"))

time: 274 us -> 269 us (0.982)
  Pallas kernels: 212 us -> 223 us
  waiting for transfers between devices: 13.5 us -> 6.57 us
  starting transfers between devices: 20.2 us -> 14.2 us
    all_to_all x1 -> x0, starting transfers between devices: 8.19 us -> none  [sum_at_owner(): lax.all_to_all(pieces, axis, split_axis=0, concat_axis=0, tiled=True)]
    pallas_call x1, Pallas kernels: 51.6 us -> 58.8 us  [sep_solve(): pl.pallas_call(functools.partial(sep_forward_kernel, n), out_shape=sol_sh...]
    all_to_all x1 -> x0, waiting for transfers between devices: 6.96 us -> none  [sum_at_owner(): lax.all_to_all(pieces, axis, split_axis=0, concat_axis=0, tiled=True)]
  transfers between devices with their start and end apart: 3 -> 2, of which waited for: 2 -> 1; matrix products, arithmetic and copies ran while one was open for 4% -> 6% of each run, Pallas kernels for 62% -> 66%
where the time goes in v7:
time: 269 us; the launch traced here: 266 us
  Pallas kernels  223 us (83%)
  starting transfers between devices  14.2 us (5%)
  matrix products  11.3 us (4%)
  local copies, waits for them, and re-layouts  6.7 us (2%)
  waiting for transfers between devices  6.57 us (2%)
  other arithmetic  3.68 us (1%)
    pallas_call x1, Pallas kernels, sep_solve(): pl.pallas_call(functools.partial(sep_backward_kernel, n), out_shape=(sol_...  64 us
    pallas_call x1, Pallas kernels, sep_solve(): pl.pallas_call(functools.partial(sep_forward_kernel, n), out_shape=sol_sh...  58.8 us
    pallas_call x1, Pallas kernels, evaluate_all(): pl.pallas_call(functools.partial(evaluate_kernel, slots), out_shape=jax.S...  47.5 us
    pallas_call x1, Pallas kernels, top_reduce(): pl.pallas_call(functools.partial(top_reduce_kernel, n, groups, span), out...  35.6 us
    pallas_call x1, Pallas kernels, top_solve(): pl.pallas_call(functools.partial(top_solve_kernel, nt, span), out_shape=(...  16.9 us
    all_to_all x1, starting transfers between devices, on_device(): lax.all_to_all(send_centre.astype(jnp.bfloat16), 'grp', split_axis=0, con...  8.18 us
    all_to_all x1, waiting for transfers between devices, on_device(): lax.all_to_all(send_coef, 'grp', split_axis=0, concat_axis=0, tiled=True)  6.57 us
    all_to_all x1, starting transfers between devices, on_device(): lax.all_to_all(send_coef, 'grp', split_axis=0, concat_axis=0, tiled=True)  6.04 us
  transfers between devices with their start and end apart: 2, of which 1 were waited for; matrix products, arithmetic and copies ran while one was open for 6% of the time, Pallas kernels for 66%

profile of v7, /device:TPU:24, one launch (start us, length us, event | category | flops | bytes accessed | tf_op | source)
XLA Modules:
  0.0 266.1 jit_solution(4802084654970679845)
XLA Ops:
  0.6 0.0 copy-start
  0.6 0.9 fusion.26
  1.5 0.7 iota_compare_fusion.2
  2.2 0.8 select_reduce_fusion
  3.1 0.9 convolution_convert_fusion.2
  4.0 0.6 copy.64
  4.6 8.2 %all-to-all-start.1 = ((bf16[16,2,3,128]{3,1,2,0:T(2,128)(2,1)}), bf16[16,2,3,128]{3,1,2,0:T(2,128)(2,1)S(1)}, u32[]{:S(2)}, u32[]{:S(2)}) async-start(bf16[16,2,3,128]{3,1,2,0:T(2,128)(2,1)} %copy.64), calls=%async_computation.1 | async-start | bytes 49152 | tf_op jit(solution)/shard_map/all_to_all | solution.py:509
  12.8 3.5 %fusion.7 = f32[16,64,128]{2,1,0:T(8,128)S(1)} fusion(f32[16,128,128]{2,1,0:T(8,128)} %param.18, f32[64,2048]{1,0:T(8,128)} %param.15), kind=kOutput, calls=%fused_computation.14 | convolution fusion | flops 201326592 | bytes 2097152 | tf_op jit(solution)/shard_map/nrs,nts->nrt/dot_general | solution.py:461
  16.3 0.8 convolution_bitcast_fusion
  17.2 2.0 fusion.2
  19.3 0.2 copy.100.part_ref
  19.5 58.8 %shard_map.174 = f32[64,256]{1,0:T(8,128)S(1)} custom-call(f32[64,256]{1,0:T(8,128)S(1)} %copy-done.5, bf16[16,64,256]{2,1,0:T(8,128)(2,1)S(1)} %copy.100.part_ref, f32[256,256]{1,0:T(8,128)S(1)} %bitcast.76, bf16[16,256,256]{2,1,0:T(8,128)(2,1)S(1)} %bitcast.74), custom_call_target="tpu_custom_call" | custom-call | tf_op jit(solution)/shard_map/pallas_call | solution.py:200
  78.3 1.1 fusion.15.term_ref
  79.4 35.6 %shard_map.175 = f32[64,2048]{1,0:T(8,128)} custom-call(f32[64,2048]{1,0:T(8,128)} %fusion.15.term_ref), custom_call_target="tpu_custom_call" | custom-call | tf_op jit(solution)/shard_map/pallas_call | solution.py:400
  115.0 1.3 sub.20.start_ref
  116.3 16.9 %shard_map.176 = (f32[64,2048]{1,0:T(8,128)}, bf16[64,2048]{1,0:T(8,128)(2,1)S(1)}) custom-call(f32[64,2048]{1,0:T(8,128)S(1)} %sub.20.start_ref, f32[16,128,128]{2,1,0:T(8,128)S(1)} %copy-done.3, bf16[2048,2048]{1,0:T(8,128)(2,1)} %lower_ref.1), custom_call_target="tpu_custom_call" | custom-call | tf_op jit(solution)/shard_map/pallas_call | solution.py:247
  133.1 0.4 convolution_subtract_fusion.start_ref
  133.6 64.0 %shard_map.177 = (f32[64,256]{1,0:T(8,128)S(1)}, bf16[16,64,256]{2,1,0:T(8,128)(2,1)S(1)}) custom-call(f32[64,256]{1,0:T(8,128)S(1)} %convolution_subtract_fusion.start_ref, f32[256,256]{1,0:T(8,128)S(1)} %bitcast.77, bf16[16,256,256]{2,1,0:T(8,128)(2,1)S(1)} %bitcast.75), custom_call_target="tpu_custom_call" | custom-call | tf_op jit(solution)/shard_map/pallas_call | solution.py:214
  197.6 0.5 convolution_convert_fusion
  198.1 0.6 fusion.5
  198.8 0.6 copy-done.10
  199.4 1.1 fusion.33
  200.4 0.3 convolution_convert_fusion.1
  200.7 0.9 copy.63
  201.7 1.4 copy.67
  203.0 6.0 %all-to-all-start = ((bf16[16,2,64,128]{3,2,1,0:T(8,128)(2,1)}), bf16[16,2,64,128]{3,2,1,0:T(8,128)(2,1)S(1)}, u32[]{:S(2)}, u32[]{:S(2)}) async-start(bf16[16,2,64,128]{3,2,1,0:T(8,128)(2,1)} %copy.63), calls=%async_computation | async-start | bytes 1048576 | tf_op jit(solution)/shard_map/all_to_all | solution.py:508
  209.1 0.8 copy_bitcast_fusion
  209.9 0.7 copy.66
  210.6 6.6 %all-to-all-done = bf16[16,2,64,128]{3,2,1,0:T(8,128)(2,1)S(1)} async-done(((bf16[16,2,64,128]{3,2,1,0:T(8,128)(2,1)}), bf16[16,2,64,128]{3,2,1,0:T(8,128)(2,1)S(1)}, u32[]{:S(2)}, u32[]{:S(2)}) %all-to-all-start) | async-done | bytes 524320 | tf_op jit(solution)/shard_map/all_to_all | solution.py:508
  217.1 0.8 copy-done.11
  218.0 47.5 %shard_map.178 = f32[64,2048]{1,0:T(8,128)} custom-call(s32[16,32]{1,0:T(8,128)} %pattern_ref.1, bf16[32,64,128]{2,1,0:T(8,128)(2,1)} %bitcast.79, f32[32,3,128]{2,1,0:T(4,128)} %bitcast.80, f32[16,128,3]{2,1,0:T(8,128)} %bitcast.78), custom_call_target="tpu_custom_call" | custom-call | tf_op jit(solution)/shard_map/pallas_call | solution.py:307
  265.5 0.6 copy.103
  (30 shorter events, 0.1 us)
Async XLA Ops:
  0.6 15.7 %copy-start = (bf16[16,2,256,128]{3,2,1,0:T(8,128)(2,1)S(1)}, bf16[16,2,256,128]{3,2,1,0:T(8,128)(2,1)}, u32[]{:S(2)}) copy-start(bf16[16,2,256,128]{3,2,1,0:T(8,128)(2,1)} %param.19) | copy-start | bytes 6291460
  4.6 198.4 %all-to-all-start.1 = ((bf16[16,2,3,128]{3,1,2,0:T(2,128)(2,1)}), bf16[16,2,3,128]{3,1,2,0:T(2,128)(2,1)S(1)}, u32[]{:S(2)}, u32[]{:S(2)}) async-start(bf16[16,2,3,128]{3,1,2,0:T(2,128)(2,1)} %copy.64), calls=%async_computation.1 | async-start | bytes 49152 | tf_op jit(solution)/shard_map/all_to_all | solution.py:509
  16.3 0.9 copy-start.6
  16.3 0.9 copy-start.13
  17.2 2.3 copy-start.1
  17.2 2.3 copy-start.4
  17.2 2.3 copy-start.5
  19.3 59.0 %copy-start.8 = (bf16[256,2048]{1,0:T(8,128)(2,1)S(1)}, bf16[256,2048]{1,0:T(8,128)(2,1)}, u32[]{:S(2)}) copy-start(bf16[256,2048]{1,0:T(8,128)(2,1)} %param.23) | copy-start | bytes 3145732
  78.3 38.0 %copy-start.3 = (f32[16,128,128]{2,1,0:T(8,128)S(1)}, f32[16,128,128]{2,1,0:T(8,128)}, u32[]{:S(2)}) copy-start(f32[16,128,128]{2,1,0:T(8,128)} %inv_ref.1) | copy-start | bytes 3145732
  116.2 16.9 %copy-start.9 = (bf16[256,2048]{1,0:T(8,128)(2,1)S(1)}, bf16[256,2048]{1,0:T(8,128)(2,1)}, u32[]{:S(2)}) copy-start(bf16[256,2048]{1,0:T(8,128)(2,1)} %param.23) | copy-start | bytes 3145732
  116.3 17.3 %copy-start.2 = (bf16[1,16,256,256]{3,2,1,0:T(8,128)(2,1)S(1)}, bf16[1,16,256,256]{3,2,1,0:T(8,128)(2,1)}, u32[]{:S(2)}) copy-start(bf16[1,16,256,256]{3,2,1,0:T(8,128)(2,1)} %param.22) | copy-start | bytes 6291460
  133.6 64.5 %copy-start.7 = (f32[16,64,128]{2,1,0:T(8,128)S(1)}, f32[16,64,128]{2,1,0:T(8,128)}, u32[]{:S(2)}) copy-start(f32[16,64,128]{2,1,0:T(8,128)} %copy-done.6) | copy-start | bytes 1572868
  198.1 1.2 copy-start.10
  199.3 2.3 copy-start.12
  203.0 14.1 %all-to-all-start = ((bf16[16,2,64,128]{3,2,1,0:T(8,128)(2,1)}), bf16[16,2,64,128]{3,2,1,0:T(8,128)(2,1)S(1)}, u32[]{:S(2)}, u32[]{:S(2)}) async-start(bf16[16,2,64,128]{3,2,1,0:T(8,128)(2,1)} %copy.63), calls=%async_computation | async-start | bytes 1048576 | tf_op jit(solution)/shard_map/all_to_all | solution.py:508
  217.1 0.8 copy-start.11

commit v8 on v7

--- a/solution.py
+++ b/solution.py
@@ -418,6 +418,61 @@
     )(term)
 
 
+def exchange_kernel(n, coef_ref, centre_ref, coef_out, centre_out, coef_buf, centre_buf, local_sem, send_sem, recv_sem):
+    me = lax.axis_index("grp")
+    leaf = lax.axis_index("leaf")
+    _greet_group(n, leaf, me)
+    pairs = ((coef_ref, coef_buf), (centre_ref, centre_buf))
+
+    def push(kind, k):
+        source, buf = pairs[kind]
+        dest = lax.rem(me + k, n)
+        return pltpu.make_async_remote_copy(
+            source.at[dest], buf.at[me], send_sem.at[kind, k], recv_sem.at[kind, me], device_id=(leaf, dest), device_id_type=MESH
+        )
+
+    owns = [pltpu.make_async_copy(source.at[me], buf.at[me], local_sem.at[kind]) for kind, (source, buf) in enumerate(pairs)]
+    for own in owns:
+        own.start()
+    for k in range(1, n):
+        for kind in range(2):
+            push(kind, k).start()
+    for own in owns:
+        own.wait()
+    for k in range(1, n):
+        src = lax.rem(me + n - k, n)
+        for kind, (source, buf) in enumerate(pairs):
+            pltpu.make_async_remote_copy(
+                source.at[src], buf.at[src], send_sem.at[kind, 0], recv_sem.at[kind, src], device_id=(leaf, src), device_id_type=MESH
+            ).wait_recv()
+    for k in range(1, n):
+        for kind in range(2):
+            push(kind, k).wait_send()
+    coef_out[...] = coef_buf[...]
+    centre_out[...] = centre_buf[...]
+
+
+def exchange(send_coef, send_centre, n):
+    vmem = pl.BlockSpec(memory_space=pltpu.VMEM)
+    return pl.pallas_call(
+        functools.partial(exchange_kernel, n),
+        out_shape=(
+            jax.ShapeDtypeStruct(send_coef.shape, send_coef.dtype),
+            jax.ShapeDtypeStruct(send_centre.shape, send_centre.dtype),
+        ),
+        in_specs=[vmem] * 2,
+        out_specs=(vmem, vmem),
+        scratch_shapes=[
+            pltpu.VMEM(send_coef.shape, send_coef.dtype),
+            pltpu.VMEM(send_centre.shape, send_centre.dtype),
+            pltpu.SemaphoreType.DMA((2,)),
+            pltpu.SemaphoreType.DMA((2, n)),
+            pltpu.SemaphoreType.DMA((2, n)),
+        ],
+        compiler_params=pltpu.CompilerParams(collective_id=3, has_side_effects=True),
+    )(send_coef, send_centre)
+
+
 def slot_ranks(dest_rows, grp_size):
     onehot = (dest_rows[..., None] == jnp.arange(grp_size)).astype(jnp.int32)
     before = jnp.cumsum(onehot, axis=-2) - onehot
@@ -504,12 +559,7 @@
     send_centre = jnp.einsum(
         "dkj,jct->dkct", selector.astype(jnp.float32), centers, precision=highest
     )
-    received, recv_centre = (
-        lax.all_to_all(send_coef, "grp", split_axis=0, concat_axis=0, tiled=True),
-        lax.all_to_all(
-            send_centre.astype(jnp.bfloat16), "grp", split_axis=0, concat_axis=0, tiled=True
-        ).astype(send_centre.dtype),
-    )
+    received, recv_centre = exchange(send_coef, send_centre, grp_size)
     slot_total = grp_size * slot_count
     coef_all = received.reshape(slot_total, snapshots, span)
     centre_all = recv_centre.reshape(slot_total, 3, span)

time: 269 us -> 259 us (0.963)
  the two profiles are of different devices: /device:TPU:24 before, /device:TPU:16 now
where the time goes in v8:
time: 259 us
  Pallas kernels  241 us (93%)
  matrix products  10.7 us (4%)
  local copies, waits for them, and re-layouts  5.25 us (2%)
    pallas_call x1, Pallas kernels, sep_solve(): pl.pallas_call(functools.partial(sep_backward_kernel, n), out_shape=(sol_...  62.4 us
    pallas_call x1, Pallas kernels, evaluate_all(): pl.pallas_call(functools.partial(evaluate_kernel, slots), out_shape=jax.S...  51.6 us
    pallas_call x1, Pallas kernels, top_reduce(): pl.pallas_call(functools.partial(top_reduce_kernel, n, groups, span), out...  49.7 us
    pallas_call x1, Pallas kernels, sep_solve(): pl.pallas_call(functools.partial(sep_forward_kernel, n), out_shape=sol_sh...  45.7 us
    pallas_call x1, Pallas kernels, top_solve(): pl.pallas_call(functools.partial(top_solve_kernel, nt, span), out_shape=(...  16.9 us
    pallas_call x1, Pallas kernels, exchange(): pl.pallas_call(functools.partial(exchange_kernel, n), out_shape=(jax.Shap...  14.4 us

profile of v8, /device:TPU:16, one launch (start us, length us, event | category | flops | bytes accessed | tf_op | source)
XLA Modules:
  0.0 259.1 jit_solution(9017336322122044692)
XLA Ops:
  0.6 0.0 copy-start
  0.6 3.7 %fusion.7 = f32[16,64,128]{2,1,0:T(8,128)S(1)} fusion(f32[16,128,128]{2,1,0:T(8,128)} %param.18, f32[64,2048]{1,0:T(8,128)} %param.15), kind=kOutput, calls=%fused_computation.12 | convolution fusion | flops 201326592 | bytes 2097152 | tf_op jit(solution)/shard_map/nrs,nts->nrt/dot_general | solution.py:516
  4.3 0.0 copy-start.14
  4.3 0.8 fusion.11
  5.2 0.0 copy-start.1
  5.2 0.0 copy-start.4
  5.2 2.0 fusion.3
  7.3 0.0 copy-start.8
  7.3 0.2 copy.66.part_ref
  7.5 45.7 %shard_map.174 = f32[64,256]{1,0:T(8,128)S(1)} custom-call(f32[64,256]{1,0:T(8,128)S(1)} %copy-done.5, bf16[16,64,256]{2,1,0:T(8,128)(2,1)S(1)} %copy.66.part_ref, f32[256,256]{1,0:T(8,128)S(1)} %bitcast.77, bf16[16,256,256]{2,1,0:T(8,128)(2,1)S(1)} %bitcast.75), custom_call_target="tpu_custom_call" | custom-call | tf_op jit(solution)/shard_map/pallas_call | solution.py:200
  53.2 1.1 fusion.17.term_ref
  54.3 49.7 %shard_map.175 = f32[64,2048]{1,0:T(8,128)} custom-call(f32[64,2048]{1,0:T(8,128)} %fusion.17.term_ref), custom_call_target="tpu_custom_call" | custom-call | tf_op jit(solution)/shard_map/pallas_call | solution.py:400
  104.1 1.3 sub.20.start_ref
  105.4 0.0 copy-start.2
  105.4 16.9 %shard_map.176 = (f32[64,2048]{1,0:T(8,128)}, bf16[64,2048]{1,0:T(8,128)(2,1)S(1)}) custom-call(f32[64,2048]{1,0:T(8,128)S(1)} %sub.20.start_ref, f32[16,128,128]{2,1,0:T(8,128)S(1)} %copy-done.3, bf16[2048,2048]{1,0:T(8,128)(2,1)} %lower_ref.1), custom_call_target="tpu_custom_call" | custom-call | tf_op jit(solution)/shard_map/pallas_call | solution.py:247
  122.2 0.4 convolution_subtract_fusion.start_ref
  122.7 62.4 %shard_map.177 = (f32[64,256]{1,0:T(8,128)S(1)}, bf16[16,64,256]{2,1,0:T(8,128)(2,1)S(1)}) custom-call(f32[64,256]{1,0:T(8,128)S(1)} %convolution_subtract_fusion.start_ref, f32[256,256]{1,0:T(8,128)S(1)} %bitcast.78, bf16[16,256,256]{2,1,0:T(8,128)(2,1)S(1)} %bitcast.76), custom_call_target="tpu_custom_call" | custom-call | tf_op jit(solution)/shard_map/pallas_call | solution.py:214
  185.1 0.5 fusion.9
  185.6 0.6 fusion.6
  186.2 0.6 copy-done.10
  186.8 1.1 fusion.36
  187.9 0.8 copy_bitcast_fusion
  188.8 0.1 fusion.29
  188.9 0.2 select_reduce_fusion
  189.1 0.3 fusion.13
  189.4 0.9 copy.65.coef_ref
  190.3 0.1 fusion.19
  190.4 0.7 copy.30.centre_ref
  191.1 14.4 %shard_map.178 = (bf16[16,2,64,128]{3,2,1,0:T(8,128)(2,1)}, f32[16,2,3,128]{3,2,1,0:T(4,128)}) custom-call(bf16[16,2,64,128]{3,2,1,0:T(8,128)(2,1)} %copy.65.coef_ref, f32[16,2,3,128]{3,2,1,0:T(4,128)} %copy.30.centre_ref), custom_call_target="tpu_custom_call" | custom-call | tf_op jit(solution)/shard_map/pallas_call | solution.py:457
  205.5 1.3 copy.31
  206.8 51.6 %shard_map.179 = f32[64,2048]{1,0:T(8,128)} custom-call(s32[16,32]{1,0:T(8,128)} %pattern_ref.1, bf16[32,64,128]{2,1,0:T(8,128)(2,1)} %bitcast.81, f32[32,3,128]{2,1,0:T(4,128)} %bitcast.83, f32[16,128,3]{2,1,0:T(8,128)} %bitcast.80), custom_call_target="tpu_custom_call" | custom-call | tf_op jit(solution)/shard_map/pallas_call | solution.py:307
  258.5 0.6 copy.69
  (27 shorter events, 0.1 us)
Async XLA Ops:
  0.6 3.7 %copy-start = (bf16[16,2,256,128]{3,2,1,0:T(8,128)(2,1)S(1)}, bf16[16,2,256,128]{3,2,1,0:T(8,128)(2,1)}, u32[]{:S(2)}) copy-start(bf16[16,2,256,128]{3,2,1,0:T(8,128)(2,1)} %param.19) | copy-start | bytes 6291460
  4.3 0.9 copy-start.6
  4.3 0.9 copy-start.14
  5.2 2.3 copy-start.1
  5.2 2.3 copy-start.4
  5.2 2.3 copy-start.5
  7.3 45.9 %copy-start.8 = (bf16[256,2048]{1,0:T(8,128)(2,1)S(1)}, bf16[256,2048]{1,0:T(8,128)(2,1)}, u32[]{:S(2)}) copy-start(bf16[256,2048]{1,0:T(8,128)(2,1)} %param.23) | copy-start | bytes 3145732
  53.2 52.1 %copy-start.3 = (f32[16,128,128]{2,1,0:T(8,128)S(1)}, f32[16,128,128]{2,1,0:T(8,128)}, u32[]{:S(2)}) copy-start(f32[16,128,128]{2,1,0:T(8,128)} %inv_ref.1) | copy-start | bytes 3145732
  105.3 16.9 %copy-start.9 = (bf16[256,2048]{1,0:T(8,128)(2,1)S(1)}, bf16[256,2048]{1,0:T(8,128)(2,1)}, u32[]{:S(2)}) copy-start(bf16[256,2048]{1,0:T(8,128)(2,1)} %param.23) | copy-start | bytes 3145732
  105.4 17.3 %copy-start.2 = (bf16[1,16,256,256]{3,2,1,0:T(8,128)(2,1)S(1)}, bf16[1,16,256,256]{3,2,1,0:T(8,128)(2,1)}, u32[]{:S(2)}) copy-start(bf16[1,16,256,256]{3,2,1,0:T(8,128)(2,1)} %param.22) | copy-start | bytes 6291460
  122.7 62.9 %copy-start.7 = (f32[16,64,128]{2,1,0:T(8,128)S(1)}, f32[16,64,128]{2,1,0:T(8,128)}, u32[]{:S(2)}) copy-start(f32[16,64,128]{2,1,0:T(8,128)} %copy-done.6) | copy-start | bytes 1572868
  185.6 1.2 copy-start.10
  186.8 1.9 copy-start.13
  186.8 3.5 %copy-start.12 = (f32[16,3,128]{2,0,1:T(8,128)S(1)}, f32[16,3,128]{2,0,1:T(8,128)}, u32[]{:S(2)}) copy-start(f32[16,3,128]{2,0,1:T(8,128)} %param.27) | copy-start | bytes 73732
  187.9 17.6 %copy-start.11 = (f32[1,3,2048]{2,0,1:T(1,128)S(1)}, f32[1,3,2048]{2,0,1:T(1,128)}, u32[]{:S(2)}) copy-start(f32[1,3,2048]{2,0,1:T(1,128)} %param.28) | copy-start | bytes 73732

commit v9 on v8

--- a/solution.py
+++ b/solution.py
@@ -92,7 +92,26 @@
     )
 
 
-def sep_forward_kernel(n, rhs_ref, part_ref, inv_ref, blocks_ref, sol_ref, halves, resid, send_sem, recv_sem, arrived, local_sem, give_sem, take_sem):
+def _send_block(n, halves, s, solved, sol_ref, send_sem, recv_sem, leaf, dests):
+    sol_ref[...] = solved
+    halves[s] = solved.astype(jnp.bfloat16)
+    for k in range(1, n):
+        dest, live = dests(s, k)
+        @pl.when(live)
+        def _():
+            _block_copy(halves, s, dest, send_sem.at[k], recv_sem, leaf).start()
+    for k in range(1, n):
+        dest, live = dests(s, k)
+        @pl.when(live)
+        def _():
+            _block_copy(halves, s, dest, send_sem.at[k], recv_sem, leaf).wait_send()
+
+
+def _through(y, hi_ref, lo_ref):
+    return _nn(y, hi_ref[...]) + _nn(y, lo_ref[...])
+
+
+def sep_forward_kernel(n, rhs_ref, part_ref, inv_ref, blocks_ref, hi_ref, lo_ref, sol_ref, halves, resid, base, send_sem, recv_sem, arrived, local_sem, give_sem, take_sem):
     me = lax.axis_index("grp")
     leaf = lax.axis_index("leaf")
     _greet_group(n, leaf, me)
@@ -124,71 +143,87 @@
         def _():
             give(dest).wait_send()
 
+    dests = lambda s, k: (s + k, s + k < n)
+
+    @pl.when(me == 0)
+    def _():
+        _send_block(n, halves, 0, _nt_exact(resid[...], inv_ref[...]), sol_ref, send_sem, recv_sem, leaf, dests)
+
+    @pl.when(me == 1)
+    def _():
+        base[...] = _nt_exact(resid[...], inv_ref[...])
+
     def step(q, carry):
-        @pl.when(me == q)
-        def _():
-            solved = _nt_exact(resid[...], inv_ref[...])
-            sol_ref[...] = solved
-            halves[q] = solved.astype(jnp.bfloat16)
-            for k in range(1, n):
-                @pl.when(q + k < n)
-                def _():
-                    _block_copy(halves, q, q + k, send_sem.at[k], recv_sem, leaf).start()
-            for k in range(1, n):
-                @pl.when(q + k < n)
-                def _():
-                    _block_copy(halves, q, q + k, send_sem.at[k], recv_sem, leaf).wait_send()
-
-        @pl.when(me > q)
+        @pl.when(me == q + 1)
+        def _():
+            _block_copy(halves, q, q, send_sem.at[0], recv_sem, leaf).wait_recv()
+            solved = base[...] - _through(halves[q], hi_ref, lo_ref)
+            _send_block(n, halves, q + 1, solved, sol_ref, send_sem, recv_sem, leaf, dests)
+
+        @pl.when(me > q + 1)
         def _():
             _block_copy(halves, q, q, send_sem.at[0], recv_sem, leaf).wait_recv()
             resid[...] = resid[...] - _nt(halves[q], blocks_ref[q])
 
+            @pl.when(me == q + 2)
+            def _():
+                base[...] = _nt_exact(resid[...], inv_ref[...])
+
         return carry
 
-    lax.fori_loop(0, n, step, 0)
-
-
-def sep_backward_kernel(n, start_ref, inv_ref, blocks_ref, sol_ref, table_ref, halves, resid, send_sem, recv_sem):
+    lax.fori_loop(0, n - 1, step, 0)
+
+
+def sep_backward_kernel(n, start_ref, inv_ref, blocks_ref, hi_ref, lo_ref, sol_ref, table_ref, halves, resid, base, send_sem, recv_sem):
     me = lax.axis_index("grp")
     leaf = lax.axis_index("leaf")
     _greet_group(n, leaf, me)
     resid[...] = start_ref[...]
+    dests = lambda s, k: (lax.rem(s - k + n, n), True)
+
+    @pl.when(me == n - 1)
+    def _():
+        _send_block(n, halves, n - 1, _nn_exact(resid[...], inv_ref[...]), sol_ref, send_sem, recv_sem, leaf, dests)
+
+    @pl.when(me == n - 2)
+    def _():
+        base[...] = _nn_exact(resid[...], inv_ref[...])
 
     def step(s, carry):
         q = n - 1 - s
 
-        @pl.when(me == q)
-        def _():
-            solved = _nn_exact(resid[...], inv_ref[...])
-            sol_ref[...] = solved
-            halves[q] = solved.astype(jnp.bfloat16)
-            for k in range(1, n):
-                dest = lax.rem(q - k + n, n)
-                _block_copy(halves, q, dest, send_sem.at[k], recv_sem, leaf).start()
-            for k in range(1, n):
-                dest = lax.rem(q - k + n, n)
-                _block_copy(halves, q, dest, send_sem.at[k], recv_sem, leaf).wait_send()
-
         @pl.when(me != q)
         def _():
             _block_copy(halves, q, q, send_sem.at[0], recv_sem, leaf).wait_recv()
 
-        @pl.when(me < q)
+        @pl.when(me == q - 1)
+        def _():
+            solved = base[...] - _through(halves[q], hi_ref, lo_ref)
+            _send_block(n, halves, q - 1, solved, sol_ref, send_sem, recv_sem, leaf, dests)
+
+        @pl.when(me < q - 1)
         def _():
             resid[...] = resid[...] - _nn(halves[q], blocks_ref[q])
 
+            @pl.when(me == q - 2)
+            def _():
+                base[...] = _nn_exact(resid[...], inv_ref[...])
+
         return carry
 
-    lax.fori_loop(0, n, step, 0)
+    lax.fori_loop(0, n - 1, step, 0)
+    @pl.when(me != 0)
+    def _():
+        _block_copy(halves, 0, 0, send_sem.at[0], recv_sem, leaf).wait_recv()
     table_ref[...] = halves[...]
 
 
-def sep_solve(kind, start, inv, blocks, n):
+def sep_solve(kind, start, inv, blocks, hi, lo, n):
     rows, width = (start[0] if kind == "forward" else start).shape
     vmem = pl.BlockSpec(memory_space=pltpu.VMEM)
     scratch = [
         pltpu.VMEM((n, rows, width), jnp.bfloat16),
+        pltpu.VMEM((rows, width), jnp.float32),
         pltpu.VMEM((rows, width), jnp.float32),
         pltpu.SemaphoreType.DMA((n,)),
         pltpu.SemaphoreType.DMA((n,)),
@@ -200,7 +235,7 @@
         return pl.pallas_call(
             functools.partial(sep_forward_kernel, n),
             out_shape=sol_shape,
-            in_specs=[vmem] * 4,
+            in_specs=[vmem] * 6,
             out_specs=vmem,
             scratch_shapes=scratch
             + [
@@ -210,15 +245,21 @@
                 pltpu.SemaphoreType.DMA((n,)),
             ],
             compiler_params=pltpu.CompilerParams(collective_id=0, **params),
-        )(rhs, parts, inv, blocks)
+        )(rhs, parts, inv, blocks, hi, lo)
     return pl.pallas_call(
         functools.partial(sep_backward_kernel, n),
         out_shape=(sol_shape, jax.ShapeDtypeStruct((n, rows, width), jnp.bfloat16)),
-        in_specs=[vmem] * 3,
+        in_specs=[vmem] * 5,
         out_specs=(vmem, vmem),
         scratch_shapes=scratch,
         compiler_params=pltpu.CompilerParams(collective_id=1, **params),
-    )(start, inv, blocks)
+    )(start, inv, blocks, hi, lo)
+
+
+def split_pair(matrix):
+    hi = matrix.astype(jnp.bfloat16)
+    lo = (matrix - hi.astype(jnp.float32)).astype(jnp.bfloat16)
+    return hi, lo
 
 
 def top_solve_kernel(nt, span, start_ref, inv_ref, lower_ref, coef_ref, half_ref, fwd_half, fwd_full):
@@ -523,7 +564,13 @@
     parts = jnp.einsum("ncq,ncrb->qrb", picked, partial_value, precision=highest).astype(jnp.bfloat16)
     inverse_own = sep_inverse[0]
     own_blocks = sep_blocks[0]
-    sep_sol = sep_solve("forward", (rhs_sep, parts), inverse_own, own_blocks, grp_size)
+    before = lax.dynamic_index_in_dim(own_blocks, jnp.maximum(my_index - 1, 0), 0, keepdims=False)
+    fwd_hi, fwd_lo = split_pair(
+        jnp.dot(before.astype(jnp.float32).T, inverse_own.T, precision=highest)
+    )
+    after = lax.dynamic_index_in_dim(own_blocks, jnp.minimum(my_index + 1, grp_size - 1), 0, keepdims=False)
+    bwd_hi, bwd_lo = split_pair(jnp.dot(after.astype(jnp.float32), inverse_own, precision=highest))
+    sep_sol = sep_solve("forward", (rhs_sep, parts), inverse_own, own_blocks, fwd_hi, fwd_lo, grp_size)
     sep_half = sep_sol.astype(jnp.bfloat16)
     top_term = jnp.dot(sep_half, top_coupling, preferred_element_type=jnp.float32)
     top_total = top_reduce(top_term, grp_size, lax.axis_size("leaf"))
@@ -533,7 +580,9 @@
         top_half, top_coupling, (((1,), (1,)), ((), ())), preferred_element_type=jnp.float32
     )
 
-    coef_sep, known_table = sep_solve("backward", back_start, inverse_own, own_blocks, grp_size)
+    coef_sep, known_table = sep_solve(
+        "backward", back_start, inverse_own, own_blocks, bwd_hi, bwd_lo, grp_size
+    )
     picked = jnp.einsum(
         "ncq,qrb->ncrb",
         onehot.astype(jnp.bfloat16),

time: 259 us -> 254 us (0.981)
  the two profiles are of different devices: /device:TPU:16 before, /device:TPU:24 now
where the time goes in v9:
time: 254 us; the launch traced here: 251 us
  Pallas kernels  227 us (89%)
  matrix products  13.2 us (5%)
  local copies, waits for them, and re-layouts  8.41 us (3%)
    pallas_call x1, Pallas kernels, sep_solve(): pl.pallas_call(functools.partial(sep_backward_kernel, n), out_shape=(sol_...  60.7 us
    pallas_call x1, Pallas kernels, sep_solve(): pl.pallas_call(functools.partial(sep_forward_kernel, n), out_shape=sol_sh...  55 us
    pallas_call x1, Pallas kernels, evaluate_all(): pl.pallas_call(functools.partial(evaluate_kernel, slots), out_shape=jax.S...  48.2 us
    pallas_call x1, Pallas kernels, top_reduce(): pl.pallas_call(functools.partial(top_reduce_kernel, n, groups, span), out...  34.4 us
    pallas_call x1, Pallas kernels, top_solve(): pl.pallas_call(functools.partial(top_solve_kernel, nt, span), out_shape=(...  16.8 us
    pallas_call x1, Pallas kernels, exchange(): pl.pallas_call(functools.partial(exchange_kernel, n), out_shape=(jax.Shap...  12.4 us

profile of v9, /device:TPU:24, one launch (start us, length us, event | category | flops | bytes accessed | tf_op | source)
XLA Modules:
  0.0 251.5 jit_solution(14400513064349546471)
XLA Ops:
  0.6 0.0 copy-start
  0.6 3.7 %fusion.7 = f32[16,64,128]{2,1,0:T(8,128)S(1)} fusion(f32[16,128,128]{2,1,0:T(8,128)} %param.18, f32[64,2048]{1,0:T(8,128)} %param.15), kind=kOutput, calls=%fused_computation.12 | convolution fusion | flops 201326592 | bytes 2097152 | tf_op jit(solution)/shard_map/nrs,nts->nrt/dot_general | solution.py:557
  4.3 0.9 fusion.11
  5.2 0.0 copy-start.3
  5.2 2.0 fusion.3
  7.3 0.2 copy.66.part_ref
  7.5 1.2 subtract_convert_fusion.1
  8.7 1.6 copy-done.1
  10.3 55.0 %shard_map.174 = f32[64,256]{1,0:T(8,128)S(1)} custom-call(f32[64,256]{1,0:T(8,128)S(1)} %copy-done.5, bf16[16,64,256]{2,1,0:T(8,128)(2,1)S(1)} %copy.66.part_ref, f32[256,256]{1,0:T(8,128)S(1)} %bitcast.95, bf16[16,256,256]{2,1,0:T(8,128)(2,1)S(1)} %bitcast.93, bf16[256,256]{1,0:T(8,128)(2,1)S(1)} %get-tuple-element.19.hi_ref, ...), custom_call_target="tpu_custom_call" | custom-call | tf_op jit(solution)/shard_map/pallas_call | solution.py:235
  65.3 1.1 fusion.23.term_ref
  66.4 34.4 %shard_map.175 = f32[64,2048]{1,0:T(8,128)} custom-call(f32[64,2048]{1,0:T(8,128)} %fusion.23.term_ref), custom_call_target="tpu_custom_call" | custom-call | tf_op jit(solution)/shard_map/pallas_call | solution.py:441
  100.8 1.3 sub.31.start_ref
  102.1 16.8 %shard_map.176 = (f32[64,2048]{1,0:T(8,128)}, bf16[64,2048]{1,0:T(8,128)(2,1)S(1)}) custom-call(f32[64,2048]{1,0:T(8,128)S(1)} %sub.31.start_ref, f32[16,128,128]{2,1,0:T(8,128)S(1)} %copy-done.4, bf16[2048,2048]{1,0:T(8,128)(2,1)} %lower_ref.1), custom_call_target="tpu_custom_call" | custom-call | tf_op jit(solution)/shard_map/pallas_call | solution.py:288
  118.9 0.4 convolution_subtract_fusion.start_ref
  119.3 1.2 subtract_convert_fusion
  120.5 1.6 copy-done.2
  122.1 60.7 %shard_map.177 = (f32[64,256]{1,0:T(8,128)S(1)}, bf16[16,64,256]{2,1,0:T(8,128)(2,1)S(1)}) custom-call(f32[64,256]{1,0:T(8,128)S(1)} %convolution_subtract_fusion.start_ref, f32[256,256]{1,0:T(8,128)S(1)} %bitcast.96, bf16[16,256,256]{2,1,0:T(8,128)(2,1)S(1)} %bitcast.94, bf16[256,256]{1,0:T(8,128)(2,1)S(1)} %get-tuple-element.17.hi_ref, ...), custom_call_target="tpu_custom_call" | custom-call | tf_op jit(solution)/shard_map/pallas_call | solution.py:249
  182.9 0.5 fusion.9
  183.4 0.6 fusion.6
  184.0 0.6 copy-done.10
  184.6 1.1 fusion.46
  185.7 0.8 copy_bitcast_fusion
  186.5 0.1 fusion.35
  186.6 0.2 select_reduce_fusion
  186.8 0.3 fusion.13
  187.1 0.9 copy.65.coef_ref
  188.1 0.1 fusion.25
  188.2 0.7 copy.30.centre_ref
  188.9 12.4 %shard_map.178 = (bf16[16,2,64,128]{3,2,1,0:T(8,128)(2,1)}, f32[16,2,3,128]{3,2,1,0:T(4,128)}) custom-call(bf16[16,2,64,128]{3,2,1,0:T(8,128)(2,1)} %copy.65.coef_ref, f32[16,2,3,128]{3,2,1,0:T(4,128)} %copy.30.centre_ref), custom_call_target="tpu_custom_call" | custom-call | tf_op jit(solution)/shard_map/pallas_call | solution.py:498
  201.3 1.4 copy.31
  202.6 48.2 %shard_map.179 = f32[64,2048]{1,0:T(8,128)} custom-call(s32[16,32]{1,0:T(8,128)} %pattern_ref.1, bf16[32,64,128]{2,1,0:T(8,128)(2,1)} %bitcast.99, f32[32,3,128]{2,1,0:T(4,128)} %bitcast.101, f32[16,128,3]{2,1,0:T(8,128)} %bitcast.98), custom_call_target="tpu_custom_call" | custom-call | tf_op jit(solution)/shard_map/pallas_call | solution.py:348
  250.8 0.6 copy.69
  (29 shorter events, 0.1 us)
Async XLA Ops:
  0.6 3.7 %copy-start = (bf16[16,2,256,128]{3,2,1,0:T(8,128)(2,1)S(1)}, bf16[16,2,256,128]{3,2,1,0:T(8,128)(2,1)}, u32[]{:S(2)}) copy-start(bf16[16,2,256,128]{3,2,1,0:T(8,128)(2,1)} %param.19) | copy-start | bytes 6291460
  4.3 0.9 copy-start.6
  4.3 0.9 copy-start.14
  5.2 2.2 copy-start.3
  5.2 3.5 %copy-start.5 = (f32[64,256]{1,0:T(8,128)S(1)}, f32[64,256]{1,0:T(8,128)}, u32[]{:S(2)}) copy-start(f32[64,256]{1,0:T(8,128)} %rhs_ref.1) | copy-start | bytes 196612
  8.7 1.6 copy-start.1
  10.3 55.0 %copy-start.8 = (bf16[256,2048]{1,0:T(8,128)(2,1)S(1)}, bf16[256,2048]{1,0:T(8,128)(2,1)}, u32[]{:S(2)}) copy-start(bf16[256,2048]{1,0:T(8,128)(2,1)} %param.23) | copy-start | bytes 3145732
  65.3 36.8 %copy-start.4 = (f32[16,128,128]{2,1,0:T(8,128)S(1)}, f32[16,128,128]{2,1,0:T(8,128)}, u32[]{:S(2)}) copy-start(f32[16,128,128]{2,1,0:T(8,128)} %inv_ref.1) | copy-start | bytes 3145732
  102.0 16.8 %copy-start.9 = (bf16[256,2048]{1,0:T(8,128)(2,1)S(1)}, bf16[256,2048]{1,0:T(8,128)(2,1)}, u32[]{:S(2)}) copy-start(bf16[256,2048]{1,0:T(8,128)(2,1)} %param.23) | copy-start | bytes 3145732
  120.5 1.6 copy-start.2
  122.1 61.2 %copy-start.7 = (f32[16,64,128]{2,1,0:T(8,128)S(1)}, f32[16,64,128]{2,1,0:T(8,128)}, u32[]{:S(2)}) copy-start(f32[16,64,128]{2,1,0:T(8,128)} %copy-done.6) | copy-start | bytes 1572868
  183.4 1.2 copy-start.10
  184.6 1.9 copy-start.13
  184.6 3.5 %copy-start.12 = (f32[16,3,128]{2,0,1:T(8,128)S(1)}, f32[16,3,128]{2,0,1:T(8,128)}, u32[]{:S(2)}) copy-start(f32[16,3,128]{2,0,1:T(8,128)} %param.27) | copy-start | bytes 73732
  185.7 15.6 %copy-start.11 = (f32[1,3,2048]{2,0,1:T(1,128)S(1)}, f32[1,3,2048]{2,0,1:T(1,128)}, u32[]{:S(2)}) copy-start(f32[1,3,2048]{2,0,1:T(1,128)} %param.28) | copy-start | bytes 73732

commit v10 on v9

--- a/solution.py
+++ b/solution.py
@@ -100,7 +100,9 @@
         @pl.when(live)
         def _():
             _block_copy(halves, s, dest, send_sem.at[k], recv_sem, leaf).start()
-    for k in range(1, n):
+            if k == 1:
+                _block_copy(halves, s, dest, send_sem.at[k], recv_sem, leaf).wait_send()
+    for k in range(2, n):
         dest, live = dests(s, k)
         @pl.when(live)
         def _():

time: 254 us -> 256 us (level)
  no operation moved by 1% of the time
where the time goes in v10:
time: 256 us; the launch traced here: 253 us
  Pallas kernels  229 us (89%)
  matrix products  13.1 us (5%)
  local copies, waits for them, and re-layouts  8.41 us (3%)
    pallas_call x1, Pallas kernels, sep_solve(): pl.pallas_call(functools.partial(sep_backward_kernel, n), out_shape=(sol_...  61.1 us
    pallas_call x1, Pallas kernels, sep_solve(): pl.pallas_call(functools.partial(sep_forward_kernel, n), out_shape=sol_sh...  56.9 us
    pallas_call x1, Pallas kernels, evaluate_all(): pl.pallas_call(functools.partial(evaluate_kernel, slots), out_shape=jax.S...  48.4 us
    pallas_call x1, Pallas kernels, top_reduce(): pl.pallas_call(functools.partial(top_reduce_kernel, n, groups, span), out...  33.1 us
    pallas_call x1, Pallas kernels, top_solve(): pl.pallas_call(functools.partial(top_solve_kernel, nt, span), out_shape=(...  16.8 us
    pallas_call x1, Pallas kernels, exchange(): pl.pallas_call(functools.partial(exchange_kernel, n), out_shape=(jax.Shap...  13 us

profile of v10, /device:TPU:24, one launch (start us, length us, event | category | flops | bytes accessed | tf_op | source)
XLA Modules:
  0.0 253.4 jit_solution(256233539775865870)
XLA Ops:
  0.6 0.0 copy-start
  0.6 3.7 %fusion.7 = f32[16,64,128]{2,1,0:T(8,128)S(1)} fusion(f32[16,128,128]{2,1,0:T(8,128)} %param.18, f32[64,2048]{1,0:T(8,128)} %param.15), kind=kOutput, calls=%fused_computation.12 | convolution fusion | flops 201326592 | bytes 2097152 | tf_op jit(solution)/shard_map/nrs,nts->nrt/dot_general | solution.py:559
  4.3 0.9 fusion.11
  5.2 0.0 copy-start.3
  5.2 2.0 fusion.3
  7.3 0.2 copy.66.part_ref
  7.5 1.2 subtract_convert_fusion.1
  8.7 1.6 copy-done.1
  10.3 56.9 %shard_map.174 = f32[64,256]{1,0:T(8,128)S(1)} custom-call(f32[64,256]{1,0:T(8,128)S(1)} %copy-done.5, bf16[16,64,256]{2,1,0:T(8,128)(2,1)S(1)} %copy.66.part_ref, f32[256,256]{1,0:T(8,128)S(1)} %bitcast.95, bf16[16,256,256]{2,1,0:T(8,128)(2,1)S(1)} %bitcast.93, bf16[256,256]{1,0:T(8,128)(2,1)S(1)} %get-tuple-element.19.hi_ref, ...), custom_call_target="tpu_custom_call" | custom-call | tf_op jit(solution)/shard_map/pallas_call | solution.py:237
  67.3 1.1 fusion.23.term_ref
  68.4 33.1 %shard_map.175 = f32[64,2048]{1,0:T(8,128)} custom-call(f32[64,2048]{1,0:T(8,128)} %fusion.23.term_ref), custom_call_target="tpu_custom_call" | custom-call | tf_op jit(solution)/shard_map/pallas_call | solution.py:443
  101.5 1.3 sub.31.start_ref
  102.8 16.8 %shard_map.176 = (f32[64,2048]{1,0:T(8,128)}, bf16[64,2048]{1,0:T(8,128)(2,1)S(1)}) custom-call(f32[64,2048]{1,0:T(8,128)S(1)} %sub.31.start_ref, f32[16,128,128]{2,1,0:T(8,128)S(1)} %copy-done.4, bf16[2048,2048]{1,0:T(8,128)(2,1)} %lower_ref.1), custom_call_target="tpu_custom_call" | custom-call | tf_op jit(solution)/shard_map/pallas_call | solution.py:290
  119.6 0.4 convolution_subtract_fusion.start_ref
  120.0 1.2 subtract_convert_fusion
  121.3 1.6 copy-done.2
  122.9 61.1 %shard_map.177 = (f32[64,256]{1,0:T(8,128)S(1)}, bf16[16,64,256]{2,1,0:T(8,128)(2,1)S(1)}) custom-call(f32[64,256]{1,0:T(8,128)S(1)} %convolution_subtract_fusion.start_ref, f32[256,256]{1,0:T(8,128)S(1)} %bitcast.96, bf16[16,256,256]{2,1,0:T(8,128)(2,1)S(1)} %bitcast.94, bf16[256,256]{1,0:T(8,128)(2,1)S(1)} %get-tuple-element.17.hi_ref, ...), custom_call_target="tpu_custom_call" | custom-call | tf_op jit(solution)/shard_map/pallas_call | solution.py:251
  183.9 0.5 fusion.9
  184.5 0.6 fusion.6
  185.1 0.6 copy-done.10
  185.7 1.1 fusion.46
  186.7 0.8 copy_bitcast_fusion
  187.6 0.1 fusion.35
  187.7 0.2 select_reduce_fusion
  187.9 0.3 fusion.13
  188.2 0.9 copy.65.coef_ref
  189.1 0.1 fusion.25
  189.3 0.7 copy.30.centre_ref
  189.9 13.0 %shard_map.178 = (bf16[16,2,64,128]{3,2,1,0:T(8,128)(2,1)}, f32[16,2,3,128]{3,2,1,0:T(4,128)}) custom-call(bf16[16,2,64,128]{3,2,1,0:T(8,128)(2,1)} %copy.65.coef_ref, f32[16,2,3,128]{3,2,1,0:T(4,128)} %copy.30.centre_ref), custom_call_target="tpu_custom_call" | custom-call | tf_op jit(solution)/shard_map/pallas_call | solution.py:500
  203.0 1.4 copy.31
  204.3 48.4 %shard_map.179 = f32[64,2048]{1,0:T(8,128)} custom-call(s32[16,32]{1,0:T(8,128)} %pattern_ref.1, bf16[32,64,128]{2,1,0:T(8,128)(2,1)} %bitcast.99, f32[32,3,128]{2,1,0:T(4,128)} %bitcast.101, f32[16,128,3]{2,1,0:T(8,128)} %bitcast.98), custom_call_target="tpu_custom_call" | custom-call | tf_op jit(solution)/shard_map/pallas_call | solution.py:350
  252.7 0.6 copy.69
  (29 shorter events, 0.1 us)
Async XLA Ops:
  0.6 3.7 %copy-start = (bf16[16,2,256,128]{3,2,1,0:T(8,128)(2,1)S(1)}, bf16[16,2,256,128]{3,2,1,0:T(8,128)(2,1)}, u32[]{:S(2)}) copy-start(bf16[16,2,256,128]{3,2,1,0:T(8,128)(2,1)} %param.19) | copy-start | bytes 6291460
  4.3 0.9 copy-start.6
  4.3 0.9 copy-start.14
  5.2 2.2 copy-start.3
  5.2 3.5 %copy-start.5 = (f32[64,256]{1,0:T(8,128)S(1)}, f32[64,256]{1,0:T(8,128)}, u32[]{:S(2)}) copy-start(f32[64,256]{1,0:T(8,128)} %rhs_ref.1) | copy-start | bytes 196612
  8.7 1.6 copy-start.1
  10.3 56.9 %copy-start.8 = (bf16[256,2048]{1,0:T(8,128)(2,1)S(1)}, bf16[256,2048]{1,0:T(8,128)(2,1)}, u32[]{:S(2)}) copy-start(bf16[256,2048]{1,0:T(8,128)(2,1)} %param.23) | copy-start | bytes 3145732
  67.2 35.5 %copy-start.4 = (f32[16,128,128]{2,1,0:T(8,128)S(1)}, f32[16,128,128]{2,1,0:T(8,128)}, u32[]{:S(2)}) copy-start(f32[16,128,128]{2,1,0:T(8,128)} %inv_ref.1) | copy-start | bytes 3145732
  102.8 16.8 %copy-start.9 = (bf16[256,2048]{1,0:T(8,128)(2,1)S(1)}, bf16[256,2048]{1,0:T(8,128)(2,1)}, u32[]{:S(2)}) copy-start(bf16[256,2048]{1,0:T(8,128)(2,1)} %param.23) | copy-start | bytes 3145732
  121.3 1.6 copy-start.2
  122.9 61.6 %copy-start.7 = (f32[16,64,128]{2,1,0:T(8,128)S(1)}, f32[16,64,128]{2,1,0:T(8,128)}, u32[]{:S(2)}) copy-start(f32[16,64,128]{2,1,0:T(8,128)} %copy-done.6) | copy-start | bytes 1572868
  184.4 1.2 copy-start.10
  185.7 1.9 copy-start.13
  185.7 3.5 %copy-start.12 = (f32[16,3,128]{2,0,1:T(8,128)S(1)}, f32[16,3,128]{2,0,1:T(8,128)}, u32[]{:S(2)}) copy-start(f32[16,3,128]{2,0,1:T(8,128)} %param.27) | copy-start | bytes 73732
  186.7 16.2 %copy-start.11 = (f32[1,3,2048]{2,0,1:T(1,128)S(1)}, f32[1,3,2048]{2,0,1:T(1,128)}, u32[]{:S(2)}) copy-start(f32[1,3,2048]{2,0,1:T(1,128)} %param.28) | copy-start | bytes 73732

commit v11 on v10

--- a/solution.py
+++ b/solution.py
@@ -181,7 +181,7 @@
     leaf = lax.axis_index("leaf")
     _greet_group(n, leaf, me)
     resid[...] = start_ref[...]
-    dests = lambda s, k: (lax.rem(s - k + n, n), True)
+    dests = lambda s, k: (s - k, s - k >= 0)
 
     @pl.when(me == n - 1)
     def _():
@@ -194,7 +194,7 @@
     def step(s, carry):
         q = n - 1 - s
 
-        @pl.when(me != q)
+        @pl.when(me < q)
         def _():
             _block_copy(halves, q, q, send_sem.at[0], recv_sem, leaf).wait_recv()
 
@@ -214,9 +214,18 @@
         return carry
 
     lax.fori_loop(0, n - 1, step, 0)
-    @pl.when(me != 0)
-    def _():
-        _block_copy(halves, 0, 0, send_sem.at[0], recv_sem, leaf).wait_recv()
+    for k in range(1, n):
+        @pl.when(me + k < n)
+        def _():
+            _block_copy(halves, me, me + k, send_sem.at[k], recv_sem, leaf).start()
+    for q in range(n):
+        @pl.when(q < me)
+        def _():
+            _block_copy(halves, q, q, send_sem.at[0], recv_sem, leaf).wait_recv()
+    for k in range(1, n):
+        @pl.when(me + k < n)
+        def _():
+            _block_copy(halves, me, me + k, send_sem.at[k], recv_sem, leaf).wait_send()
     table_ref[...] = halves[...]
 
 

time: 256 us -> 252 us (0.984)
  Pallas kernels: 229 us -> 224 us
    pallas_call x1, Pallas kernels: 61.1 us -> 57.4 us  [sep_solve(): pl.pallas_call(functools.partial(sep_backward_kernel, n), out_shape=(sol_...]
    pallas_call x1, Pallas kernels: 48.4 us -> 45.5 us  [evaluate_all(): pl.pallas_call(functools.partial(evaluate_kernel, slots), out_shape=jax.S...]
where the time goes in v11:
time: 252 us; the launch traced here: 248 us
  Pallas kernels  224 us (89%)
  matrix products  13.2 us (5%)
  local copies, waits for them, and re-layouts  8.41 us (3%)
    pallas_call x1, Pallas kernels, sep_solve(): pl.pallas_call(functools.partial(sep_backward_kernel, n), out_shape=(sol_...  57.4 us
    pallas_call x1, Pallas kernels, sep_solve(): pl.pallas_call(functools.partial(sep_forward_kernel, n), out_shape=sol_sh...  56.9 us
    pallas_call x1, Pallas kernels, evaluate_all(): pl.pallas_call(functools.partial(evaluate_kernel, slots), out_shape=jax.S...  45.5 us
    pallas_call x1, Pallas kernels, top_reduce(): pl.pallas_call(functools.partial(top_reduce_kernel, n, groups, span), out...  33.1 us
    pallas_call x1, Pallas kernels, top_solve(): pl.pallas_call(functools.partial(top_solve_kernel, nt, span), out_shape=(...  16.8 us
    pallas_call x1, Pallas kernels, exchange(): pl.pallas_call(functools.partial(exchange_kernel, n), out_shape=(jax.Shap...  14.6 us

profile of v11, /device:TPU:24, one launch (start us, length us, event | category | flops | bytes accessed | tf_op | source)
XLA Modules:
  0.0 248.3 jit_solution(12726974060976422164)
XLA Ops:
  0.6 0.0 copy-start
  0.6 3.7 %fusion.7 = f32[16,64,128]{2,1,0:T(8,128)S(1)} fusion(f32[16,128,128]{2,1,0:T(8,128)} %param.18, f32[64,2048]{1,0:T(8,128)} %param.15), kind=kOutput, calls=%fused_computation.12 | convolution fusion | flops 201326592 | bytes 2097152 | tf_op jit(solution)/shard_map/nrs,nts->nrt/dot_general | solution.py:568
  4.3 0.9 fusion.11
  5.2 0.0 copy-start.3
  5.2 2.0 fusion.3
  7.3 0.2 copy.66.part_ref
  7.5 1.2 subtract_convert_fusion.1
  8.7 1.6 copy-done.1
  10.3 56.9 %shard_map.174 = f32[64,256]{1,0:T(8,128)S(1)} custom-call(f32[64,256]{1,0:T(8,128)S(1)} %copy-done.5, bf16[16,64,256]{2,1,0:T(8,128)(2,1)S(1)} %copy.66.part_ref, f32[256,256]{1,0:T(8,128)S(1)} %bitcast.95, bf16[16,256,256]{2,1,0:T(8,128)(2,1)S(1)} %bitcast.93, bf16[256,256]{1,0:T(8,128)(2,1)S(1)} %get-tuple-element.19.hi_ref, ...), custom_call_target="tpu_custom_call" | custom-call | tf_op jit(solution)/shard_map/pallas_call | solution.py:246
  67.3 1.1 fusion.23.term_ref
  68.4 33.1 %shard_map.175 = f32[64,2048]{1,0:T(8,128)} custom-call(f32[64,2048]{1,0:T(8,128)} %fusion.23.term_ref), custom_call_target="tpu_custom_call" | custom-call | tf_op jit(solution)/shard_map/pallas_call | solution.py:452
  101.5 1.3 sub.31.start_ref
  102.8 16.8 %shard_map.176 = (f32[64,2048]{1,0:T(8,128)}, bf16[64,2048]{1,0:T(8,128)(2,1)S(1)}) custom-call(f32[64,2048]{1,0:T(8,128)S(1)} %sub.31.start_ref, f32[16,128,128]{2,1,0:T(8,128)S(1)} %copy-done.4, bf16[2048,2048]{1,0:T(8,128)(2,1)} %lower_ref.1), custom_call_target="tpu_custom_call" | custom-call | tf_op jit(solution)/shard_map/pallas_call | solution.py:299
  119.6 0.4 convolution_subtract_fusion.start_ref
  120.0 1.2 subtract_convert_fusion
  121.3 1.6 copy-done.2
  122.9 57.4 %shard_map.177 = (f32[64,256]{1,0:T(8,128)S(1)}, bf16[16,64,256]{2,1,0:T(8,128)(2,1)S(1)}) custom-call(f32[64,256]{1,0:T(8,128)S(1)} %convolution_subtract_fusion.start_ref, f32[256,256]{1,0:T(8,128)S(1)} %bitcast.96, bf16[16,256,256]{2,1,0:T(8,128)(2,1)S(1)} %bitcast.94, bf16[256,256]{1,0:T(8,128)(2,1)S(1)} %get-tuple-element.17.hi_ref, ...), custom_call_target="tpu_custom_call" | custom-call | tf_op jit(solution)/shard_map/pallas_call | solution.py:260
  180.2 0.5 fusion.9
  180.8 0.6 fusion.6
  181.4 0.6 copy-done.10
  182.0 1.1 fusion.46
  183.1 0.8 copy_bitcast_fusion
  183.9 0.1 fusion.35
  184.0 0.2 select_reduce_fusion
  184.2 0.3 fusion.13
  184.5 0.9 copy.65.coef_ref
  185.4 0.1 fusion.25
  185.6 0.7 copy.30.centre_ref
  186.2 14.6 %shard_map.178 = (bf16[16,2,64,128]{3,2,1,0:T(8,128)(2,1)}, f32[16,2,3,128]{3,2,1,0:T(4,128)}) custom-call(bf16[16,2,64,128]{3,2,1,0:T(8,128)(2,1)} %copy.65.coef_ref, f32[16,2,3,128]{3,2,1,0:T(4,128)} %copy.30.centre_ref), custom_call_target="tpu_custom_call" | custom-call | tf_op jit(solution)/shard_map/pallas_call | solution.py:509
  200.8 1.4 copy.31
  202.2 45.5 %shard_map.179 = f32[64,2048]{1,0:T(8,128)} custom-call(s32[16,32]{1,0:T(8,128)} %pattern_ref.1, bf16[32,64,128]{2,1,0:T(8,128)(2,1)} %bitcast.99, f32[32,3,128]{2,1,0:T(4,128)} %bitcast.101, f32[16,128,3]{2,1,0:T(8,128)} %bitcast.98), custom_call_target="tpu_custom_call" | custom-call | tf_op jit(solution)/shard_map/pallas_call | solution.py:359
  247.7 0.6 copy.69
  (29 shorter events, 0.1 us)
Async XLA Ops:
  0.6 3.7 %copy-start = (bf16[16,2,256,128]{3,2,1,0:T(8,128)(2,1)S(1)}, bf16[16,2,256,128]{3,2,1,0:T(8,128)(2,1)}, u32[]{:S(2)}) copy-start(bf16[16,2,256,128]{3,2,1,0:T(8,128)(2,1)} %param.19) | copy-start | bytes 6291460
  4.3 0.9 copy-start.6
  4.3 0.9 copy-start.14
  5.2 2.2 copy-start.3
  5.2 3.5 %copy-start.5 = (f32[64,256]{1,0:T(8,128)S(1)}, f32[64,256]{1,0:T(8,128)}, u32[]{:S(2)}) copy-start(f32[64,256]{1,0:T(8,128)} %rhs_ref.1) | copy-start | bytes 196612
  8.7 1.6 copy-start.1
  10.3 56.9 %copy-start.8 = (bf16[256,2048]{1,0:T(8,128)(2,1)S(1)}, bf16[256,2048]{1,0:T(8,128)(2,1)}, u32[]{:S(2)}) copy-start(bf16[256,2048]{1,0:T(8,128)(2,1)} %param.23) | copy-start | bytes 3145732
  67.2 35.5 %copy-start.4 = (f32[16,128,128]{2,1,0:T(8,128)S(1)}, f32[16,128,128]{2,1,0:T(8,128)}, u32[]{:S(2)}) copy-start(f32[16,128,128]{2,1,0:T(8,128)} %inv_ref.1) | copy-start | bytes 3145732
  102.8 16.8 %copy-start.9 = (bf16[256,2048]{1,0:T(8,128)(2,1)S(1)}, bf16[256,2048]{1,0:T(8,128)(2,1)}, u32[]{:S(2)}) copy-start(bf16[256,2048]{1,0:T(8,128)(2,1)} %param.23) | copy-start | bytes 3145732
  121.3 1.6 copy-start.2
  122.9 57.9 %copy-start.7 = (f32[16,64,128]{2,1,0:T(8,128)S(1)}, f32[16,64,128]{2,1,0:T(8,128)}, u32[]{:S(2)}) copy-start(f32[16,64,128]{2,1,0:T(8,128)} %copy-done.6) | copy-start | bytes 1572868
  180.7 1.2 copy-start.10
  182.0 1.9 copy-start.13
  182.0 3.5 %copy-start.12 = (f32[16,3,128]{2,0,1:T(8,128)S(1)}, f32[16,3,128]{2,0,1:T(8,128)}, u32[]{:S(2)}) copy-start(f32[16,3,128]{2,0,1:T(8,128)} %param.27) | copy-start | bytes 73732
  183.0 17.8 %copy-start.11 = (f32[1,3,2048]{2,0,1:T(1,128)S(1)}, f32[1,3,2048]{2,0,1:T(1,128)}, u32[]{:S(2)}) copy-start(f32[1,3,2048]{2,0,1:T(1,128)} %param.28) | copy-start | bytes 73732

commit v12 on v11

--- a/solution.py
+++ b/solution.py
@@ -312,25 +312,18 @@
     )(top_start, top_inverse, top_lower)
 
 
-def evaluate_kernel(slots, pattern_ref, coef_ref, centre_ref, column_ref, out_ref, acc, spread):
+def evaluate_kernel(slots, pattern_ref, coef_ref, centre_ref, point_ref, out_ref, acc):
     m = pl.program_id(0)
     acc[...] = jnp.zeros_like(acc)
-    column = column_ref[0]
-    width = centre_ref.shape[2]
-    for comp in range(3):
-        spread[comp] = jnp.broadcast_to(column[:, comp : comp + 1], (column.shape[0], width))
+    points_here = point_ref[0]
 
     def one_slot(s, carry):
         @pl.when(pattern_ref[m, s] != 0)
         def _():
-            centre = centre_ref[s]
-            dist = None
-            for comp in range(3):
-                delta = centre[comp : comp + 1, :] - spread[comp]
-                dist = delta * delta if dist is None else dist + delta * delta
+            dist = _nn_exact(centre_ref[s], points_here)
             weight = jnp.maximum(1.0 - dist * (1.0 / support_sq), 0.0)
             kernel = (weight * weight * weight).astype(jnp.bfloat16)
-            acc[...] += _nt(coef_ref[s], kernel)
+            acc[...] += _nn(coef_ref[s], kernel)
 
         return carry
 
@@ -338,9 +331,9 @@
     out_ref[...] = acc[...]
 
 
-def evaluate_all(coef_all, centre_all, point_columns, pattern):
+def evaluate_all(coef_all, centre_all, point_rows, pattern):
     slots, rows, span = coef_all.shape
-    blocks = point_columns.shape[0]
+    blocks = point_rows.shape[0]
     full = lambda shape: pl.BlockSpec(shape, lambda m, pat: (0,) * len(shape))
     grid_spec = pltpu.PrefetchScalarGridSpec(
         num_scalar_prefetch=1,
@@ -348,19 +341,25 @@
         in_specs=[
             full(coef_all.shape),
             full(centre_all.shape),
-            pl.BlockSpec((1, span, point_columns.shape[2]), lambda m, pat: (m, 0, 0)),
+            pl.BlockSpec((1,) + point_rows.shape[1:], lambda m, pat: (m, 0, 0)),
         ],
         out_specs=pl.BlockSpec((rows, span), lambda m, pat: (0, m)),
-        scratch_shapes=[
-            pltpu.VMEM((rows, span), jnp.float32),
-            pltpu.VMEM((3, span, centre_all.shape[2]), jnp.float32),
-        ],
+        scratch_shapes=[pltpu.VMEM((rows, span), jnp.float32)],
     )
     return pl.pallas_call(
         functools.partial(evaluate_kernel, slots),
         out_shape=jax.ShapeDtypeStruct((rows, blocks * span), jnp.float32),
         grid_spec=grid_spec,
-    )(pattern, coef_all, centre_all, point_columns)
+    )(pattern, coef_all, centre_all, point_rows)
+
+
+def augmented(coords, scale, axis):
+    squares = jnp.sum(coords * coords, axis=axis, keepdims=True)
+    ones = jnp.ones_like(squares)
+    zeros = jnp.zeros_like(jnp.concatenate([squares] * 3, axis=axis))
+    if scale == 1:
+        return jnp.concatenate([coords, squares, ones, zeros], axis=axis)
+    return jnp.concatenate([coords * scale, ones, squares, zeros], axis=axis)
 
 
 def top_reduce_kernel(n, groups, span, term_ref, total_ref, parts_a, parts_b, gathered, local_sem, send_a, recv_a, send_b, recv_b, send_c, recv_c):
@@ -624,8 +623,9 @@
     coef_all = received.reshape(slot_total, snapshots, span)
     centre_all = recv_centre.reshape(slot_total, 3, span)
     point_blocks = eval_pattern.shape[0]
-    point_columns = points[0].T.reshape(point_blocks, span, points.shape[1])
-    values = evaluate_all(coef_all, centre_all, point_columns, eval_pattern)
+    centre_rows = augmented(jnp.swapaxes(centre_all, 1, 2), 1, 2)
+    point_rows = augmented(points[0].reshape(3, point_blocks, span).transpose(1, 0, 2), -2.0, 1)
+    values = evaluate_all(coef_all, centre_rows, point_rows, eval_pattern)
     return (coef_leaf, coef_sep, coef_top, values)
 
 

time: 252 us -> 305 us (1.21); the launches traced: 248 us -> 305 us
  Pallas kernels: 224 us -> 270 us
  other arithmetic: 1.57 us -> 8.69 us
  local copies, waits for them, and re-layouts: 8.41 us -> 12.1 us
    pallas_call x1, Pallas kernels: 45.5 us -> 91.3 us  [evaluate_all(): pl.pallas_call(functools.partial(evaluate_kernel, slots), out_shape=jax.S...]
    concatenate x0 -> x2, other arithmetic: none -> 4.88 us  [the longest x1 4.17 us: augmented(): return jnp.concatenate([coords, squares, ones, zeros], axis=axis)]
where the time goes in v12:
time: 305 us
  Pallas kernels  270 us (89%)
  matrix products  13.2 us (4%)
  local copies, waits for them, and re-layouts  12.1 us (4%)
  other arithmetic  8.69 us (3%)
    pallas_call x1, Pallas kernels, evaluate_all(): pl.pallas_call(functools.partial(evaluate_kernel, slots), out_shape=jax.S...  91.3 us
    pallas_call x1, Pallas kernels, sep_solve(): pl.pallas_call(functools.partial(sep_backward_kernel, n), out_shape=(sol_...  57.4 us
    pallas_call x1, Pallas kernels, sep_solve(): pl.pallas_call(functools.partial(sep_forward_kernel, n), out_shape=sol_sh...  56.9 us
    pallas_call x1, Pallas kernels, top_reduce(): pl.pallas_call(functools.partial(top_reduce_kernel, n, groups, span), out...  33.1 us
    pallas_call x1, Pallas kernels, top_solve(): pl.pallas_call(functools.partial(top_solve_kernel, nt, span), out_shape=(...  16.8 us
    pallas_call x1, Pallas kernels, exchange(): pl.pallas_call(functools.partial(exchange_kernel, n), out_shape=(jax.Shap...  14.6 us

profile of v12, /device:TPU:24, one launch (start us, length us, event | category | flops | bytes accessed | tf_op | source)
XLA Modules:
  0.0 304.9 jit_solution(3519096168527473357)
XLA Ops:
  0.6 3.7 %fusion.7 = f32[16,64,128]{2,1,0:T(8,128)S(1)} fusion(f32[16,128,128]{2,1,0:T(8,128)} %param.18, f32[64,2048]{1,0:T(8,128)} %param.15), kind=kOutput, calls=%fused_computation.15 | convolution fusion | flops 201326592 | bytes 2097152 | tf_op jit(solution)/shard_map/nrs,nts->nrt/dot_general | solution.py:567
  4.3 0.9 convolution_bitcast_fusion
  5.2 2.0 fusion.2
  7.3 0.2 copy.92.part_ref
  7.5 1.2 subtract_convert_fusion.1
  8.7 1.6 copy-done.1
  10.3 56.9 %shard_map.174 = f32[64,256]{1,0:T(8,128)S(1)} custom-call(f32[64,256]{1,0:T(8,128)S(1)} %copy-done.5, bf16[16,64,256]{2,1,0:T(8,128)(2,1)S(1)} %copy.92.part_ref, f32[256,256]{1,0:T(8,128)S(1)} %bitcast.99, bf16[16,256,256]{2,1,0:T(8,128)(2,1)S(1)} %bitcast.97, bf16[256,256]{1,0:T(8,128)(2,1)S(1)} %get-tuple-element.19.hi_ref, ...), custom_call_target="tpu_custom_call" | custom-call | tf_op jit(solution)/shard_map/pallas_call | solution.py:246
  67.3 1.1 fusion.22.term_ref
  68.4 33.1 %shard_map.175 = f32[64,2048]{1,0:T(8,128)} custom-call(f32[64,2048]{1,0:T(8,128)} %fusion.22.term_ref), custom_call_target="tpu_custom_call" | custom-call | tf_op jit(solution)/shard_map/pallas_call | solution.py:451
  101.5 1.3 sub.31.start_ref
  102.8 16.8 %shard_map.176 = (f32[64,2048]{1,0:T(8,128)}, bf16[64,2048]{1,0:T(8,128)(2,1)S(1)}) custom-call(f32[64,2048]{1,0:T(8,128)S(1)} %sub.31.start_ref, f32[16,128,128]{2,1,0:T(8,128)S(1)} %copy-done.4, bf16[2048,2048]{1,0:T(8,128)(2,1)} %lower_ref.1), custom_call_target="tpu_custom_call" | custom-call | tf_op jit(solution)/shard_map/pallas_call | solution.py:299
  119.6 0.4 convolution_subtract_fusion.start_ref
  120.0 1.2 subtract_convert_fusion
  121.3 1.6 copy-done.2
  122.9 57.4 %shard_map.177 = (f32[64,256]{1,0:T(8,128)S(1)}, bf16[16,64,256]{2,1,0:T(8,128)(2,1)S(1)}) custom-call(f32[64,256]{1,0:T(8,128)S(1)} %convolution_subtract_fusion.start_ref, f32[256,256]{1,0:T(8,128)S(1)} %bitcast.100, bf16[16,256,256]{2,1,0:T(8,128)(2,1)S(1)} %bitcast.98, bf16[256,256]{1,0:T(8,128)(2,1)S(1)} %get-tuple-element.17.hi_ref, ...), custom_call_target="tpu_custom_call" | custom-call | tf_op jit(solution)/shard_map/pallas_call | solution.py:260
  180.2 0.5 convolution_convert_fusion
  180.8 0.6 fusion.5
  181.4 0.6 copy-done.10
  182.0 1.1 fusion.45
  183.1 0.8 copy_bitcast_fusion
  184.0 0.2 select_reduce_fusion
  184.2 0.3 fusion.12
  184.5 0.9 copy.91.coef_ref
  185.6 0.7 copy.56.centre_ref
  186.3 14.6 %shard_map.178 = (bf16[16,2,64,128]{3,2,1,0:T(8,128)(2,1)}, f32[16,2,3,128]{3,2,1,0:T(4,128)}) custom-call(bf16[16,2,64,128]{3,2,1,0:T(8,128)(2,1)} %copy.91.coef_ref, f32[16,2,3,128]{3,2,1,0:T(4,128)} %copy.56.centre_ref), custom_call_target="tpu_custom_call" | custom-call | tf_op jit(solution)/shard_map/pallas_call | solution.py:508
  200.8 2.8 copy.57
  203.6 2.2 multiply_reduce_fusion
  205.8 2.0 copy.58
  208.0 4.2 %maximum_maximum_fusion.centre_ref = f32[32,128,8]{2,1,0:T(8,128)} fusion(f32[32,128,1]{2,1,0:T(8,128)} %copy.58, f32[32,128,3]{2,1,0:T(8,128)} %bitcast.101, f32[8]{0:T(128)S(1)} %pad.7.clone, f32[8]{0:T(128)S(1)} %pad.6.clone), kind=kLoop, calls=%fused_computation | loop fusion | flops 98304 | bytes 196672 | tf_op jit(solution)/shard_map/concatenate | solution.py:361
  212.3 0.7 maximum_maximum_fusion.1.point_ref
  213.0 91.3 %shard_map.179 = f32[64,2048]{1,0:T(8,128)} custom-call(s32[16,32]{1,0:T(8,128)} %pattern_ref.1, bf16[32,64,128]{2,1,0:T(8,128)(2,1)} %bitcast.102, f32[32,128,8]{2,1,0:T(8,128)} %maximum_maximum_fusion.centre_ref, f32[16,8,128]{2,1,0:T(8,128)} %maximum_maximum_fusion.1.point_ref), custom_call_target="tpu_custom_call" | custom-call | tf_op jit(solution)/shard_map/pallas_call | solution.py:349
  304.3 0.6 copy.95
  (38 shorter events, 0.6 us)
Async XLA Ops:
  0.6 3.7 %copy-start = (bf16[16,2,256,128]{3,2,1,0:T(8,128)(2,1)S(1)}, bf16[16,2,256,128]{3,2,1,0:T(8,128)(2,1)}, u32[]{:S(2)}) copy-start(bf16[16,2,256,128]{3,2,1,0:T(8,128)(2,1)} %param.19) | copy-start | bytes 6291460
  4.3 0.9 copy-start.6
  4.3 0.9 copy-start.14
  5.2 2.2 copy-start.3
  5.2 3.5 %copy-start.5 = (f32[64,256]{1,0:T(8,128)S(1)}, f32[64,256]{1,0:T(8,128)}, u32[]{:S(2)}) copy-start(f32[64,256]{1,0:T(8,128)} %rhs_ref.1) | copy-start | bytes 196612
  8.7 1.6 copy-start.1
  10.3 56.9 %copy-start.8 = (bf16[256,2048]{1,0:T(8,128)(2,1)S(1)}, bf16[256,2048]{1,0:T(8,128)(2,1)}, u32[]{:S(2)}) copy-start(bf16[256,2048]{1,0:T(8,128)(2,1)} %param.23) | copy-start | bytes 3145732
  67.3 35.5 %copy-start.4 = (f32[16,128,128]{2,1,0:T(8,128)S(1)}, f32[16,128,128]{2,1,0:T(8,128)}, u32[]{:S(2)}) copy-start(f32[16,128,128]{2,1,0:T(8,128)} %inv_ref.1) | copy-start | bytes 3145732
  102.8 16.8 %copy-start.9 = (bf16[256,2048]{1,0:T(8,128)(2,1)S(1)}, bf16[256,2048]{1,0:T(8,128)(2,1)}, u32[]{:S(2)}) copy-start(bf16[256,2048]{1,0:T(8,128)(2,1)} %param.23) | copy-start | bytes 3145732
  121.3 1.6 copy-start.2
  122.9 57.9 %copy-start.7 = (f32[16,64,128]{2,1,0:T(8,128)S(1)}, f32[16,64,128]{2,1,0:T(8,128)}, u32[]{:S(2)}) copy-start(f32[16,64,128]{2,1,0:T(8,128)} %copy-done.6) | copy-start | bytes 1572868
  180.8 1.2 copy-start.10
  182.0 1.9 copy-start.13
  182.0 3.4 %copy-start.12 = (f32[16,3,128]{2,0,1:T(8,128)S(1)}, f32[16,3,128]{2,0,1:T(8,128)}, u32[]{:S(2)}) copy-start(f32[16,3,128]{2,0,1:T(8,128)} %param.27) | copy-start | bytes 73732
  208.0 4.2 %copy-start.11 = (f32[1,3,2048]{2,0,1:T(1,128)S(1)}, f32[1,3,2048]{2,0,1:T(1,128)}, u32[]{:S(2)}) copy-start(f32[1,3,2048]{2,0,1:T(1,128)} %param.28) | copy-start | bytes 73732

commit v13 on v11

--- a/solution.py
+++ b/solution.py
@@ -625,7 +625,9 @@
     centre_all = recv_centre.reshape(slot_total, 3, span)
     point_blocks = eval_pattern.shape[0]
     point_columns = points[0].T.reshape(point_blocks, span, points.shape[1])
-    values = evaluate_all(coef_all, centre_all, point_columns, eval_pattern)
+    filled = jnp.any(coef_all != 0, axis=(1, 2))
+    flags = ((eval_pattern != 0) & filled[None, :]).astype(jnp.int32)
+    values = evaluate_all(coef_all, centre_all, point_columns, flags)
     return (coef_leaf, coef_sep, coef_top, values)
 
 

time: 252 us -> 253 us (level)
  the two profiles are of different devices: /device:TPU:24 before, /device:TPU:122 now
where the time goes in v13:
time: 253 us; the launch traced here: 252 us
  Pallas kernels  225 us (89%)
  matrix products  13.1 us (5%)
  local copies, waits for them, and re-layouts  8.51 us (3%)
  other arithmetic  3.88 us (2%)
    pallas_call x1, Pallas kernels, sep_solve(): pl.pallas_call(functools.partial(sep_forward_kernel, n), out_shape=sol_sh...  61 us
    pallas_call x1, Pallas kernels, sep_solve(): pl.pallas_call(functools.partial(sep_backward_kernel, n), out_shape=(sol_...  59.4 us
    pallas_call x1, Pallas kernels, evaluate_all(): pl.pallas_call(functools.partial(evaluate_kernel, slots), out_shape=jax.S...  48.9 us
    pallas_call x1, Pallas kernels, top_reduce(): pl.pallas_call(functools.partial(top_reduce_kernel, n, groups, span), out...  25.2 us
    pallas_call x1, Pallas kernels, top_solve(): pl.pallas_call(functools.partial(top_solve_kernel, nt, span), out_shape=(...  16.8 us
    pallas_call x1, Pallas kernels, exchange(): pl.pallas_call(functools.partial(exchange_kernel, n), out_shape=(jax.Shap...  14.2 us

profile of v13, /device:TPU:122, one launch (start us, length us, event | category | flops | bytes accessed | tf_op | source)
XLA Modules:
  0.0 252.0 jit_solution(16500563148837453841)
XLA Ops:
  0.6 3.7 %fusion.7 = f32[16,64,128]{2,1,0:T(8,128)S(1)} fusion(f32[16,128,128]{2,1,0:T(8,128)} %param.18, f32[64,2048]{1,0:T(8,128)} %param.15), kind=kOutput, calls=%fused_computation.13 | convolution fusion | flops 201326592 | bytes 2097152 | tf_op jit(solution)/shard_map/nrs,nts->nrt/dot_general | solution.py:568
  4.4 0.8 fusion.11
  5.2 2.0 fusion.3
  7.3 0.2 copy.66.part_ref
  7.5 1.2 subtract_convert_fusion.1
  8.7 1.6 copy-done.1
  10.3 61.0 %shard_map.174 = f32[64,256]{1,0:T(8,128)S(1)} custom-call(f32[64,256]{1,0:T(8,128)S(1)} %copy-done.5, bf16[16,64,256]{2,1,0:T(8,128)(2,1)S(1)} %copy.66.part_ref, f32[256,256]{1,0:T(8,128)S(1)} %bitcast.95, bf16[16,256,256]{2,1,0:T(8,128)(2,1)S(1)} %bitcast.93, bf16[256,256]{1,0:T(8,128)(2,1)S(1)} %get-tuple-element.19.hi_ref, ...), custom_call_target="tpu_custom_call" | custom-call | tf_op jit(solution)/shard_map/pallas_call | solution.py:246
  71.4 1.1 fusion.23.term_ref
  72.5 25.2 %shard_map.175 = f32[64,2048]{1,0:T(8,128)} custom-call(f32[64,2048]{1,0:T(8,128)} %fusion.23.term_ref), custom_call_target="tpu_custom_call" | custom-call | tf_op jit(solution)/shard_map/pallas_call | solution.py:452
  97.7 1.3 sub.31.start_ref
  99.0 16.8 %shard_map.176 = (f32[64,2048]{1,0:T(8,128)}, bf16[64,2048]{1,0:T(8,128)(2,1)S(1)}) custom-call(f32[64,2048]{1,0:T(8,128)S(1)} %sub.31.start_ref, f32[16,128,128]{2,1,0:T(8,128)S(1)} %copy-done.4, bf16[2048,2048]{1,0:T(8,128)(2,1)} %lower_ref.1), custom_call_target="tpu_custom_call" | custom-call | tf_op jit(solution)/shard_map/pallas_call | solution.py:299
  115.8 0.4 convolution_subtract_fusion.start_ref
  116.3 1.2 subtract_convert_fusion
  117.5 1.6 copy-done.2
  119.1 59.4 %shard_map.177 = (f32[64,256]{1,0:T(8,128)S(1)}, bf16[16,64,256]{2,1,0:T(8,128)(2,1)S(1)}) custom-call(f32[64,256]{1,0:T(8,128)S(1)} %convolution_subtract_fusion.start_ref, f32[256,256]{1,0:T(8,128)S(1)} %bitcast.96, bf16[16,256,256]{2,1,0:T(8,128)(2,1)S(1)} %bitcast.94, bf16[256,256]{1,0:T(8,128)(2,1)S(1)} %get-tuple-element.17.hi_ref, ...), custom_call_target="tpu_custom_call" | custom-call | tf_op jit(solution)/shard_map/pallas_call | solution.py:260
  178.5 0.5 fusion.9
  179.0 0.6 fusion.6
  179.6 0.6 copy-done.10
  180.2 1.1 fusion.46
  181.3 0.8 copy_bitcast_fusion
  182.2 0.2 select_reduce_fusion
  182.4 0.3 fusion.13
  182.7 0.9 copy.65.coef_ref
  183.7 0.1 fusion.25
  183.8 0.7 copy.30.centre_ref
  184.5 14.2 %shard_map.178 = (bf16[16,2,64,128]{3,2,1,0:T(8,128)(2,1)}, f32[16,2,3,128]{3,2,1,0:T(4,128)}) custom-call(bf16[16,2,64,128]{3,2,1,0:T(8,128)(2,1)} %copy.65.coef_ref, f32[16,2,3,128]{3,2,1,0:T(4,128)} %copy.30.centre_ref), custom_call_target="tpu_custom_call" | custom-call | tf_op jit(solution)/shard_map/pallas_call | solution.py:509
  198.7 1.7 compare_reduce_fusion
  200.4 0.1 and.27
  200.5 0.6 and_convert_fusion.pattern_ref
  201.1 1.3 copy.31
  202.4 48.9 %shard_map.179 = f32[64,2048]{1,0:T(8,128)} custom-call(s32[16,32]{1,0:T(8,128)} %and_convert_fusion.pattern_ref, bf16[32,64,128]{2,1,0:T(8,128)(2,1)} %bitcast.99, f32[32,3,128]{2,1,0:T(4,128)} %bitcast.101, f32[16,128,3]{2,1,0:T(8,128)} %bitcast.98), custom_call_target="tpu_custom_call" | custom-call | tf_op jit(solution)/shard_map/pallas_call | solution.py:359
  251.3 0.6 copy.69
  (34 shorter events, 0.2 us)
Async XLA Ops:
  0.6 3.7 %copy-start = (bf16[16,2,256,128]{3,2,1,0:T(8,128)(2,1)S(1)}, bf16[16,2,256,128]{3,2,1,0:T(8,128)(2,1)}, u32[]{:S(2)}) copy-start(bf16[16,2,256,128]{3,2,1,0:T(8,128)(2,1)} %param.19) | copy-start | bytes 6291460
  4.3 0.9 copy-start.6
  4.3 0.9 copy-start.15
  5.2 2.2 copy-start.3
  5.2 3.5 %copy-start.5 = (f32[64,256]{1,0:T(8,128)S(1)}, f32[64,256]{1,0:T(8,128)}, u32[]{:S(2)}) copy-start(f32[64,256]{1,0:T(8,128)} %rhs_ref.1) | copy-start | bytes 196612
  8.7 1.6 copy-start.1
  10.3 61.1 %copy-start.8 = (bf16[256,2048]{1,0:T(8,128)(2,1)S(1)}, bf16[256,2048]{1,0:T(8,128)(2,1)}, u32[]{:S(2)}) copy-start(bf16[256,2048]{1,0:T(8,128)(2,1)} %param.23) | copy-start | bytes 3145732
  71.4 27.6 %copy-start.4 = (f32[16,128,128]{2,1,0:T(8,128)S(1)}, f32[16,128,128]{2,1,0:T(8,128)}, u32[]{:S(2)}) copy-start(f32[16,128,128]{2,1,0:T(8,128)} %inv_ref.1) | copy-start | bytes 3145732
  99.0 16.8 %copy-start.9 = (bf16[256,2048]{1,0:T(8,128)(2,1)S(1)}, bf16[256,2048]{1,0:T(8,128)(2,1)}, u32[]{:S(2)}) copy-start(bf16[256,2048]{1,0:T(8,128)(2,1)} %param.23) | copy-start | bytes 3145732
  117.5 1.6 copy-start.2
  119.1 59.9 %copy-start.7 = (f32[16,64,128]{2,1,0:T(8,128)S(1)}, f32[16,64,128]{2,1,0:T(8,128)}, u32[]{:S(2)}) copy-start(f32[16,64,128]{2,1,0:T(8,128)} %copy-done.6) | copy-start | bytes 1572868
  179.0 1.2 copy-start.10
  180.2 1.9 copy-start.14
  180.2 3.5 %copy-start.12 = (f32[16,3,128]{2,0,1:T(8,128)S(1)}, f32[16,3,128]{2,0,1:T(8,128)}, u32[]{:S(2)}) copy-start(f32[16,3,128]{2,0,1:T(8,128)} %param.27) | copy-start | bytes 73732
  181.3 19.2 %copy-start.13 = (s32[16,32]{1,0:T(8,128)S(1)}, s32[16,32]{1,0:T(8,128)}, u32[]{:S(2)}) copy-start(s32[16,32]{1,0:T(8,128)} %param.29) | copy-start | bytes 6148
  181.3 19.8 %copy-start.11 = (f32[1,3,2048]{2,0,1:T(1,128)S(1)}, f32[1,3,2048]{2,0,1:T(1,128)}, u32[]{:S(2)}) copy-start(f32[1,3,2048]{2,0,1:T(1,128)} %param.28) | copy-start | bytes 73732

commit v14 on v13

--- a/solution.py
+++ b/solution.py
@@ -312,25 +312,30 @@
     )(top_start, top_inverse, top_lower)
 
 
-def evaluate_kernel(slots, pattern_ref, coef_ref, centre_ref, column_ref, out_ref, acc, spread):
+def evaluate_kernel(slots, pattern_ref, coef_ref, centre_ref, point_ref, out_ref, acc, spread):
     m = pl.program_id(0)
+    width = point_ref.shape[2]
+
+    @pl.when(m == 0)
+    def _():
+        for s in range(slots):
+            column = centre_ref[s]
+            for comp in range(3):
+                spread[s, comp] = jnp.broadcast_to(column[:, comp : comp + 1], (column.shape[0], width))
+
     acc[...] = jnp.zeros_like(acc)
-    column = column_ref[0]
-    width = centre_ref.shape[2]
-    for comp in range(3):
-        spread[comp] = jnp.broadcast_to(column[:, comp : comp + 1], (column.shape[0], width))
+    row = point_ref[0]
 
     def one_slot(s, carry):
         @pl.when(pattern_ref[m, s] != 0)
         def _():
-            centre = centre_ref[s]
             dist = None
             for comp in range(3):
-                delta = centre[comp : comp + 1, :] - spread[comp]
+                delta = spread[s, comp] - row[comp : comp + 1, :]
                 dist = delta * delta if dist is None else dist + delta * delta
-            weight = jnp.maximum(1.0 - dist * (1.0 / support_sq), 0.0)
+            weight = jnp.maximum(1.0 - dist, 0.0)
             kernel = (weight * weight * weight).astype(jnp.bfloat16)
-            acc[...] += _nt(coef_ref[s], kernel)
+            acc[...] += _nn(coef_ref[s], kernel)
 
         return carry
 
@@ -338,29 +343,30 @@
     out_ref[...] = acc[...]
 
 
-def evaluate_all(coef_all, centre_all, point_columns, pattern):
+def evaluate_all(coef_all, centre_columns, point_rows, pattern):
     slots, rows, span = coef_all.shape
-    blocks = point_columns.shape[0]
+    blocks = point_rows.shape[0]
     full = lambda shape: pl.BlockSpec(shape, lambda m, pat: (0,) * len(shape))
     grid_spec = pltpu.PrefetchScalarGridSpec(
         num_scalar_prefetch=1,
         grid=(blocks,),
         in_specs=[
             full(coef_all.shape),
-            full(centre_all.shape),
-            pl.BlockSpec((1, span, point_columns.shape[2]), lambda m, pat: (m, 0, 0)),
+            full(centre_columns.shape),
+            pl.BlockSpec((1,) + point_rows.shape[1:], lambda m, pat: (m, 0, 0)),
         ],
         out_specs=pl.BlockSpec((rows, span), lambda m, pat: (0, m)),
         scratch_shapes=[
             pltpu.VMEM((rows, span), jnp.float32),
-            pltpu.VMEM((3, span, centre_all.shape[2]), jnp.float32),
+            pltpu.VMEM((slots, 3, centre_columns.shape[1], point_rows.shape[2]), jnp.float32),
         ],
     )
     return pl.pallas_call(
         functools.partial(evaluate_kernel, slots),
         out_shape=jax.ShapeDtypeStruct((rows, blocks * span), jnp.float32),
         grid_spec=grid_spec,
-    )(pattern, coef_all, centre_all, point_columns)
+        compiler_params=pltpu.CompilerParams(vmem_limit_bytes=48 * 1024 * 1024),
+    )(pattern, coef_all, centre_columns, point_rows)
 
 
 def top_reduce_kernel(n, groups, span, term_ref, total_ref, parts_a, parts_b, gathered, local_sem, send_a, recv_a, send_b, recv_b, send_c, recv_c):
@@ -624,10 +630,12 @@
     coef_all = received.reshape(slot_total, snapshots, span)
     centre_all = recv_centre.reshape(slot_total, 3, span)
     point_blocks = eval_pattern.shape[0]
-    point_columns = points[0].T.reshape(point_blocks, span, points.shape[1])
+    scale = support_sq**-0.5
+    centre_columns = jnp.swapaxes(centre_all * scale, 1, 2)
+    point_rows = (points[0] * scale).reshape(3, point_blocks, span).transpose(1, 0, 2)
     filled = jnp.any(coef_all != 0, axis=(1, 2))
     flags = ((eval_pattern != 0) & filled[None, :]).astype(jnp.int32)
-    values = evaluate_all(coef_all, centre_all, point_columns, flags)
+    values = evaluate_all(coef_all, centre_columns, point_rows, flags)
     return (coef_leaf, coef_sep, coef_top, values)
 
 

time: 253 us -> 254 us (level)
  the two profiles are of different devices: /device:TPU:122 before, /device:TPU:10 now
where the time goes in v14:
time: 254 us; the launch traced here: 253 us
  Pallas kernels  223 us (88%)
  matrix products  14.3 us (6%)
  local copies, waits for them, and re-layouts  7.59 us (3%)
  other arithmetic  7.13 us (3%)
    pallas_call x1, Pallas kernels, sep_solve(): pl.pallas_call(functools.partial(sep_backward_kernel, n), out_shape=(sol_...  57.7 us
    pallas_call x1, Pallas kernels, top_reduce(): pl.pallas_call(functools.partial(top_reduce_kernel, n, groups, span), out...  56.8 us
    pallas_call x1, Pallas kernels, evaluate_all(): pl.pallas_call(functools.partial(evaluate_kernel, slots), out_shape=jax.S...  43.3 us
    pallas_call x1, Pallas kernels, sep_solve(): pl.pallas_call(functools.partial(sep_forward_kernel, n), out_shape=sol_sh...  31.9 us
    pallas_call x1, Pallas kernels, top_solve(): pl.pallas_call(functools.partial(top_solve_kernel, nt, span), out_shape=(...  16.9 us
    pallas_call x1, Pallas kernels, exchange(): pl.pallas_call(functools.partial(exchange_kernel, n), out_shape=(jax.Shap...  16.5 us

profile of v14, /device:TPU:10, one launch (start us, length us, event | category | flops | bytes accessed | tf_op | source)
XLA Modules:
  0.0 253.2 jit_solution(18045932591709146663)
XLA Ops:
  0.7 0.8 iota_compare_fusion.2
  1.5 0.8 fusion.35
  2.3 0.8 select_reduce_fusion
  3.2 0.8 broadcast_multiply_fusion.1
  3.9 0.9 fusion.25
  4.8 0.7 copy.30.centre_ref
  5.5 1.3 subtract_convert_fusion.1
  6.8 2.0 subtract_convert_fusion
  8.9 3.2 %fusion.7 = f32[16,64,128]{2,1,0:T(8,128)S(1)} fusion(f32[16,128,128]{2,1,0:T(8,128)S(1)} %copy-done.14, f32[64,2048]{1,0:T(8,128)} %param.15), kind=kOutput, calls=%fused_computation.13 | convolution fusion | flops 201326592 | bytes 2097152 | tf_op jit(solution)/shard_map/nrs,nts->nrt/dot_general | solution.py:574
  12.1 0.8 fusion.11
  13.0 2.0 fusion.3
  15.3 31.9 %shard_map.174 = f32[64,256]{1,0:T(8,128)S(1)} custom-call(f32[64,256]{1,0:T(8,128)S(1)} %copy-done.9, bf16[16,64,256]{2,1,0:T(8,128)(2,1)S(1)} %copy.66.part_ref, f32[256,256]{1,0:T(8,128)S(1)} %bitcast.96, bf16[16,256,256]{2,1,0:T(8,128)(2,1)S(1)} %bitcast.93, bf16[256,256]{1,0:T(8,128)(2,1)S(1)} %get-tuple-element.19.hi_ref, ...), custom_call_target="tpu_custom_call" | custom-call | tf_op jit(solution)/shard_map/pallas_call | solution.py:246
  47.2 1.1 fusion.23.term_ref
  48.3 56.8 %shard_map.175 = f32[64,2048]{1,0:T(8,128)} custom-call(f32[64,2048]{1,0:T(8,128)} %fusion.23.term_ref), custom_call_target="tpu_custom_call" | custom-call | tf_op jit(solution)/shard_map/pallas_call | solution.py:458
  105.1 1.3 sub.31.start_ref
  106.4 16.9 %shard_map.176 = (f32[64,2048]{1,0:T(8,128)}, bf16[64,2048]{1,0:T(8,128)(2,1)S(1)}) custom-call(f32[64,2048]{1,0:T(8,128)S(1)} %sub.31.start_ref, f32[16,128,128]{2,1,0:T(8,128)S(1)} %copy-done.6, bf16[2048,2048]{1,0:T(8,128)(2,1)} %lower_ref.1), custom_call_target="tpu_custom_call" | custom-call | tf_op jit(solution)/shard_map/pallas_call | solution.py:299
  123.3 0.4 convolution_subtract_fusion.start_ref
  123.8 57.7 %shard_map.177 = (f32[64,256]{1,0:T(8,128)S(1)}, bf16[16,64,256]{2,1,0:T(8,128)(2,1)S(1)}) custom-call(f32[64,256]{1,0:T(8,128)S(1)} %convolution_subtract_fusion.start_ref, f32[256,256]{1,0:T(8,128)S(1)} %bitcast.97, bf16[16,256,256]{2,1,0:T(8,128)(2,1)S(1)} %bitcast.94, bf16[256,256]{1,0:T(8,128)(2,1)S(1)} %copy-done.8, bf16[256,256]{1,0:T(8,128)(2,1)S(1)} %copy-done.7), custom_call_target="tpu_custom_call" | custom-call | tf_op jit(solution)/shard_map/pallas_call | solution.py:260
  181.5 0.5 fusion.9
  182.1 0.6 fusion.6
  182.7 0.6 copy-done.15
  183.3 1.1 fusion.46
  184.3 0.3 fusion.13
  184.6 0.9 copy.65.coef_ref
  185.6 16.5 %shard_map.178 = (bf16[16,2,64,128]{3,2,1,0:T(8,128)(2,1)}, f32[16,2,3,128]{3,2,1,0:T(4,128)}) custom-call(bf16[16,2,64,128]{3,2,1,0:T(8,128)(2,1)} %copy.65.coef_ref, f32[16,2,3,128]{3,2,1,0:T(4,128)} %copy.30.centre_ref), custom_call_target="tpu_custom_call" | custom-call | tf_op jit(solution)/shard_map/pallas_call | solution.py:515
  202.1 0.9 broadcast_multiply_fusion
  203.0 1.7 compare_reduce_fusion
  204.9 0.8 copy_bitcast_fusion
  205.7 2.0 copy.31
  207.7 1.6 copy-done.3
  209.3 43.3 %shard_map.179 = f32[64,2048]{1,0:T(8,128)} custom-call(s32[16,32]{1,0:T(8,128)S(1)} %and_convert_fusion.pattern_ref, bf16[32,64,128]{2,1,0:T(8,128)(2,1)S(1)} %bitcast.98, f32[32,128,3]{2,1,0:T(8,128)S(1)} %bitcast.95, f32[16,3,128]{2,1,0:T(4,128)S(1)} %bitcast.100), custom_call_target="tpu_custom_call" | custom-call | tf_op jit(solution)/shard_map/pallas_call | solution.py:364
  252.6 0.6 copy.69
  (40 shorter events, 0.4 us)
Async XLA Ops:
  0.6 11.4 %copy-start = (bf16[16,2,256,128]{3,2,1,0:T(8,128)(2,1)S(1)}, bf16[16,2,256,128]{3,2,1,0:T(8,128)(2,1)}, u32[]{:S(2)}) copy-start(bf16[16,2,256,128]{3,2,1,0:T(8,128)(2,1)} %param.19) | copy-start | bytes 6291460
  0.6 8.2 %copy-start.14 = (f32[16,128,128]{2,1,0:T(8,128)S(1)}, f32[16,128,128]{2,1,0:T(8,128)}, u32[]{:S(2)}) copy-start(f32[16,128,128]{2,1,0:T(8,128)} %param.18) | copy-start | bytes 3145732
  12.1 0.9 copy-start.10
  12.1 0.9 copy-start.17
  13.0 2.3 copy-start.1
  13.0 2.3 copy-start.4
  13.0 2.3 copy-start.9
  15.0 32.1 %copy-start.12 = (bf16[256,2048]{1,0:T(8,128)(2,1)S(1)}, bf16[256,2048]{1,0:T(8,128)(2,1)}, u32[]{:S(2)}) copy-start(bf16[256,2048]{1,0:T(8,128)(2,1)} %param.23) | copy-start | bytes 3145732
  47.2 59.2 %copy-start.6 = (f32[16,128,128]{2,1,0:T(8,128)S(1)}, f32[16,128,128]{2,1,0:T(8,128)}, u32[]{:S(2)}) copy-start(f32[16,128,128]{2,1,0:T(8,128)} %inv_ref.1) | copy-start | bytes 3145732
  106.4 16.9 %copy-start.13 = (bf16[256,2048]{1,0:T(8,128)(2,1)S(1)}, bf16[256,2048]{1,0:T(8,128)(2,1)}, u32[]{:S(2)}) copy-start(bf16[256,2048]{1,0:T(8,128)(2,1)} %param.23) | copy-start | bytes 3145732
  106.4 17.3 %copy-start.2 = (bf16[1,16,256,256]{3,2,1,0:T(8,128)(2,1)S(1)}, bf16[1,16,256,256]{3,2,1,0:T(8,128)(2,1)}, u32[]{:S(2)}) copy-start(bf16[1,16,256,256]{3,2,1,0:T(8,128)(2,1)} %param.22) | copy-start | bytes 6291460
  106.4 17.3 %copy-start.7 = (bf16[256,256]{1,0:T(8,128)(2,1)S(1)}, bf16[256,256]{1,0:T(8,128)(2,1)}, u32[]{:S(2)}) copy-start(bf16[256,256]{1,0:T(8,128)(2,1)} %get-tuple-element.16.lo_ref) | copy-start | bytes 393220
  106.4 17.3 %copy-start.8 = (bf16[256,256]{1,0:T(8,128)(2,1)S(1)}, bf16[256,256]{1,0:T(8,128)(2,1)}, u32[]{:S(2)}) copy-start(bf16[256,256]{1,0:T(8,128)(2,1)} %get-tuple-element.17.hi_ref) | copy-start | bytes 393220
  123.8 58.3 %copy-start.11 = (f32[16,64,128]{2,1,0:T(8,128)S(1)}, f32[16,64,128]{2,1,0:T(8,128)}, u32[]{:S(2)}) copy-start(f32[16,64,128]{2,1,0:T(8,128)} %copy-done.10) | copy-start | bytes 1572868
  182.0 1.2 copy-start.15
  184.3 20.5 %copy-start.16 = (s32[16,32]{1,0:T(8,128)S(1)}, s32[16,32]{1,0:T(8,128)}, u32[]{:S(2)}) copy-start(s32[16,32]{1,0:T(8,128)} %param.29) | copy-start | bytes 6148
  202.1 5.6 %copy-start.5 = (bf16[16,2,64,128]{3,2,1,0:T(8,128)(2,1)S(1)}, bf16[16,2,64,128]{3,2,1,0:T(8,128)(2,1)}, u32[]{:S(2)}) copy-start(bf16[16,2,64,128]{3,2,1,0:T(8,128)(2,1)} %get-tuple-element.14) | copy-start | bytes 1572868
  207.7 1.6 copy-start.3

commit v15 on v14

--- a/solution.py
+++ b/solution.py
@@ -633,9 +633,7 @@
     scale = support_sq**-0.5
     centre_columns = jnp.swapaxes(centre_all * scale, 1, 2)
     point_rows = (points[0] * scale).reshape(3, point_blocks, span).transpose(1, 0, 2)
-    filled = jnp.any(coef_all != 0, axis=(1, 2))
-    flags = ((eval_pattern != 0) & filled[None, :]).astype(jnp.int32)
-    values = evaluate_all(coef_all, centre_columns, point_rows, flags)
+    values = evaluate_all(coef_all, centre_columns, point_rows, eval_pattern)
     return (coef_leaf, coef_sep, coef_top, values)
 
 

time: 254 us -> 256 us (level)
  the two profiles are of different devices: /device:TPU:10 before, /device:TPU:24 now
where the time goes in v15:
time: 256 us; the launch traced here: 252 us
  Pallas kernels  222 us (87%)
  matrix products  15.2 us (6%)
  local copies, waits for them, and re-layouts  8.54 us (3%)
  other arithmetic  5.42 us (2%)
    pallas_call x1, Pallas kernels, sep_solve(): pl.pallas_call(functools.partial(sep_backward_kernel, n), out_shape=(sol_...  57.5 us
    pallas_call x1, Pallas kernels, sep_solve(): pl.pallas_call(functools.partial(sep_forward_kernel, n), out_shape=sol_sh...  57.1 us
    pallas_call x1, Pallas kernels, evaluate_all(): pl.pallas_call(functools.partial(evaluate_kernel, slots), out_shape=jax.S...  42.3 us
    pallas_call x1, Pallas kernels, top_reduce(): pl.pallas_call(functools.partial(top_reduce_kernel, n, groups, span), out...  33.1 us
    pallas_call x1, Pallas kernels, top_solve(): pl.pallas_call(functools.partial(top_solve_kernel, nt, span), out_shape=(...  16.9 us
    pallas_call x1, Pallas kernels, exchange(): pl.pallas_call(functools.partial(exchange_kernel, n), out_shape=(jax.Shap...  15.3 us

profile of v15, /device:TPU:24, one launch (start us, length us, event | category | flops | bytes accessed | tf_op | source)
XLA Modules:
  0.0 252.4 jit_solution(4039616227986653953)
XLA Ops:
  0.7 0.8 iota_compare_fusion.2
  1.5 0.8 fusion.35
  2.3 0.8 select_reduce_fusion
  3.2 0.8 broadcast_multiply_fusion.1
  3.9 0.9 fusion.25
  4.8 0.7 copy.30.centre_ref
  5.5 1.3 subtract_convert_fusion.1
  6.8 2.0 subtract_convert_fusion
  8.9 3.2 %fusion.7 = f32[16,64,128]{2,1,0:T(8,128)S(1)} fusion(f32[16,128,128]{2,1,0:T(8,128)S(1)} %copy-done.15, f32[64,2048]{1,0:T(8,128)} %param.15), kind=kOutput, calls=%fused_computation.12 | convolution fusion | flops 201326592 | bytes 2097152 | tf_op jit(solution)/shard_map/nrs,nts->nrt/dot_general | solution.py:574
  12.1 0.8 fusion.11
  13.0 2.0 fusion.3
  15.1 0.2 copy.66.part_ref
  15.3 57.1 %shard_map.174 = f32[64,256]{1,0:T(8,128)S(1)} custom-call(f32[64,256]{1,0:T(8,128)S(1)} %copy-done.9, bf16[16,64,256]{2,1,0:T(8,128)(2,1)S(1)} %copy.66.part_ref, f32[256,256]{1,0:T(8,128)S(1)} %bitcast.96, bf16[16,256,256]{2,1,0:T(8,128)(2,1)S(1)} %bitcast.93, bf16[256,256]{1,0:T(8,128)(2,1)S(1)} %get-tuple-element.19.hi_ref, ...), custom_call_target="tpu_custom_call" | custom-call | tf_op jit(solution)/shard_map/pallas_call | solution.py:246
  72.4 1.1 fusion.23.term_ref
  73.5 33.1 %shard_map.175 = f32[64,2048]{1,0:T(8,128)} custom-call(f32[64,2048]{1,0:T(8,128)} %fusion.23.term_ref), custom_call_target="tpu_custom_call" | custom-call | tf_op jit(solution)/shard_map/pallas_call | solution.py:458
  106.7 1.3 sub.31.start_ref
  108.0 16.9 %shard_map.176 = (f32[64,2048]{1,0:T(8,128)}, bf16[64,2048]{1,0:T(8,128)(2,1)S(1)}) custom-call(f32[64,2048]{1,0:T(8,128)S(1)} %sub.31.start_ref, f32[16,128,128]{2,1,0:T(8,128)S(1)} %copy-done.5, bf16[2048,2048]{1,0:T(8,128)(2,1)} %lower_ref.1), custom_call_target="tpu_custom_call" | custom-call | tf_op jit(solution)/shard_map/pallas_call | solution.py:299
  124.8 0.4 convolution_subtract_fusion.start_ref
  125.3 57.5 %shard_map.177 = (f32[64,256]{1,0:T(8,128)S(1)}, bf16[16,64,256]{2,1,0:T(8,128)(2,1)S(1)}) custom-call(f32[64,256]{1,0:T(8,128)S(1)} %convolution_subtract_fusion.start_ref, f32[256,256]{1,0:T(8,128)S(1)} %bitcast.97, bf16[16,256,256]{2,1,0:T(8,128)(2,1)S(1)} %bitcast.94, bf16[256,256]{1,0:T(8,128)(2,1)S(1)} %copy-done.8, bf16[256,256]{1,0:T(8,128)(2,1)S(1)} %copy-done.7), custom_call_target="tpu_custom_call" | custom-call | tf_op jit(solution)/shard_map/pallas_call | solution.py:260
  182.9 0.5 fusion.9
  183.4 0.6 fusion.6
  184.0 0.6 copy-done.16
  184.6 1.9 fusion.46
  186.5 0.3 fusion.13
  186.8 0.9 copy.65.coef_ref
  187.8 15.3 %shard_map.178 = (bf16[16,2,64,128]{3,2,1,0:T(8,128)(2,1)}, f32[16,2,3,128]{3,2,1,0:T(4,128)}) custom-call(bf16[16,2,64,128]{3,2,1,0:T(8,128)(2,1)} %copy.65.coef_ref, f32[16,2,3,128]{3,2,1,0:T(4,128)} %copy.30.centre_ref), custom_call_target="tpu_custom_call" | custom-call | tf_op jit(solution)/shard_map/pallas_call | solution.py:515
  203.1 0.9 broadcast_multiply_fusion
  204.0 1.9 copy_bitcast_fusion
  205.9 2.0 copy.31
  207.9 1.6 copy-done.3
  209.5 42.3 %shard_map.179 = f32[64,2048]{1,0:T(8,128)} custom-call(s32[16,32]{1,0:T(8,128)S(1)} %copy-done.10, bf16[32,64,128]{2,1,0:T(8,128)(2,1)S(1)} %bitcast.98, f32[32,128,3]{2,1,0:T(8,128)S(1)} %bitcast.95, f32[16,3,128]{2,1,0:T(4,128)S(1)} %bitcast.100), custom_call_target="tpu_custom_call" | custom-call | tf_op jit(solution)/shard_map/pallas_call | solution.py:364
  251.8 0.6 copy.69
  (37 shorter events, 0.2 us)
Async XLA Ops:
  0.6 11.4 %copy-start = (bf16[16,2,256,128]{3,2,1,0:T(8,128)(2,1)S(1)}, bf16[16,2,256,128]{3,2,1,0:T(8,128)(2,1)}, u32[]{:S(2)}) copy-start(bf16[16,2,256,128]{3,2,1,0:T(8,128)(2,1)} %param.19) | copy-start | bytes 6291460
  0.6 8.2 %copy-start.15 = (f32[16,128,128]{2,1,0:T(8,128)S(1)}, f32[16,128,128]{2,1,0:T(8,128)}, u32[]{:S(2)}) copy-start(f32[16,128,128]{2,1,0:T(8,128)} %param.18) | copy-start | bytes 3145732
  12.1 0.9 copy-start.11
  12.1 0.9 copy-start.17
  13.0 2.3 copy-start.1
  13.0 2.3 copy-start.4
  13.0 2.3 copy-start.9
  15.0 57.4 %copy-start.13 = (bf16[256,2048]{1,0:T(8,128)(2,1)S(1)}, bf16[256,2048]{1,0:T(8,128)(2,1)}, u32[]{:S(2)}) copy-start(bf16[256,2048]{1,0:T(8,128)(2,1)} %param.23) | copy-start | bytes 3145732
  72.4 35.5 %copy-start.5 = (f32[16,128,128]{2,1,0:T(8,128)S(1)}, f32[16,128,128]{2,1,0:T(8,128)}, u32[]{:S(2)}) copy-start(f32[16,128,128]{2,1,0:T(8,128)} %inv_ref.1) | copy-start | bytes 3145732
  107.9 16.9 %copy-start.14 = (bf16[256,2048]{1,0:T(8,128)(2,1)S(1)}, bf16[256,2048]{1,0:T(8,128)(2,1)}, u32[]{:S(2)}) copy-start(bf16[256,2048]{1,0:T(8,128)(2,1)} %param.23) | copy-start | bytes 3145732
  107.9 17.3 %copy-start.2 = (bf16[1,16,256,256]{3,2,1,0:T(8,128)(2,1)S(1)}, bf16[1,16,256,256]{3,2,1,0:T(8,128)(2,1)}, u32[]{:S(2)}) copy-start(bf16[1,16,256,256]{3,2,1,0:T(8,128)(2,1)} %param.22) | copy-start | bytes 6291460
  108.0 17.3 %copy-start.7 = (bf16[256,256]{1,0:T(8,128)(2,1)S(1)}, bf16[256,256]{1,0:T(8,128)(2,1)}, u32[]{:S(2)}) copy-start(bf16[256,256]{1,0:T(8,128)(2,1)} %get-tuple-element.16.lo_ref) | copy-start | bytes 393220
  108.0 17.3 %copy-start.8 = (bf16[256,256]{1,0:T(8,128)(2,1)S(1)}, bf16[256,256]{1,0:T(8,128)(2,1)}, u32[]{:S(2)}) copy-start(bf16[256,256]{1,0:T(8,128)(2,1)} %get-tuple-element.17.hi_ref) | copy-start | bytes 393220
  125.3 58.1 %copy-start.12 = (f32[16,64,128]{2,1,0:T(8,128)S(1)}, f32[16,64,128]{2,1,0:T(8,128)}, u32[]{:S(2)}) copy-start(f32[16,64,128]{2,1,0:T(8,128)} %copy-done.11) | copy-start | bytes 1572868
  183.4 1.2 copy-start.16
  187.8 20.1 %copy-start.10 = (s32[16,32]{1,0:T(8,128)S(1)}, s32[16,32]{1,0:T(8,128)}, u32[]{:S(2)}) copy-start(s32[16,32]{1,0:T(8,128)} %pattern_ref.1) | copy-start | bytes 6148
  203.1 4.8 %copy-start.6 = (bf16[16,2,64,128]{3,2,1,0:T(8,128)(2,1)S(1)}, bf16[16,2,64,128]{3,2,1,0:T(8,128)(2,1)}, u32[]{:S(2)}) copy-start(bf16[16,2,64,128]{3,2,1,0:T(8,128)(2,1)} %get-tuple-element.14) | copy-start | bytes 1572868
  207.9 1.6 copy-start.3

commit v16 on v11

--- a/solution.py
+++ b/solution.py
@@ -273,13 +273,20 @@
     return hi, lo
 
 
-def top_solve_kernel(nt, span, start_ref, inv_ref, lower_ref, coef_ref, half_ref, fwd_half, fwd_full):
+def _three_pass(x, hi, lo, dims):
+    x_hi = x.astype(jnp.bfloat16)
+    x_lo = (x - x_hi.astype(jnp.float32)).astype(jnp.bfloat16)
+    dot = lambda u, v: lax.dot_general(u, v, (dims, ((), ())), preferred_element_type=jnp.float32)
+    return dot(x_hi, hi) + (dot(x_hi, lo) + dot(x_lo, hi))
+
+
+def top_solve_kernel(nt, span, start_ref, hi_ref, lo_ref, lower_ref, coef_ref, half_ref, fwd_half, fwd_full):
     for t in range(nt):
         cols = slice(t * span, (t + 1) * span)
         residue = start_ref[:, cols]
         if t > 0:
             residue = residue - _nt(fwd_half[:, : t * span], lower_ref[cols, : t * span])
-        solved = _nt_exact(residue, inv_ref[t])
+        solved = _three_pass(residue, hi_ref[t], lo_ref[t], ((1,), (1,)))
         fwd_full[:, cols] = solved
         fwd_half[:, cols] = solved.astype(jnp.bfloat16)
     for t in reversed(range(nt)):
@@ -287,7 +294,7 @@
         residue = fwd_full[:, cols]
         if t < nt - 1:
             residue = residue - _nn(half_ref[:, (t + 1) * span :], lower_ref[(t + 1) * span :, cols])
-        solved = _nn_exact(residue, inv_ref[t])
+        solved = _three_pass(residue, hi_ref[t], lo_ref[t], ((1,), (0,)))
         coef_ref[:, cols] = solved
         half_ref[:, cols] = solved.astype(jnp.bfloat16)
 
@@ -302,14 +309,14 @@
             jax.ShapeDtypeStruct((rows, width), jnp.float32),
             jax.ShapeDtypeStruct((rows, width), jnp.bfloat16),
         ),
-        in_specs=[vmem] * 3,
+        in_specs=[vmem] * 4,
         out_specs=(vmem, vmem),
         scratch_shapes=[
             pltpu.VMEM((rows, width), jnp.bfloat16),
             pltpu.VMEM((rows, width), jnp.float32),
         ],
         compiler_params=pltpu.CompilerParams(vmem_limit_bytes=48 * 1024 * 1024),
-    )(top_start, top_inverse, top_lower)
+    )(top_start, *split_pair(top_inverse), top_lower)
 
 
 def evaluate_kernel(slots, pattern_ref, coef_ref, centre_ref, column_ref, out_ref, acc, spread):

time: 252 us -> 252 us (level)
  no operation moved by 1% of the time
where the time goes in v16:
time: 252 us; the launch traced here: 248 us
  Pallas kernels  224 us (89%)
  matrix products  13.2 us (5%)
  local copies, waits for them, and re-layouts  8.58 us (3%)
    pallas_call x1, Pallas kernels, sep_solve(): pl.pallas_call(functools.partial(sep_backward_kernel, n), out_shape=(sol_...  57.3 us
    pallas_call x1, Pallas kernels, sep_solve(): pl.pallas_call(functools.partial(sep_forward_kernel, n), out_shape=sol_sh...  56.9 us
    pallas_call x1, Pallas kernels, evaluate_all(): pl.pallas_call(functools.partial(evaluate_kernel, slots), out_shape=jax.S...  46.9 us
    pallas_call x1, Pallas kernels, top_reduce(): pl.pallas_call(functools.partial(top_reduce_kernel, n, groups, span), out...  33.2 us
    pallas_call x1, Pallas kernels, top_solve(): pl.pallas_call(functools.partial(top_solve_kernel, nt, span), out_shape=(...  14.6 us
    pallas_call x1, Pallas kernels, exchange(): pl.pallas_call(functools.partial(exchange_kernel, n), out_shape=(jax.Shap...  14.6 us

profile of v16, /device:TPU:24, one launch (start us, length us, event | category | flops | bytes accessed | tf_op | source)
XLA Modules:
  0.0 248.1 jit_solution(1972627475730661704)
XLA Ops:
  0.6 3.7 %fusion.7 = f32[16,64,128]{2,1,0:T(8,128)S(1)} fusion(f32[16,128,128]{2,1,0:T(8,128)} %param.18, f32[64,2048]{1,0:T(8,128)} %param.15), kind=kOutput, calls=%fused_computation.13 | convolution fusion | flops 201326592 | bytes 2097152 | tf_op jit(solution)/shard_map/nrs,nts->nrt/dot_general | solution.py:575
  4.3 0.8 fusion.11
  5.2 2.0 fusion.3
  7.3 0.2 copy.66.part_ref
  7.4 1.2 subtract_convert_fusion.2
  8.7 1.6 copy-done.1
  10.3 56.9 %shard_map.174 = f32[64,256]{1,0:T(8,128)S(1)} custom-call(f32[64,256]{1,0:T(8,128)S(1)} %copy-done.4, bf16[16,64,256]{2,1,0:T(8,128)(2,1)S(1)} %copy.66.part_ref, f32[256,256]{1,0:T(8,128)S(1)} %bitcast.95, bf16[16,256,256]{2,1,0:T(8,128)(2,1)S(1)} %bitcast.93, bf16[256,256]{1,0:T(8,128)(2,1)S(1)} %get-tuple-element.21.hi_ref, ...), custom_call_target="tpu_custom_call" | custom-call | tf_op jit(solution)/shard_map/pallas_call | solution.py:246
  67.2 1.1 fusion.23.term_ref
  68.3 33.2 %shard_map.175 = f32[64,2048]{1,0:T(8,128)} custom-call(f32[64,2048]{1,0:T(8,128)} %fusion.23.term_ref), custom_call_target="tpu_custom_call" | custom-call | tf_op jit(solution)/shard_map/pallas_call | solution.py:459
  101.5 1.3 sub.34.start_ref
  102.8 0.2 copy-done.8
  103.0 0.2 subtract_convert_fusion
  103.3 14.6 %shard_map.176 = (f32[64,2048]{1,0:T(8,128)}, bf16[64,2048]{1,0:T(8,128)(2,1)S(1)}) custom-call(f32[64,2048]{1,0:T(8,128)S(1)} %sub.34.start_ref, bf16[16,128,128]{2,1,0:T(8,128)(2,1)S(1)} %get-tuple-element.19.hi_ref, bf16[16,128,128]{2,1,0:T(8,128)(2,1)S(1)} %get-tuple-element.18.lo_ref, bf16[2048,2048]{1,0:T(8,128)(2,1)} %lower_ref.1), custom_call_target="tpu_custom_call" | custom-call | tf_op jit(solution)/shard_map/pallas_call | solution.py:306
  117.9 0.4 convolution_subtract_fusion.start_ref
  118.4 1.2 subtract_convert_fusion.1
  119.6 1.6 copy-done.2
  121.2 57.3 %shard_map.177 = (f32[64,256]{1,0:T(8,128)S(1)}, bf16[16,64,256]{2,1,0:T(8,128)(2,1)S(1)}) custom-call(f32[64,256]{1,0:T(8,128)S(1)} %convolution_subtract_fusion.start_ref, f32[256,256]{1,0:T(8,128)S(1)} %bitcast.96, bf16[16,256,256]{2,1,0:T(8,128)(2,1)S(1)} %bitcast.94, bf16[256,256]{1,0:T(8,128)(2,1)S(1)} %get-tuple-element.17.hi_ref, ...), custom_call_target="tpu_custom_call" | custom-call | tf_op jit(solution)/shard_map/pallas_call | solution.py:260
  178.5 0.5 fusion.9
  179.0 0.6 fusion.6
  179.7 0.6 copy-done.7
  180.3 1.1 fusion.46
  181.4 0.8 copy_bitcast_fusion
  182.2 0.1 fusion.35
  182.3 0.2 select_reduce_fusion
  182.6 0.3 fusion.13
  182.8 0.9 copy.65.coef_ref
  183.8 0.1 fusion.25
  183.9 0.7 copy.30.centre_ref
  184.6 14.6 %shard_map.178 = (bf16[16,2,64,128]{3,2,1,0:T(8,128)(2,1)}, f32[16,2,3,128]{3,2,1,0:T(4,128)}) custom-call(bf16[16,2,64,128]{3,2,1,0:T(8,128)(2,1)} %copy.65.coef_ref, f32[16,2,3,128]{3,2,1,0:T(4,128)} %copy.30.centre_ref), custom_call_target="tpu_custom_call" | custom-call | tf_op jit(solution)/shard_map/pallas_call | solution.py:516
  199.2 1.4 copy.31
  200.6 46.9 %shard_map.179 = f32[64,2048]{1,0:T(8,128)} custom-call(s32[16,32]{1,0:T(8,128)} %pattern_ref.1, bf16[32,64,128]{2,1,0:T(8,128)(2,1)} %bitcast.99, f32[32,3,128]{2,1,0:T(4,128)} %bitcast.101, f32[16,128,3]{2,1,0:T(8,128)} %bitcast.98), custom_call_target="tpu_custom_call" | custom-call | tf_op jit(solution)/shard_map/pallas_call | solution.py:366
  247.5 0.6 copy.69
  (26 shorter events, 0.1 us)
Async XLA Ops:
  0.6 3.7 %copy-start = (bf16[16,2,256,128]{3,2,1,0:T(8,128)(2,1)S(1)}, bf16[16,2,256,128]{3,2,1,0:T(8,128)(2,1)}, u32[]{:S(2)}) copy-start(bf16[16,2,256,128]{3,2,1,0:T(8,128)(2,1)} %param.19) | copy-start | bytes 6291460
  4.3 0.9 copy-start.12
  5.2 2.2 copy-start.3
  5.2 3.5 %copy-start.4 = (f32[64,256]{1,0:T(8,128)S(1)}, f32[64,256]{1,0:T(8,128)}, u32[]{:S(2)}) copy-start(f32[64,256]{1,0:T(8,128)} %rhs_ref.1) | copy-start | bytes 196612
  8.7 1.6 copy-start.1
  10.3 56.9 %copy-start.5 = (bf16[256,2048]{1,0:T(8,128)(2,1)S(1)}, bf16[256,2048]{1,0:T(8,128)(2,1)}, u32[]{:S(2)}) copy-start(bf16[256,2048]{1,0:T(8,128)(2,1)} %param.23) | copy-start | bytes 3145732
  101.5 1.5 copy-start.8
  103.3 14.7 %copy-start.6 = (bf16[256,2048]{1,0:T(8,128)(2,1)S(1)}, bf16[256,2048]{1,0:T(8,128)(2,1)}, u32[]{:S(2)}) copy-start(bf16[256,2048]{1,0:T(8,128)(2,1)} %param.23) | copy-start | bytes 3145732
  119.6 1.6 copy-start.2
  179.0 1.2 copy-start.7
  180.3 2.0 copy-start.11
  180.3 3.5 %copy-start.10 = (f32[16,3,128]{2,0,1:T(8,128)S(1)}, f32[16,3,128]{2,0,1:T(8,128)}, u32[]{:S(2)}) copy-start(f32[16,3,128]{2,0,1:T(8,128)} %param.27) | copy-start | bytes 73732
  181.4 17.8 %copy-start.9 = (f32[1,3,2048]{2,0,1:T(1,128)S(1)}, f32[1,3,2048]{2,0,1:T(1,128)}, u32[]{:S(2)}) copy-start(f32[1,3,2048]{2,0,1:T(1,128)} %param.28) | copy-start | bytes 73732

commit v17 on v16

--- a/solution.py
+++ b/solution.py
@@ -13,6 +13,7 @@
 
 
 highest = lax.Precision.HIGHEST
+three_pass = lax.Precision.HIGH
 support_sq = 0.25
 
 
@@ -572,22 +573,22 @@
     span = leaf_inverse.shape[1]
     slot_count = CAP
     leaf_rhs = rhs_leaf.reshape(snapshots, blocks_here, span).transpose(1, 0, 2)
-    leaf_sol = jnp.einsum("nrs,nts->nrt", leaf_rhs, leaf_inverse, precision=highest)
+    leaf_sol = jnp.einsum("nrs,nts->nrt", leaf_rhs, leaf_inverse, precision=three_pass)
     leaf_half = leaf_sol.astype(jnp.bfloat16)
     partial_value = jnp.einsum(
         "nrs,ncbs->ncrb", leaf_half, leaf_coupling, preferred_element_type=jnp.float32
     )
     onehot = (leaf_targets[:, :, None] == jnp.arange(grp_size)[None, None, :]).astype(jnp.float32)
     picked = onehot
-    parts = jnp.einsum("ncq,ncrb->qrb", picked, partial_value, precision=highest).astype(jnp.bfloat16)
+    parts = jnp.einsum("ncq,ncrb->qrb", picked, partial_value, precision=three_pass).astype(jnp.bfloat16)
     inverse_own = sep_inverse[0]
     own_blocks = sep_blocks[0]
     before = lax.dynamic_index_in_dim(own_blocks, jnp.maximum(my_index - 1, 0), 0, keepdims=False)
     fwd_hi, fwd_lo = split_pair(
-        jnp.dot(before.astype(jnp.float32).T, inverse_own.T, precision=highest)
+        jnp.dot(before.astype(jnp.float32).T, inverse_own.T, precision=three_pass)
     )
     after = lax.dynamic_index_in_dim(own_blocks, jnp.minimum(my_index + 1, grp_size - 1), 0, keepdims=False)
-    bwd_hi, bwd_lo = split_pair(jnp.dot(after.astype(jnp.float32), inverse_own, precision=highest))
+    bwd_hi, bwd_lo = split_pair(jnp.dot(after.astype(jnp.float32), inverse_own, precision=three_pass))
     sep_sol = sep_solve("forward", (rhs_sep, parts), inverse_own, own_blocks, fwd_hi, fwd_lo, grp_size)
     sep_half = sep_sol.astype(jnp.bfloat16)
     top_term = jnp.dot(sep_half, top_coupling, preferred_element_type=jnp.float32)
@@ -610,7 +611,7 @@
     reduced = jnp.einsum(
         "ncrb,ncbs->nrs", picked, leaf_coupling, preferred_element_type=jnp.float32
     )
-    leaf_coef = jnp.einsum("nrs,nst->nrt", leaf_sol - reduced, leaf_inverse, precision=highest)
+    leaf_coef = jnp.einsum("nrs,nst->nrt", leaf_sol - reduced, leaf_inverse, precision=three_pass)
     coef_leaf = leaf_coef.transpose(1, 0, 2).reshape(snapshots, blocks_here * span)
     leaf_out = leaf_coef.astype(jnp.bfloat16)
     slot_ids = jnp.arange(slot_count)

time: 252 us -> 249 us (0.988); the launches traced: 248 us -> 248 us
  no operation moved by 1% of the time
where the time goes in v17:
time: 249 us; the launch traced here: 248 us
  Pallas kernels  225 us (90%)
  matrix products  11.1 us (4%)
  local copies, waits for them, and re-layouts  8.59 us (3%)
    pallas_call x1, Pallas kernels, sep_solve(): pl.pallas_call(functools.partial(sep_backward_kernel, n), out_shape=(sol_...  57.3 us
    pallas_call x1, Pallas kernels, sep_solve(): pl.pallas_call(functools.partial(sep_forward_kernel, n), out_shape=sol_sh...  56.9 us
    pallas_call x1, Pallas kernels, evaluate_all(): pl.pallas_call(functools.partial(evaluate_kernel, slots), out_shape=jax.S...  48.6 us
    pallas_call x1, Pallas kernels, top_reduce(): pl.pallas_call(functools.partial(top_reduce_kernel, n, groups, span), out...  33.1 us
    pallas_call x1, Pallas kernels, exchange(): pl.pallas_call(functools.partial(exchange_kernel, n), out_shape=(jax.Shap...  14.7 us
    pallas_call x1, Pallas kernels, top_solve(): pl.pallas_call(functools.partial(top_solve_kernel, nt, span), out_shape=(...  14.6 us

profile of v17, /device:TPU:24, one launch (start us, length us, event | category | flops | bytes accessed | tf_op | source)
XLA Modules:
  0.0 247.8 jit_solution(10819073913815155672)
XLA Ops:
  0.6 2.7 %fusion.7 = f32[16,64,128]{2,1,0:T(8,128)S(1)} fusion(f32[16,128,128]{2,1,0:T(8,128)} %param.18, f32[64,2048]{1,0:T(8,128)} %param.15), kind=kOutput, calls=%fused_computation.13 | convolution fusion | flops 100663296 | bytes 2097152 | tf_op jit(solution)/shard_map/nrs,nts->nrt/dot_general | solution.py:576
  3.3 0.8 fusion.11
  4.2 1.6 fusion.3
  5.8 0.2 copy.66.part_ref
  6.0 1.2 subtract_convert_fusion.2
  7.2 1.6 copy-done.1
  8.8 56.9 %shard_map.174 = f32[64,256]{1,0:T(8,128)S(1)} custom-call(f32[64,256]{1,0:T(8,128)S(1)} %copy-done.4, bf16[16,64,256]{2,1,0:T(8,128)(2,1)S(1)} %copy.66.part_ref, f32[256,256]{1,0:T(8,128)S(1)} %bitcast.95, bf16[16,256,256]{2,1,0:T(8,128)(2,1)S(1)} %bitcast.93, bf16[256,256]{1,0:T(8,128)(2,1)S(1)} %get-tuple-element.21.hi_ref, ...), custom_call_target="tpu_custom_call" | custom-call | tf_op jit(solution)/shard_map/pallas_call | solution.py:247
  65.8 1.1 fusion.23.term_ref
  66.9 33.1 %shard_map.175 = f32[64,2048]{1,0:T(8,128)} custom-call(f32[64,2048]{1,0:T(8,128)} %fusion.23.term_ref), custom_call_target="tpu_custom_call" | custom-call | tf_op jit(solution)/shard_map/pallas_call | solution.py:460
  100.0 1.3 sub.34.start_ref
  101.4 0.2 copy-done.8
  101.5 0.2 subtract_convert_fusion
  101.8 14.6 %shard_map.176 = (f32[64,2048]{1,0:T(8,128)}, bf16[64,2048]{1,0:T(8,128)(2,1)S(1)}) custom-call(f32[64,2048]{1,0:T(8,128)S(1)} %sub.34.start_ref, bf16[16,128,128]{2,1,0:T(8,128)(2,1)S(1)} %get-tuple-element.19.hi_ref, bf16[16,128,128]{2,1,0:T(8,128)(2,1)S(1)} %get-tuple-element.18.lo_ref, bf16[2048,2048]{1,0:T(8,128)(2,1)} %lower_ref.1), custom_call_target="tpu_custom_call" | custom-call | tf_op jit(solution)/shard_map/pallas_call | solution.py:307
  116.5 0.4 convolution_subtract_fusion.start_ref
  116.9 1.1 subtract_convert_fusion.1
  118.1 1.6 copy-done.2
  119.7 57.3 %shard_map.177 = (f32[64,256]{1,0:T(8,128)S(1)}, bf16[16,64,256]{2,1,0:T(8,128)(2,1)S(1)}) custom-call(f32[64,256]{1,0:T(8,128)S(1)} %convolution_subtract_fusion.start_ref, f32[256,256]{1,0:T(8,128)S(1)} %bitcast.96, bf16[16,256,256]{2,1,0:T(8,128)(2,1)S(1)} %bitcast.94, bf16[256,256]{1,0:T(8,128)(2,1)S(1)} %get-tuple-element.17.hi_ref, ...), custom_call_target="tpu_custom_call" | custom-call | tf_op jit(solution)/shard_map/pallas_call | solution.py:261
  177.0 0.5 fusion.9
  177.5 0.6 fusion.6
  178.1 0.6 copy-done.7
  178.7 0.6 fusion.46
  179.3 0.8 copy_bitcast_fusion
  180.2 0.1 fusion.35
  180.3 0.2 select_reduce_fusion
  180.5 0.3 fusion.13
  180.8 0.9 copy.65.coef_ref
  181.7 0.1 fusion.25
  181.9 0.7 copy.30.centre_ref
  182.5 14.7 %shard_map.178 = (bf16[16,2,64,128]{3,2,1,0:T(8,128)(2,1)}, f32[16,2,3,128]{3,2,1,0:T(4,128)}) custom-call(bf16[16,2,64,128]{3,2,1,0:T(8,128)(2,1)} %copy.65.coef_ref, f32[16,2,3,128]{3,2,1,0:T(4,128)} %copy.30.centre_ref), custom_call_target="tpu_custom_call" | custom-call | tf_op jit(solution)/shard_map/pallas_call | solution.py:517
  197.2 1.4 copy.31
  198.6 48.6 %shard_map.179 = f32[64,2048]{1,0:T(8,128)} custom-call(s32[16,32]{1,0:T(8,128)} %pattern_ref.1, bf16[32,64,128]{2,1,0:T(8,128)(2,1)} %bitcast.99, f32[32,3,128]{2,1,0:T(4,128)} %bitcast.101, f32[16,128,3]{2,1,0:T(8,128)} %bitcast.98), custom_call_target="tpu_custom_call" | custom-call | tf_op jit(solution)/shard_map/pallas_call | solution.py:367
  247.2 0.6 copy.69
  (26 shorter events, 0.1 us)
Async XLA Ops:
  0.6 2.7 %copy-start = (bf16[16,2,256,128]{3,2,1,0:T(8,128)(2,1)S(1)}, bf16[16,2,256,128]{3,2,1,0:T(8,128)(2,1)}, u32[]{:S(2)}) copy-start(bf16[16,2,256,128]{3,2,1,0:T(8,128)(2,1)} %param.19) | copy-start | bytes 6291460
  3.3 0.9 copy-start.12
  4.2 1.8 copy-start.3
  4.2 3.0 %copy-start.4 = (f32[64,256]{1,0:T(8,128)S(1)}, f32[64,256]{1,0:T(8,128)}, u32[]{:S(2)}) copy-start(f32[64,256]{1,0:T(8,128)} %rhs_ref.1) | copy-start | bytes 196612
  7.2 1.6 copy-start.1
  8.8 56.9 %copy-start.5 = (bf16[256,2048]{1,0:T(8,128)(2,1)S(1)}, bf16[256,2048]{1,0:T(8,128)(2,1)}, u32[]{:S(2)}) copy-start(bf16[256,2048]{1,0:T(8,128)(2,1)} %param.23) | copy-start | bytes 3145732
  100.0 1.5 copy-start.8
  101.8 14.7 %copy-start.6 = (bf16[256,2048]{1,0:T(8,128)(2,1)S(1)}, bf16[256,2048]{1,0:T(8,128)(2,1)}, u32[]{:S(2)}) copy-start(bf16[256,2048]{1,0:T(8,128)(2,1)} %param.23) | copy-start | bytes 3145732
  118.1 1.6 copy-start.2
  177.5 1.2 copy-start.7
  178.7 1.4 copy-start.11
  178.7 3.0 %copy-start.10 = (f32[16,3,128]{2,0,1:T(8,128)S(1)}, f32[16,3,128]{2,0,1:T(8,128)}, u32[]{:S(2)}) copy-start(f32[16,3,128]{2,0,1:T(8,128)} %param.27) | copy-start | bytes 73732
  179.3 17.9 %copy-start.9 = (f32[1,3,2048]{2,0,1:T(1,128)S(1)}, f32[1,3,2048]{2,0,1:T(1,128)}, u32[]{:S(2)}) copy-start(f32[1,3,2048]{2,0,1:T(1,128)} %param.28) | copy-start | bytes 73732

commit v18 on v17

--- a/solution.py
+++ b/solution.py
@@ -61,16 +61,24 @@
     return lax.dot_general(a, b, (((1,), (0,)), ((), ())), preferred_element_type=jnp.float32)
 
 
+def _split(x):
+    hi = x.astype(jnp.bfloat16)
+    return hi, (x - hi.astype(jnp.float32)).astype(jnp.bfloat16)
+
+
+def _three_products(a, b, dims):
+    a_hi, a_lo = _split(a)
+    b_hi, b_lo = _split(b)
+    dot = lambda u, v: lax.dot_general(u, v, (dims, ((), ())), preferred_element_type=jnp.float32)
+    return dot(a_hi, b_hi) + (dot(a_hi, b_lo) + dot(a_lo, b_hi))
+
+
 def _nt_exact(a, b):
-    return lax.dot_general(
-        a, b, (((1,), (1,)), ((), ())), precision=highest, preferred_element_type=jnp.float32
-    )
+    return _three_products(a, b, ((1,), (1,)))
 
 
 def _nn_exact(a, b):
-    return lax.dot_general(
-        a, b, (((1,), (0,)), ((), ())), precision=highest, preferred_element_type=jnp.float32
-    )
+    return _three_products(a, b, ((1,), (0,)))
 
 
 def _greet_group(n, leaf, me):

time: 249 us -> 248 us (level)
  no operation moved by 1% of the time
where the time goes in v18:
time: 248 us; the launch traced here: 247 us
  Pallas kernels  224 us (90%)
  matrix products  11.1 us (4%)
  local copies, waits for them, and re-layouts  8.59 us (3%)
    pallas_call x1, Pallas kernels, sep_solve(): pl.pallas_call(functools.partial(sep_backward_kernel, n), out_shape=(sol_...  57.3 us
    pallas_call x1, Pallas kernels, sep_solve(): pl.pallas_call(functools.partial(sep_forward_kernel, n), out_shape=sol_sh...  56.5 us
    pallas_call x1, Pallas kernels, evaluate_all(): pl.pallas_call(functools.partial(evaluate_kernel, slots), out_shape=jax.S...  48.2 us
    pallas_call x1, Pallas kernels, top_reduce(): pl.pallas_call(functools.partial(top_reduce_kernel, n, groups, span), out...  33.1 us
    pallas_call x1, Pallas kernels, exchange(): pl.pallas_call(functools.partial(exchange_kernel, n), out_shape=(jax.Shap...  14.7 us
    pallas_call x1, Pallas kernels, top_solve(): pl.pallas_call(functools.partial(top_solve_kernel, nt, span), out_shape=(...  14.6 us

profile of v18, /device:TPU:24, one launch (start us, length us, event | category | flops | bytes accessed | tf_op | source)
XLA Modules:
  0.0 246.9 jit_solution(12569263406414851221)
XLA Ops:
  0.6 2.7 %fusion.7 = f32[16,64,128]{2,1,0:T(8,128)S(1)} fusion(f32[16,128,128]{2,1,0:T(8,128)} %param.18, f32[64,2048]{1,0:T(8,128)} %param.15), kind=kOutput, calls=%fused_computation.13 | convolution fusion | flops 100663296 | bytes 2097152 | tf_op jit(solution)/shard_map/nrs,nts->nrt/dot_general | solution.py:584
  3.3 0.8 fusion.11
  4.2 1.6 fusion.3
  5.8 0.2 copy.66.part_ref
  6.0 1.2 subtract_convert_fusion.2
  7.2 1.6 copy-done.1
  8.8 56.5 %shard_map.174 = f32[64,256]{1,0:T(8,128)S(1)} custom-call(f32[64,256]{1,0:T(8,128)S(1)} %copy-done.4, bf16[16,64,256]{2,1,0:T(8,128)(2,1)S(1)} %copy.66.part_ref, f32[256,256]{1,0:T(8,128)S(1)} %bitcast.95, bf16[16,256,256]{2,1,0:T(8,128)(2,1)S(1)} %bitcast.93, bf16[256,256]{1,0:T(8,128)(2,1)S(1)} %get-tuple-element.21.hi_ref, ...), custom_call_target="tpu_custom_call" | custom-call | tf_op jit(solution)/shard_map/pallas_call | solution.py:255
  65.4 1.1 fusion.23.term_ref
  66.5 33.1 %shard_map.175 = f32[64,2048]{1,0:T(8,128)} custom-call(f32[64,2048]{1,0:T(8,128)} %fusion.23.term_ref), custom_call_target="tpu_custom_call" | custom-call | tf_op jit(solution)/shard_map/pallas_call | solution.py:468
  99.6 1.3 sub.34.start_ref
  100.9 0.2 copy-done.8
  101.1 0.2 subtract_convert_fusion
  101.4 14.6 %shard_map.176 = (f32[64,2048]{1,0:T(8,128)}, bf16[64,2048]{1,0:T(8,128)(2,1)S(1)}) custom-call(f32[64,2048]{1,0:T(8,128)S(1)} %sub.34.start_ref, bf16[16,128,128]{2,1,0:T(8,128)(2,1)S(1)} %get-tuple-element.19.hi_ref, bf16[16,128,128]{2,1,0:T(8,128)(2,1)S(1)} %get-tuple-element.18.lo_ref, bf16[2048,2048]{1,0:T(8,128)(2,1)} %lower_ref.1), custom_call_target="tpu_custom_call" | custom-call | tf_op jit(solution)/shard_map/pallas_call | solution.py:315
  116.0 0.4 convolution_subtract_fusion.start_ref
  116.5 1.1 subtract_convert_fusion.1
  117.6 1.6 copy-done.2
  119.2 57.3 %shard_map.177 = (f32[64,256]{1,0:T(8,128)S(1)}, bf16[16,64,256]{2,1,0:T(8,128)(2,1)S(1)}) custom-call(f32[64,256]{1,0:T(8,128)S(1)} %convolution_subtract_fusion.start_ref, f32[256,256]{1,0:T(8,128)S(1)} %bitcast.96, bf16[16,256,256]{2,1,0:T(8,128)(2,1)S(1)} %bitcast.94, bf16[256,256]{1,0:T(8,128)(2,1)S(1)} %get-tuple-element.17.hi_ref, ...), custom_call_target="tpu_custom_call" | custom-call | tf_op jit(solution)/shard_map/pallas_call | solution.py:269
  176.5 0.5 fusion.9
  177.0 0.6 fusion.6
  177.6 0.6 copy-done.7
  178.2 0.6 fusion.46
  178.8 0.8 copy_bitcast_fusion
  179.7 0.1 fusion.35
  179.8 0.2 select_reduce_fusion
  180.0 0.3 fusion.13
  180.3 0.9 copy.65.coef_ref
  181.2 0.1 fusion.25
  181.4 0.7 copy.30.centre_ref
  182.0 14.7 %shard_map.178 = (bf16[16,2,64,128]{3,2,1,0:T(8,128)(2,1)}, f32[16,2,3,128]{3,2,1,0:T(4,128)}) custom-call(bf16[16,2,64,128]{3,2,1,0:T(8,128)(2,1)} %copy.65.coef_ref, f32[16,2,3,128]{3,2,1,0:T(4,128)} %copy.30.centre_ref), custom_call_target="tpu_custom_call" | custom-call | tf_op jit(solution)/shard_map/pallas_call | solution.py:525
  196.7 1.4 copy.31
  198.1 48.2 %shard_map.179 = f32[64,2048]{1,0:T(8,128)} custom-call(s32[16,32]{1,0:T(8,128)} %pattern_ref.1, bf16[32,64,128]{2,1,0:T(8,128)(2,1)} %bitcast.99, f32[32,3,128]{2,1,0:T(4,128)} %bitcast.101, f32[16,128,3]{2,1,0:T(8,128)} %bitcast.98), custom_call_target="tpu_custom_call" | custom-call | tf_op jit(solution)/shard_map/pallas_call | solution.py:375
  246.3 0.6 copy.69
  (26 shorter events, 0.1 us)
Async XLA Ops:
  0.6 2.7 %copy-start = (bf16[16,2,256,128]{3,2,1,0:T(8,128)(2,1)S(1)}, bf16[16,2,256,128]{3,2,1,0:T(8,128)(2,1)}, u32[]{:S(2)}) copy-start(bf16[16,2,256,128]{3,2,1,0:T(8,128)(2,1)} %param.19) | copy-start | bytes 6291460
  3.3 0.9 copy-start.12
  4.2 1.8 copy-start.3
  4.2 3.0 %copy-start.4 = (f32[64,256]{1,0:T(8,128)S(1)}, f32[64,256]{1,0:T(8,128)}, u32[]{:S(2)}) copy-start(f32[64,256]{1,0:T(8,128)} %rhs_ref.1) | copy-start | bytes 196612
  7.2 1.6 copy-start.1
  8.8 56.5 %copy-start.5 = (bf16[256,2048]{1,0:T(8,128)(2,1)S(1)}, bf16[256,2048]{1,0:T(8,128)(2,1)}, u32[]{:S(2)}) copy-start(bf16[256,2048]{1,0:T(8,128)(2,1)} %param.23) | copy-start | bytes 3145732
  99.6 1.5 copy-start.8
  101.4 14.7 %copy-start.6 = (bf16[256,2048]{1,0:T(8,128)(2,1)S(1)}, bf16[256,2048]{1,0:T(8,128)(2,1)}, u32[]{:S(2)}) copy-start(bf16[256,2048]{1,0:T(8,128)(2,1)} %param.23) | copy-start | bytes 3145732
  117.6 1.6 copy-start.2
  177.0 1.2 copy-start.7
  178.2 1.4 copy-start.11
  178.2 3.0 %copy-start.10 = (f32[16,3,128]{2,0,1:T(8,128)S(1)}, f32[16,3,128]{2,0,1:T(8,128)}, u32[]{:S(2)}) copy-start(f32[16,3,128]{2,0,1:T(8,128)} %param.27) | copy-start | bytes 73732
  178.8 17.9 %copy-start.9 = (f32[1,3,2048]{2,0,1:T(1,128)S(1)}, f32[1,3,2048]{2,0,1:T(1,128)}, u32[]{:S(2)}) copy-start(f32[1,3,2048]{2,0,1:T(1,128)} %param.28) | copy-start | bytes 73732

commit v19 on v18

--- a/solution.py
+++ b/solution.py
@@ -122,9 +122,11 @@
     return _nn(y, hi_ref[...]) + _nn(y, lo_ref[...])
 
 
-def sep_forward_kernel(n, rhs_ref, part_ref, inv_ref, blocks_ref, hi_ref, lo_ref, sol_ref, halves, resid, base, send_sem, recv_sem, arrived, local_sem, give_sem, take_sem):
+def sep_forward_kernel(n, rhs_ref, part_ref, inv_ref, blocks_hbm, hi_ref, lo_ref, sol_ref, halves, resid, base, send_sem, recv_sem, blocks_ref, block_sem, arrived, local_sem, give_sem, take_sem):
     me = lax.axis_index("grp")
     leaf = lax.axis_index("leaf")
+    fetch = pltpu.make_async_copy(blocks_hbm, blocks_ref, block_sem.at[0])
+    fetch.start()
     _greet_group(n, leaf, me)
 
     def give(dest):
@@ -155,6 +157,7 @@
             give(dest).wait_send()
 
     dests = lambda s, k: (s + k, s + k < n)
+    fetch.wait()
 
     @pl.when(me == 0)
     def _():
@@ -185,12 +188,15 @@
     lax.fori_loop(0, n - 1, step, 0)
 
 
-def sep_backward_kernel(n, start_ref, inv_ref, blocks_ref, hi_ref, lo_ref, sol_ref, table_ref, halves, resid, base, send_sem, recv_sem):
+def sep_backward_kernel(n, start_ref, inv_ref, blocks_hbm, hi_ref, lo_ref, sol_ref, table_ref, halves, resid, base, send_sem, recv_sem, blocks_ref, block_sem):
     me = lax.axis_index("grp")
     leaf = lax.axis_index("leaf")
+    fetch = pltpu.make_async_copy(blocks_hbm, blocks_ref, block_sem.at[0])
+    fetch.start()
     _greet_group(n, leaf, me)
     resid[...] = start_ref[...]
     dests = lambda s, k: (s - k, s - k >= 0)
+    fetch.wait()
 
     @pl.when(me == n - 1)
     def _():
@@ -247,7 +253,10 @@
         pltpu.VMEM((rows, width), jnp.float32),
         pltpu.SemaphoreType.DMA((n,)),
         pltpu.SemaphoreType.DMA((n,)),
+        pltpu.VMEM(blocks.shape, blocks.dtype),
+        pltpu.SemaphoreType.DMA((1,)),
     ]
+    anywhere = pl.BlockSpec(memory_space=pl.ANY)
     sol_shape = jax.ShapeDtypeStruct((rows, width), jnp.float32)
     params = dict(has_side_effects=True, vmem_limit_bytes=48 * 1024 * 1024)
     if kind == "forward":
@@ -255,7 +264,7 @@
         return pl.pallas_call(
             functools.partial(sep_forward_kernel, n),
             out_shape=sol_shape,
-            in_specs=[vmem] * 6,
+            in_specs=[vmem, vmem, vmem, anywhere, vmem, vmem],
             out_specs=vmem,
             scratch_shapes=scratch
             + [
@@ -269,7 +278,7 @@
     return pl.pallas_call(
         functools.partial(sep_backward_kernel, n),
         out_shape=(sol_shape, jax.ShapeDtypeStruct((n, rows, width), jnp.bfloat16)),
-        in_specs=[vmem] * 5,
+        in_specs=[vmem, vmem, anywhere, vmem, vmem],
         out_specs=(vmem, vmem),
         scratch_shapes=scratch,
         compiler_params=pltpu.CompilerParams(collective_id=1, **params),

time: 248 us -> 249 us (level)
  no operation moved by 1% of the time
where the time goes in v19:
time: 249 us; the launch traced here: 246 us
  Pallas kernels  223 us (90%)
  matrix products  11.1 us (4%)
  local copies, waits for them, and re-layouts  8.59 us (3%)
    pallas_call x1, Pallas kernels, sep_solve(): pl.pallas_call(functools.partial(sep_backward_kernel, n), out_shape=(sol_...  57.5 us
    pallas_call x1, Pallas kernels, sep_solve(): pl.pallas_call(functools.partial(sep_forward_kernel, n), out_shape=sol_sh...  56.8 us
    pallas_call x1, Pallas kernels, evaluate_all(): pl.pallas_call(functools.partial(evaluate_kernel, slots), out_shape=jax.S...  46.3 us
    pallas_call x1, Pallas kernels, top_reduce(): pl.pallas_call(functools.partial(top_reduce_kernel, n, groups, span), out...  33.1 us
    pallas_call x1, Pallas kernels, exchange(): pl.pallas_call(functools.partial(exchange_kernel, n), out_shape=(jax.Shap...  14.7 us
    pallas_call x1, Pallas kernels, top_solve(): pl.pallas_call(functools.partial(top_solve_kernel, nt, span), out_shape=(...  14.6 us

profile of v19, /device:TPU:24, one launch (start us, length us, event | category | flops | bytes accessed | tf_op | source)
XLA Modules:
  0.0 245.6 jit_solution(4064140852156346718)
XLA Ops:
  0.6 2.7 %fusion.7 = f32[16,64,128]{2,1,0:T(8,128)S(1)} fusion(f32[16,128,128]{2,1,0:T(8,128)} %param.18, f32[64,2048]{1,0:T(8,128)} %param.15), kind=kOutput, calls=%fused_computation.13 | convolution fusion | flops 100663296 | bytes 2097152 | tf_op jit(solution)/shard_map/nrs,nts->nrt/dot_general | solution.py:593
  3.3 0.8 fusion.11
  4.2 1.6 fusion.3
  5.8 0.2 copy.66.part_ref
  6.0 1.2 subtract_convert_fusion.2
  7.2 1.6 copy-done.1
  8.8 56.8 %shard_map.174 = f32[64,256]{1,0:T(8,128)S(1)} custom-call(f32[64,256]{1,0:T(8,128)S(1)} %copy-done.4, bf16[16,64,256]{2,1,0:T(8,128)(2,1)S(1)} %copy.66.part_ref, f32[256,256]{1,0:T(8,128)S(1)} %bitcast.95, bf16[16,256,256]{2,1,0:T(8,128)(2,1)S(1)} %bitcast.93, bf16[256,256]{1,0:T(8,128)(2,1)S(1)} %get-tuple-element.21.hi_ref, ...), custom_call_target="tpu_custom_call" | custom-call | tf_op jit(solution)/shard_map/pallas_call | solution.py:264
  65.7 1.1 fusion.23.term_ref
  66.7 33.1 %shard_map.175 = f32[64,2048]{1,0:T(8,128)} custom-call(f32[64,2048]{1,0:T(8,128)} %fusion.23.term_ref), custom_call_target="tpu_custom_call" | custom-call | tf_op jit(solution)/shard_map/pallas_call | solution.py:477
  99.8 1.3 sub.34.start_ref
  101.2 0.2 copy-done.8
  101.4 0.2 subtract_convert_fusion
  101.6 14.6 %shard_map.176 = (f32[64,2048]{1,0:T(8,128)}, bf16[64,2048]{1,0:T(8,128)(2,1)S(1)}) custom-call(f32[64,2048]{1,0:T(8,128)S(1)} %sub.34.start_ref, bf16[16,128,128]{2,1,0:T(8,128)(2,1)S(1)} %get-tuple-element.19.hi_ref, bf16[16,128,128]{2,1,0:T(8,128)(2,1)S(1)} %get-tuple-element.18.lo_ref, bf16[2048,2048]{1,0:T(8,128)(2,1)} %lower_ref.1), custom_call_target="tpu_custom_call" | custom-call | tf_op jit(solution)/shard_map/pallas_call | solution.py:324
  116.3 0.4 convolution_subtract_fusion.start_ref
  116.7 1.1 subtract_convert_fusion.1
  117.9 1.6 copy-done.2
  119.5 57.5 %shard_map.177 = (f32[64,256]{1,0:T(8,128)S(1)}, bf16[16,64,256]{2,1,0:T(8,128)(2,1)S(1)}) custom-call(f32[64,256]{1,0:T(8,128)S(1)} %convolution_subtract_fusion.start_ref, f32[256,256]{1,0:T(8,128)S(1)} %bitcast.96, bf16[16,256,256]{2,1,0:T(8,128)(2,1)S(1)} %bitcast.94, bf16[256,256]{1,0:T(8,128)(2,1)S(1)} %get-tuple-element.17.hi_ref, ...), custom_call_target="tpu_custom_call" | custom-call | tf_op jit(solution)/shard_map/pallas_call | solution.py:278
  177.0 0.5 fusion.9
  177.6 0.6 fusion.6
  178.2 0.6 copy-done.7
  178.8 0.6 fusion.46
  179.4 0.8 copy_bitcast_fusion
  180.2 0.1 fusion.35
  180.3 0.2 select_reduce_fusion
  180.5 0.3 fusion.13
  180.8 0.9 copy.65.coef_ref
  181.8 0.1 fusion.25
  181.9 0.7 copy.30.centre_ref
  182.6 14.7 %shard_map.178 = (bf16[16,2,64,128]{3,2,1,0:T(8,128)(2,1)}, f32[16,2,3,128]{3,2,1,0:T(4,128)}) custom-call(bf16[16,2,64,128]{3,2,1,0:T(8,128)(2,1)} %copy.65.coef_ref, f32[16,2,3,128]{3,2,1,0:T(4,128)} %copy.30.centre_ref), custom_call_target="tpu_custom_call" | custom-call | tf_op jit(solution)/shard_map/pallas_call | solution.py:534
  197.3 1.4 copy.31
  198.6 46.3 %shard_map.179 = f32[64,2048]{1,0:T(8,128)} custom-call(s32[16,32]{1,0:T(8,128)} %pattern_ref.1, bf16[32,64,128]{2,1,0:T(8,128)(2,1)} %bitcast.99, f32[32,3,128]{2,1,0:T(4,128)} %bitcast.101, f32[16,128,3]{2,1,0:T(8,128)} %bitcast.98), custom_call_target="tpu_custom_call" | custom-call | tf_op jit(solution)/shard_map/pallas_call | solution.py:384
  244.9 0.6 copy.69
  (26 shorter events, 0.1 us)
Async XLA Ops:
  0.6 2.7 %copy-start = (bf16[16,2,256,128]{3,2,1,0:T(8,128)(2,1)S(1)}, bf16[16,2,256,128]{3,2,1,0:T(8,128)(2,1)}, u32[]{:S(2)}) copy-start(bf16[16,2,256,128]{3,2,1,0:T(8,128)(2,1)} %param.19) | copy-start | bytes 6291460
  3.3 0.9 copy-start.12
  4.2 1.8 copy-start.3
  4.2 3.0 %copy-start.4 = (f32[64,256]{1,0:T(8,128)S(1)}, f32[64,256]{1,0:T(8,128)}, u32[]{:S(2)}) copy-start(f32[64,256]{1,0:T(8,128)} %rhs_ref.1) | copy-start | bytes 196612
  7.2 1.6 copy-start.1
  8.8 56.8 %copy-start.5 = (bf16[256,2048]{1,0:T(8,128)(2,1)S(1)}, bf16[256,2048]{1,0:T(8,128)(2,1)}, u32[]{:S(2)}) copy-start(bf16[256,2048]{1,0:T(8,128)(2,1)} %param.23) | copy-start | bytes 3145732
  99.8 1.5 copy-start.8
  101.6 14.7 %copy-start.6 = (bf16[256,2048]{1,0:T(8,128)(2,1)S(1)}, bf16[256,2048]{1,0:T(8,128)(2,1)}, u32[]{:S(2)}) copy-start(bf16[256,2048]{1,0:T(8,128)(2,1)} %param.23) | copy-start | bytes 3145732
  117.9 1.6 copy-start.2
  177.5 1.2 copy-start.7
  178.8 1.4 copy-start.11
  178.8 3.0 %copy-start.10 = (f32[16,3,128]{2,0,1:T(8,128)S(1)}, f32[16,3,128]{2,0,1:T(8,128)}, u32[]{:S(2)}) copy-start(f32[16,3,128]{2,0,1:T(8,128)} %param.27) | copy-start | bytes 73732
  179.4 17.9 %copy-start.9 = (f32[1,3,2048]{2,0,1:T(1,128)S(1)}, f32[1,3,2048]{2,0,1:T(1,128)}, u32[]{:S(2)}) copy-start(f32[1,3,2048]{2,0,1:T(1,128)} %param.28) | copy-start | bytes 73732
